TPU v7x, 32 devices: a whole 2x2x4 slice. The times are simulated.
32 devices in a mesh: parts: 2 (over y), gx: 4 (over z), gy: 2 (over x), gz: 2 (over core).
Axes of the slice: x: 2, y: 2, z: 4, core: 2. Of those that a mesh axis runs over, the one named last changes fastest.
Arguments:
- forward_pops: bfloat16 [19, 256, 16, 256], P(None, ('parts', 'gx'), 'gy', 'gz'), parts along dimension 1, as said below
- adjoint_pops: bfloat16 [19, 256, 16, 256], P(None, ('parts', 'gx'), 'gy', 'gz'), parts along dimension 1, may hold values from -6 to 6
- coefficients: float32 [64, 4, 64], P(('parts', 'gx'), 'gy', 'gz'), parts along dimension 0, may hold values from -3 to 3
- node_kind: int32 [256, 16, 256], P(('parts', 'gx'), 'gy', 'gz'), parts along dimension 0, may hold values from 0 to 3, as said below
Outputs:
- prior_adjoint: bfloat16 [19, 256, 16, 256], P(None, ('parts', 'gx'), 'gy', 'gz'), parts along dimension 1
- coef_gradient: float32 [64, 4, 64], P(('parts', 'gx'), 'gy', 'gz'), parts along dimension 0
There are 2 independent parts, one for each index of `parts`. A program takes and returns all parts, laid end to end along the dimension named above; each array names one. Nothing has to cross between parts.
Inputs may be any that keep to these rules, and one draw needn't show every extreme that they name: `node_kind`: node kinds: 0 fluid, 1 solid, 2 inlet, 3 outlet. `forward_pops`: every population lies between 0.4 and 1.7 times the lattice weight of its velocity.
All inputs are finite; a program needn't handle non-finite values.
Results may differ from a plain program's by a relative error of at most 0.001.
Values may be sent and summed in bfloat16 or wider, within the bound.
A program may use at most 64 MiB of HBM per device.

v0:
```python
import jax
import jax.numpy as jnp
from jax import lax
from jax.sharding import PartitionSpec as P

VELOCITY = (
    (0, 0, 0),
    (1, 0, 0),
    (-1, 0, 0),
    (0, 1, 0),
    (0, -1, 0),
    (0, 0, 1),
    (0, 0, -1),
    (1, 1, 0),
    (-1, -1, 0),
    (1, -1, 0),
    (-1, 1, 0),
    (1, 0, 1),
    (-1, 0, -1),
    (1, 0, -1),
    (-1, 0, 1),
    (0, 1, 1),
    (0, -1, -1),
    (0, 1, -1),
    (0, -1, 1),
)
OPPOSITE = (0, 2, 1, 4, 3, 6, 5, 8, 7, 10, 9, 12, 11, 14, 13, 16, 15, 18, 17)
WEIGHTS = (1.0 / 3.0,) + (1.0 / 18.0,) * 6 + (1.0 / 36.0,) * 12
relaxation = 1.6
inlet_speed = 0.05
highest = lax.Precision.HIGHEST


def padded(block, sides, width):
    for axis, dim in sides:
        count = lax.axis_size(axis)
        forward = [(i, i + 1) for i in range(count - 1)]
        backward = [(target, source) for source, target in forward]
        low = lax.ppermute(
            lax.slice_in_dim(block, block.shape[dim] - width, None, axis=dim), axis, forward
        )
        high = lax.ppermute(lax.slice_in_dim(block, 0, width, axis=dim), axis, backward)
        block = jnp.concatenate([low, block, high], axis=dim)
    return block


def equilibrium(density, flow_x, flow_y, flow_z):
    square = flow_x * flow_x + flow_y * flow_y + flow_z * flow_z
    layers = []
    for component in range(19):
        step_x, step_y, step_z = VELOCITY[component]
        projection = step_x * flow_x + step_y * flow_y + step_z * flow_z
        layers.append(
            WEIGHTS[component]
            * density
            * (1.0 + 3.0 * projection + 4.5 * projection * projection - 1.5 * square)
        )
    return jnp.stack(layers)


def moment(populations, dimension):
    total = jnp.zeros_like(populations[0])
    for component in range(19):
        factor = VELOCITY[component][dimension]
        if factor != 0:
            total = total + factor * populations[component]
    return total


def collide(populations, porosity, node_kind):
    density = jnp.sum(populations, axis=0)
    flow_x = moment(populations, 0) / density
    flow_y = moment(populations, 1) / density
    flow_z = moment(populations, 2) / density
    retained = 1.0 - porosity
    fluid_post = populations - relaxation * (
        populations - equilibrium(density, retained * flow_x, retained * flow_y, retained * flow_z)
    )
    solid_post = jnp.stack([populations[OPPOSITE[component]] for component in range(19)])
    unit_density = jnp.ones_like(density)
    inlet_post = equilibrium(
        unit_density, inlet_speed * unit_density, jnp.zeros_like(density), jnp.zeros_like(density)
    )
    outlet_post = equilibrium(unit_density, flow_x, flow_y, flow_z)
    kind_here = node_kind[None]
    return jnp.where(
        kind_here == 0,
        fluid_post,
        jnp.where(kind_here == 1, solid_post, jnp.where(kind_here == 2, inlet_post, outlet_post)),
    )


def basis_matrix(fine_count, coarse_count, fine_offset, coarse_offset):
    fine_pos = jnp.arange(fine_count, dtype=jnp.float32) + fine_offset
    coarse_pos = jnp.arange(coarse_count, dtype=jnp.float32) + coarse_offset
    distance = fine_pos[:, None] - 4.0 * coarse_pos[None, :] - 1.5
    radius = jnp.abs(distance) / 6.0
    return jnp.where(radius < 1.0, (1.0 - radius) ** 4 * (1.0 + 4.0 * radius), 0.0)


def moving(dimension):
    return [component for component in range(19) if VELOCITY[component][dimension] != 0]


def pull_along(lane_list, dimension, extended):
    length_here = lane_list[0].shape[dimension]
    result = list(lane_list)
    for position, component in enumerate(moving(dimension)):
        offset = 1 + VELOCITY[component][dimension]
        result[component] = lax.slice_in_dim(
            extended[position], offset, offset + length_here, axis=dimension
        )
    return result


def fold_rim(bordered, dimension):
    length_here = bordered.shape[dimension]
    middle = lax.slice_in_dim(bordered, 2, length_here - 2, axis=dimension)
    head_slice = lax.slice_in_dim(bordered, 0, 1, axis=dimension)
    tail_slice = lax.slice_in_dim(bordered, length_here - 1, length_here, axis=dimension)
    middle_count = length_here - 4
    head_pads = [(0, 0)] * 3
    tail_pads = [(0, 0)] * 3
    head_pads[dimension] = (0, middle_count - 1)
    tail_pads[dimension] = (middle_count - 1, 0)
    return middle + jnp.pad(head_slice, head_pads) + jnp.pad(tail_slice, tail_pads)


def per_device(forward_pops, adjoint_pops, coefficients, node_kind):
    cells_x, cells_y, cells_z = node_kind.shape
    coarse_x, coarse_y, coarse_z = coefficients.shape
    window = padded(coefficients, (("gx", 0), ("gy", 1), ("gz", 2)), 1)
    basis_x = basis_matrix(cells_x, coarse_x + 2, 0, -1)
    basis_y = basis_matrix(cells_y, coarse_y + 2, 0, -1)
    basis_z = basis_matrix(cells_z, coarse_z + 2, 0, -1)
    partway = jnp.einsum("ijk,zk->ijz", window, basis_z, precision=highest)
    partway = jnp.einsum("ijz,yj->iyz", partway, basis_y, precision=highest)
    level_set = jnp.einsum("iyz,xi->xyz", partway, basis_x, precision=highest)
    bent = jnp.tanh(4.0 * level_set)
    porosity = 0.45 * (1.0 - bent)
    slope_phi = -1.8 * (1.0 - bent * bent)
    lane_list = [adjoint_pops[component] for component in range(19)]
    extended = padded(jnp.stack([lane_list[component] for component in moving(0)]), (("gx", 1),), 1)
    lane_list = pull_along(lane_list, 0, extended)
    extended = padded(jnp.stack([lane_list[component] for component in moving(1)]), (("gy", 2),), 1)
    lane_list = pull_along(lane_list, 1, extended)
    extended = padded(jnp.stack([lane_list[component] for component in moving(2)]), (("gz", 3),), 1)
    lane_list = pull_along(lane_list, 2, extended)
    pulled = jnp.stack(lane_list).astype(jnp.float32)
    forward = forward_pops.astype(jnp.float32)

    def local_collide(populations, porosity_here):
        return collide(populations, porosity_here, node_kind)

    unused, pullback = jax.vjp(local_collide, forward, porosity)
    prior, porosity_bar = pullback(pulled)
    prior_adjoint = prior.astype(jnp.bfloat16)
    sensitivity = porosity_bar * slope_phi
    partial_value = jnp.einsum("xyz,xi->iyz", sensitivity, basis_x, precision=highest)
    partial_value = jnp.einsum("iyz,yj->ijz", partial_value, basis_y, precision=highest)
    partial_value = jnp.einsum("ijz,zk->ijk", partial_value, basis_z, precision=highest)
    bordered = padded(partial_value, (("gx", 0), ("gy", 1), ("gz", 2)), 1)
    gradient = fold_rim(fold_rim(fold_rim(bordered, 0), 1), 2)
    return (prior_adjoint, gradient)


def solution(mesh):
    in_specs = (
        P(None, ("parts", "gx"), "gy", "gz"),
        P(None, ("parts", "gx"), "gy", "gz"),
        P(("parts", "gx"), "gy", "gz"),
        P(("parts", "gx"), "gy", "gz"),
    )
    out_specs = (P(None, ("parts", "gx"), "gy", "gz"), P(("parts", "gx"), "gy", "gz"))
    return jax.shard_map(
        per_device, mesh=mesh, in_specs=in_specs, out_specs=out_specs, check_vma=False
    )
```

profile of v0, /device:TPU:0, one launch (start us, length us, event | category | flops | bytes accessed | tf_op | source)
XLA Modules:
  0.0 95.0 jit_solution(15775273977151735013)
XLA Ops:
  0.6 0.8 fusion.396
  1.4 1.3 %collective-permute-start.7 = (f32[1,2,32]{2,1,0:T(2,128)S(1)}, f32[1,2,32]{2,1,0:T(2,128)S(1)}, u32[]{:S(2)}, u32[]{:S(2)}) collective-permute-start(f32[1,2,32]{2,1,0:T(2,128)S(1)} %get-tuple-element.147), channel_id=1, source_target_pairs={{4,0},{8,4},{12,8},{5,1},{9,5},{13,9},{6,2},{10,6},{14,10},{7,3},{... | collective-permute-start | bytes 776 | tf_op jit(solution)/shard_map/ppermute | solution.py:42
  2.7 5.6 %collective-permute-start.6 = (f32[1,2,32]{2,1,0:T(2,128)S(1)}, f32[1,2,32]{2,1,0:T(2,128)S(1)}, u32[]{:S(2)}, u32[]{:S(2)}) collective-permute-start(f32[1,2,32]{2,1,0:T(2,128)S(1)} %get-tuple-element.148), channel_id=1, source_target_pairs={{0,4},{4,8},{8,12},{1,5},{5,9},{9,13},{2,6},{6,10},{10,14},{3,7},{... | collective-permute-start | bytes 776 | tf_op jit(solution)/shard_map/ppermute | solution.py:39
  8.3 1.1 %fusion.388 = (bf16[2,32,8,128]{3,2,1,0:T(8,128)(2,1)S(1)}, bf16[2,32,8,128]{3,2,1,0:T(8,128)(2,1)S(1)}, bf16[2,32,8,128]{3,2,1,0:T(8,128)(2,1)S(1)}) fusion(bf16[19,32,8,128]{3,2,1,0:T(8,128)(2,1)} %param.5), kind=kLoop, calls=%fused_computation.691 | loop fusion | bytes 786432 | tf_op jit(solution)/shard_map/slice | solution.py:142
  9.4 1.1 %slice.379 = bf16[8,32,8,128]{3,2,1,0:T(8,128)(2,1)S(1)} slice(bf16[19,32,8,128]{3,2,1,0:T(8,128)(2,1)} %param.5), slice={[7:15], [0:32], [0:8], [0:128]} | slice | bytes 1048576 | tf_op jit(solution)/shard_map/slice | solution.py:142
  10.5 0.1 copy_dynamic-update-slice_fusion
  10.7 3.9 %collective-permute-start.1 = (bf16[10,1,8,128]{3,1,2,0:T(2,128)(2,1)S(1)}, bf16[10,1,8,128]{3,1,2,0:T(2,128)(2,1)S(1)}, u32[]{:S(2)}, u32[]{:S(2)}) collective-permute-start(bf16[10,1,8,128]{3,1,2,0:T(2,128)(2,1)S(1)} %get-tuple-element.118), channel_id=1, source_target_pairs={{0,4},{4,8},{8,12},{1,5},{5,9},{9,13},{2,6},{6,10},{10,14},{3,7},{... | collective-permute-start | bytes 61448 | tf_op jit(solution)/shard_map/ppermute | solution.py:39
  14.7 1.3 %collective-permute-start = (bf16[10,1,8,128]{3,1,2,0:T(2,128)(2,1)S(1)}, bf16[10,1,8,128]{3,1,2,0:T(2,128)(2,1)S(1)}, u32[]{:S(2)}, u32[]{:S(2)}) collective-permute-start(bf16[10,1,8,128]{3,1,2,0:T(2,128)(2,1)S(1)} %get-tuple-element.119), channel_id=1, source_target_pairs={{4,0},{8,4},{12,8},{5,1},{9,5},{13,9},{6,2},{10,6},{14,10},{7,3},{... | collective-permute-start | bytes 61448 | tf_op jit(solution)/shard_map/ppermute | solution.py:42
  16.1 0.3 copy_convert_fusion
  16.5 0.4 copy-done.4
  17.0 0.6 constant_dynamic-update-slice_fusion.30
  17.7 3.4 %collective-permute-start.8 = (f32[10,1,32]{2,1,0:T(1,128)S(1)}, f32[10,1,32]{2,1,0:T(1,128)S(1)}, u32[]{:S(2)}, u32[]{:S(2)}) collective-permute-start(f32[10,1,32]{2,1,0:T(1,128)S(1)} %get-tuple-element.145), channel_id=1, source_target_pairs={{0,2},{1,3},{4,6},{5,7},{8,10},{9,11},{12,14},{13,15},{16,18},{17,... | collective-permute-start | bytes 3848 | tf_op jit(solution)/shard_map/ppermute | solution.py:39
  21.1 1.3 %collective-permute-start.9 = (f32[10,1,32]{2,1,0:T(1,128)S(1)}, f32[10,1,32]{2,1,0:T(1,128)S(1)}, u32[]{:S(2)}, u32[]{:S(2)}) collective-permute-start(f32[10,1,32]{2,1,0:T(1,128)S(1)} %get-tuple-element.146), channel_id=1, source_target_pairs={{2,0},{3,1},{6,4},{7,5},{10,8},{11,9},{14,12},{15,13},{18,16},{19,... | collective-permute-start | bytes 3848 | tf_op jit(solution)/shard_map/ppermute | solution.py:42
  22.5 4.1 %collective-permute-done.9 = f32[10,1,32]{2,1,0:T(1,128)S(1)} collective-permute-done((f32[10,1,32]{2,1,0:T(1,128)S(1)}, f32[10,1,32]{2,1,0:T(1,128)S(1)}, u32[]{:S(2)}, u32[]{:S(2)}) %collective-permute-start.9) | collective-permute-done | bytes 1312 | tf_op jit(solution)/shard_map/ppermute | solution.py:42
  26.8 1.3 %collective-permute-start.10 = (f32[10,4,1]{2,1,0:T(4,128)S(1)}, f32[10,4,1]{2,1,0:T(4,128)S(1)}, u32[]{:S(2)}, u32[]{:S(2)}) collective-permute-start(f32[10,4,1]{2,1,0:T(4,128)S(1)} %get-tuple-element.143), channel_id=1, source_target_pairs={{0,1},{2,3},{4,5},{6,7},{8,9},{10,11},{12,13},{14,15},{16,17},{18,... | collective-permute-start | bytes 488 | tf_op jit(solution)/shard_map/ppermute | solution.py:39
  28.1 1.3 %collective-permute-start.11 = (f32[10,4,1]{2,1,0:T(4,128)S(1)}, f32[10,4,1]{2,1,0:T(4,128)S(1)}, u32[]{:S(2)}, u32[]{:S(2)}) collective-permute-start(f32[10,4,1]{2,1,0:T(4,128)S(1)} %get-tuple-element.144), channel_id=1, source_target_pairs={{1,0},{3,2},{5,4},{7,6},{9,8},{11,10},{13,12},{15,14},{17,16},{19,... | collective-permute-start | bytes 488 | tf_op jit(solution)/shard_map/ppermute | solution.py:42
  29.4 1.7 %collective-permute-done.11 = f32[10,4,1]{2,1,0:T(4,128)S(1)} collective-permute-done((f32[10,4,1]{2,1,0:T(4,128)S(1)}, f32[10,4,1]{2,1,0:T(4,128)S(1)}, u32[]{:S(2)}, u32[]{:S(2)}) %collective-permute-start.11) | collective-permute-done | bytes 192 | tf_op jit(solution)/shard_map/ppermute | solution.py:42
  31.1 0.1 pad_maximum_fusion.7
  31.3 0.2 fusion.313
  31.6 0.7 constant_dynamic-update-slice_fusion.9
  32.4 0.7 constant_dynamic-update-slice_fusion.8
  33.2 1.7 %collective-permute-start.2 = (bf16[10,32,1,128]{3,1,2,0:T(8,128)(2,1)S(1)}, bf16[10,32,1,128]{3,1,2,0:T(8,128)(2,1)S(1)}, u32[]{:S(2)}, u32[]{:S(2)}) collective-permute-start(bf16[10,32,1,128]{3,1,2,0:T(8,128)(2,1)S(1)} %get-tuple-element.116), channel_id=1, source_target_pairs={{0,2},{1,3},{4,6},{5,7},{8,10},{9,11},{12,14},{13,15},{16,18},{17,... | collective-permute-start | bytes 245768 | tf_op jit(solution)/shard_map/ppermute | solution.py:39
  34.8 1.3 %collective-permute-start.3 = (bf16[10,32,1,128]{3,1,2,0:T(8,128)(2,1)S(1)}, bf16[10,32,1,128]{3,1,2,0:T(8,128)(2,1)S(1)}, u32[]{:S(2)}, u32[]{:S(2)}) collective-permute-start(bf16[10,32,1,128]{3,1,2,0:T(8,128)(2,1)S(1)} %get-tuple-element.117), channel_id=1, source_target_pairs={{2,0},{3,1},{6,4},{7,5},{10,8},{11,9},{14,12},{15,13},{18,16},{19,... | collective-permute-start | bytes 245768 | tf_op jit(solution)/shard_map/ppermute | solution.py:42
  36.1 0.8 fusion.328
  37.0 4.2 %collective-permute-done.3 = bf16[10,32,1,128]{3,1,2,0:T(8,128)(2,1)S(1)} collective-permute-done((bf16[10,32,1,128]{3,1,2,0:T(8,128)(2,1)S(1)}, bf16[10,32,1,128]{3,1,2,0:T(8,128)(2,1)S(1)}, u32[]{:S(2)}, u32[]{:S(2)}) %collective-permute-start.3) | collective-permute-done | bytes 81952 | tf_op jit(solution)/shard_map/ppermute | solution.py:42
  41.3 0.8 slice_bitcast_fusion.31
  42.1 1.3 %fusion.389 = (bf16[10,32,8,1]{3,1,2,0:T(8,128)(2,1)}, bf16[10,32,8,1]{3,1,2,0:T(8,128)(2,1)}) fusion(bf16[10,32,8,128]{3,1,2,0:T(8,128)(2,1)S(1)} %constant_dynamic-update-slice_fusion.4), kind=kLoop, calls=%fused_computation.692 | loop fusion | bytes 20480 | tf_op jit(solution)/shard_map/slice | solution.py:40
  43.5 2.2 %copy.26 = bf16[10,32,8,1]{1,2,3,0:T(8,128)(2,1)} copy(bf16[10,32,8,1]{3,1,2,0:T(8,128)(2,1)} %get-tuple-element.114) | data formatting | bytes 10240 | tf_op jit(solution)/shard_map/slice | solution.py:40
  45.7 2.2 %copy.27 = bf16[10,32,8,1]{1,2,3,0:T(8,128)(2,1)} copy(bf16[10,32,8,1]{3,1,2,0:T(8,128)(2,1)} %get-tuple-element.115) | data formatting | bytes 10240 | tf_op jit(solution)/shard_map/slice | solution.py:42
  47.9 1.3 %collective-permute-start.5 = (bf16[10,32,8,1]{1,2,3,0:T(8,128)(2,1)}, bf16[10,32,8,1]{1,2,3,0:T(8,128)(2,1)}, u32[]{:S(2)}, u32[]{:S(2)}) collective-permute-start(bf16[10,32,8,1]{1,2,3,0:T(8,128)(2,1)} %copy.27), channel_id=1, source_target_pairs={{1,0},{3,2},{5,4},{7,6},{9,8},{11,10},{13,12},{15,14},{17,16},{19,... | collective-permute-start | bytes 15368 | tf_op jit(solution)/shard_map/ppermute | solution.py:42
  49.2 4.2 %collective-permute-start.4 = (bf16[10,32,8,1]{1,2,3,0:T(8,128)(2,1)}, bf16[10,32,8,1]{1,2,3,0:T(8,128)(2,1)}, u32[]{:S(2)}, u32[]{:S(2)}) collective-permute-start(bf16[10,32,8,1]{1,2,3,0:T(8,128)(2,1)} %copy.26), channel_id=1, source_target_pairs={{0,1},{2,3},{4,5},{6,7},{8,9},{10,11},{12,13},{14,15},{16,17},{18,... | collective-permute-start | bytes 15368 | tf_op jit(solution)/shard_map/ppermute | solution.py:39
  53.4 1.5 %constant_dynamic-update-slice_fusion.27 = bf16[19,32,8,128]{3,1,2,0:T(8,128)(2,1)} fusion(bf16[19,32,8,128]{3,1,2,0:T(8,128)(2,1)} %get-tuple-element.106, bf16[32,10,128]{2,0,1:T(8,128)(2,1)} %get-tuple-element.103), kind=kLoop, calls=%fused_computation.548 | loop fusion | bytes 131072
  54.9 1.5 %constant_dynamic-update-slice_fusion.26 = bf16[19,32,8,128]{3,1,2,0:T(8,128)(2,1)} fusion(bf16[19,32,8,128]{3,1,2,0:T(8,128)(2,1)} %constant_dynamic-update-slice_fusion.27, bf16[32,10,128]{2,0,1:T(8,128)(2,1)} %get-tuple-element.102), kind=kLoop, calls=%fused_computation.547 | loop fusion | bytes 131072
  56.4 2.1 %copy.28 = bf16[10,32,8,1]{3,1,2,0:T(8,128)(2,1)} copy(bf16[10,32,8,1]{1,2,3,0:T(8,128)(2,1)} %collective-permute-done.4) | data formatting | bytes 10240 | tf_op jit(solution)/shard_map/ppermute | solution.py:39
  58.5 2.1 %copy.29 = bf16[10,32,8,1]{3,1,2,0:T(8,128)(2,1)} copy(bf16[10,32,8,1]{1,2,3,0:T(8,128)(2,1)} %collective-permute-done.5) | data formatting | bytes 10240 | tf_op jit(solution)/shard_map/ppermute | solution.py:42
  60.6 2.1 %pad_maximum_fusion = bf16[10,32,8,130]{3,1,2,0:T(8,128)(2,1)S(1)} fusion(bf16[10,32,8,1]{3,1,2,0:T(8,128)(2,1)} %copy.29, bf16[10,32,8,128]{3,1,2,0:T(8,128)(2,1)S(1)} %constant_dynamic-update-slice_fusion.4, bf16[10,32,8,1]{3,1,2,0:T(8,128)(2,1)} %copy.28), kind=kLoop, calls=%fused_computation.34 | loop fusion | flops 1996800 | bytes 1331200 | tf_op jit(solution)/shard_map/concatenate | solution.py:43
  62.7 0.1 slice_bitcast_fusion.21
  62.9 0.1 constant_dynamic-update-slice_fusion.25
  63.1 0.1 constant_dynamic-update-slice_fusion.19
  63.3 0.1 constant_dynamic-update-slice_fusion.16
  63.5 0.1 constant_dynamic-update-slice_fusion.12
  63.6 1.1 %fusion.1 = (f32[19,32,8,128]{3,1,2,0:T(8,128)S(1)}, f32[19,32,8,128]{3,1,2,0:T(8,128)S(1)}, f32[19,32,8,128]{3,1,2,0:T(8,128)S(1)}) fusion(bf16[19,32,8,128]{3,1,2,0:T(8,128)(2,1)S(1)} %constant_dynamic-update-slice_fusion.12, pred[32,8,128]{2,0,1:T(8,128)(4,1)S(1)} %copy.19, pred[32,8,128]{2,0,1:T(8,128)(4,1)S(1)} %copy.18, pred[32,8,128]{2,0,1:T(8,128)(4,1)S(1)} %copy.31), kind=kLoop, calls=%fused_computation.3 | loop fusion | flops 5603328 | bytes 8814592 | tf_op jit(solution)/shard_map/transpose(jvp(jit(_where)))/select_n | solution.py:89
  64.7 0.3 bitcast_add_fusion.11
  65.0 0.4 copy-done.5
  65.5 0.5 bitcast_add_fusion.17
  66.0 0.2 fusion.34
  66.2 0.7 fusion.60
  66.9 0.7 bitcast_add_fusion.16
  67.6 2.8 %negate_add_fusion = (f32[32,8,128]{2,0,1:T(8,128)S(1)}, f32[32,8,128]{2,0,1:T(8,128)S(1)}, f32[32,8,128]{2,0,1:T(8,128)S(1)}, f32[32,8,128]{2,0,1:T(8,128)S(1)}...) fusion(f32[32,8,128]{2,0,1:T(8,128)S(1)} %get-tuple-element.15, ...), kind=kLoop, calls=%fused_computation.452 | loop fusion | flops 17006592 | bytes 12320768 | tf_op jit(solution)/shard_map/transpose(jvp())/add_any | solution.py:72
  70.4 0.3 fusion.273
  70.7 0.2 fusion.308
  70.9 0.2 fusion.310
  71.2 4.5 %collective-permute-start.12 = (f32[1,4,34]{2,0,1:T(1,128)S(1)}, f32[1,4,34]{2,0,1:T(1,128)S(1)}, u32[]{:S(2)}, u32[]{:S(2)}) collective-permute-start(f32[1,4,34]{2,0,1:T(1,128)S(1)} %get-tuple-element.141), channel_id=1, source_target_pairs={{0,4},{4,8},{8,12},{1,5},{5,9},{9,13},{2,6},{6,10},{10,14},{3,7},{... | collective-permute-start | bytes 1640 | tf_op jit(solution)/shard_map/ppermute | solution.py:39
  75.7 1.3 %collective-permute-start.13 = (f32[1,4,34]{2,0,1:T(1,128)S(1)}, f32[1,4,34]{2,0,1:T(1,128)S(1)}, u32[]{:S(2)}, u32[]{:S(2)}) collective-permute-start(f32[1,4,34]{2,0,1:T(1,128)S(1)} %get-tuple-element.142), channel_id=1, source_target_pairs={{4,0},{8,4},{12,8},{5,1},{9,5},{13,9},{6,2},{10,6},{14,10},{7,3},{... | collective-permute-start | bytes 1640 | tf_op jit(solution)/shard_map/ppermute | solution.py:42
  77.0 0.3 fusion.387
  77.3 3.9 %collective-permute-done.13 = f32[1,4,34]{2,0,1:T(1,128)S(1)} collective-permute-done((f32[1,4,34]{2,0,1:T(1,128)S(1)}, f32[1,4,34]{2,0,1:T(1,128)S(1)}, u32[]{:S(2)}, u32[]{:S(2)}) %collective-permute-start.13) | collective-permute-done | bytes 576 | tf_op jit(solution)/shard_map/ppermute | solution.py:42
  81.2 1.6 %collective-permute-start.14 = (f32[12,1,34]{2,0,1:T(8,128)S(1)}, f32[12,1,34]{2,0,1:T(8,128)S(1)}, u32[]{:S(2)}, u32[]{:S(2)}) collective-permute-start(f32[12,1,34]{2,0,1:T(8,128)S(1)} %get-tuple-element.139), channel_id=1, source_target_pairs={{0,2},{1,3},{4,6},{5,7},{8,10},{9,11},{12,14},{13,15},{16,18},{17,... | collective-permute-start | bytes 4904 | tf_op jit(solution)/shard_map/ppermute | solution.py:39
  82.8 1.3 %collective-permute-start.15 = (f32[12,1,34]{2,0,1:T(8,128)S(1)}, f32[12,1,34]{2,0,1:T(8,128)S(1)}, u32[]{:S(2)}, u32[]{:S(2)}) collective-permute-start(f32[12,1,34]{2,0,1:T(8,128)S(1)} %get-tuple-element.140), channel_id=1, source_target_pairs={{2,0},{3,1},{6,4},{7,5},{10,8},{11,9},{14,12},{15,13},{18,16},{19,... | collective-permute-start | bytes 4904 | tf_op jit(solution)/shard_map/ppermute | solution.py:42
  84.2 4.2 %collective-permute-done.15 = f32[12,1,34]{2,0,1:T(8,128)S(1)} collective-permute-done((f32[12,1,34]{2,0,1:T(8,128)S(1)}, f32[12,1,34]{2,0,1:T(8,128)S(1)}, u32[]{:S(2)}, u32[]{:S(2)}) %collective-permute-start.15) | collective-permute-done | bytes 1664 | tf_op jit(solution)/shard_map/ppermute | solution.py:42
  88.4 1.3 %collective-permute-start.16 = (f32[12,6,1]{2,0,1:T(8,128)S(1)}, f32[12,6,1]{2,0,1:T(8,128)S(1)}, u32[]{:S(2)}, u32[]{:S(2)}) collective-permute-start(f32[12,6,1]{2,0,1:T(8,128)S(1)} %get-tuple-element.137), channel_id=1, source_target_pairs={{0,1},{2,3},{4,5},{6,7},{8,9},{10,11},{12,13},{14,15},{16,17},{18,... | collective-permute-start | bytes 872 | tf_op jit(solution)/shard_map/ppermute | solution.py:39
  89.7 1.3 %collective-permute-start.17 = (f32[12,6,1]{2,0,1:T(8,128)S(1)}, f32[12,6,1]{2,0,1:T(8,128)S(1)}, u32[]{:S(2)}, u32[]{:S(2)}) collective-permute-start(f32[12,6,1]{2,0,1:T(8,128)S(1)} %get-tuple-element.138), channel_id=1, source_target_pairs={{1,0},{3,2},{5,4},{7,6},{9,8},{11,10},{13,12},{15,14},{17,16},{19,... | collective-permute-start | bytes 872 | tf_op jit(solution)/shard_map/ppermute | solution.py:42
  91.0 1.3 %add_convert_fusion = bf16[19,32,8,128]{3,1,2,0:T(8,128)(2,1)S(1)} fusion(f32[1,32,8,128]{3,1,2,0:T(8,128)S(1)} %get-tuple-element.130, f32[1,32,8,128]{3,1,2,0:T(8,128)S(1)} %get-tuple-element.131, bf16[19,32,8,128]{3,1,2,0:T(8,128)(2,1)S(1)} %constant_dynamic-update-slice_fusion.12, f32[1,32,8,128]{3,1,2,0:T(8,128)S(1)} %get-tuple-element.132, ...), kind=kLoop, calls=%fused_computation.33 | loop fusion | flops 36732928 | bytes 5832723 | tf_op jit(solution)/shard_map/convert_element_type | solution.py:157
  92.3 1.6 %copy.32 = bf16[19,32,8,128]{3,2,1,0:T(8,128)(2,1)} copy(bf16[19,32,8,128]{3,1,2,0:T(8,128)(2,1)S(1)} %add_convert_fusion) | data formatting | bytes 2490368
  94.4 0.6 copy.33
  (84 shorter events, 1.8 us)
Async XLA Ops:
  0.6 15.3 %copy-start.1 = (bf16[19,32,8,128]{3,2,1,0:T(8,128)(2,1)S(1)}, bf16[19,32,8,128]{3,2,1,0:T(8,128)(2,1)}, u32[]{:S(2)}) copy-start(bf16[19,32,8,128]{3,2,1,0:T(8,128)(2,1)} %param.4) | copy-start | bytes 3735556
  1.4 16.3 %collective-permute-start.7 = (f32[1,2,32]{2,1,0:T(2,128)S(1)}, f32[1,2,32]{2,1,0:T(2,128)S(1)}, u32[]{:S(2)}, u32[]{:S(2)}) collective-permute-start(f32[1,2,32]{2,1,0:T(2,128)S(1)} %get-tuple-element.147), channel_id=1, source_target_pairs={{4,0},{8,4},{12,8},{5,1},{9,5},{13,9},{6,2},{10,6},{14,10},{7,3},{... | collective-permute-start | bytes 776 | tf_op jit(solution)/shard_map/ppermute | solution.py:42
  2.7 14.9 %collective-permute-start.6 = (f32[1,2,32]{2,1,0:T(2,128)S(1)}, f32[1,2,32]{2,1,0:T(2,128)S(1)}, u32[]{:S(2)}, u32[]{:S(2)}) collective-permute-start(f32[1,2,32]{2,1,0:T(2,128)S(1)} %get-tuple-element.148), channel_id=1, source_target_pairs={{0,4},{4,8},{8,12},{1,5},{5,9},{9,13},{2,6},{6,10},{10,14},{3,7},{... | collective-permute-start | bytes 776 | tf_op jit(solution)/shard_map/ppermute | solution.py:39
  10.7 20.9 %collective-permute-start.1 = (bf16[10,1,8,128]{3,1,2,0:T(2,128)(2,1)S(1)}, bf16[10,1,8,128]{3,1,2,0:T(2,128)(2,1)S(1)}, u32[]{:S(2)}, u32[]{:S(2)}) collective-permute-start(bf16[10,1,8,128]{3,1,2,0:T(2,128)(2,1)S(1)} %get-tuple-element.118), channel_id=1, source_target_pairs={{0,4},{4,8},{8,12},{1,5},{5,9},{9,13},{2,6},{6,10},{10,14},{3,7},{... | collective-permute-start | bytes 61448 | tf_op jit(solution)/shard_map/ppermute | solution.py:39
  14.7 16.8 %collective-permute-start = (bf16[10,1,8,128]{3,1,2,0:T(2,128)(2,1)S(1)}, bf16[10,1,8,128]{3,1,2,0:T(2,128)(2,1)S(1)}, u32[]{:S(2)}, u32[]{:S(2)}) collective-permute-start(bf16[10,1,8,128]{3,1,2,0:T(2,128)(2,1)S(1)} %get-tuple-element.119), channel_id=1, source_target_pairs={{4,0},{8,4},{12,8},{5,1},{9,5},{13,9},{6,2},{10,6},{14,10},{7,3},{... | collective-permute-start | bytes 61448 | tf_op jit(solution)/shard_map/ppermute | solution.py:42
  16.0 0.9 copy-start.4
  16.0 1.0 %slice-start = ((bf16[19,32,8,128]{3,2,1,0:T(8,128)(2,1)}), bf16[1,32,8,128]{3,2,1,0:T(8,128)(2,1)S(1)}, s32[]{:S(2)}) async-start(bf16[19,32,8,128]{3,2,1,0:T(8,128)(2,1)} %param.5), calls=%async_computation | async-start | bytes 131072 | tf_op jit(solution)/shard_map/slice | solution.py:142
  16.1 1.6 %copy-start.6 = (f32[8,2,32]{2,1,0:T(2,128)S(1)}, f32[8,2,32]{2,1,0:T(2,128)}, u32[]{:S(2)}) copy-start(f32[8,2,32]{2,1,0:T(2,128)} %param.6) | copy-start | bytes 6148
  17.6 15.5 %slice-start.1 = ((bf16[19,32,8,128]{3,2,1,0:T(8,128)(2,1)}), bf16[4,32,8,128]{3,2,1,0:T(8,128)(2,1)S(1)}, s32[]{:S(2)}) async-start(bf16[19,32,8,128]{3,2,1,0:T(8,128)(2,1)} %param.5), calls=%async_computation.1 | async-start | bytes 524288 | tf_op jit(solution)/shard_map/slice | solution.py:142
  17.7 4.8 %collective-permute-start.8 = (f32[10,1,32]{2,1,0:T(1,128)S(1)}, f32[10,1,32]{2,1,0:T(1,128)S(1)}, u32[]{:S(2)}, u32[]{:S(2)}) collective-permute-start(f32[10,1,32]{2,1,0:T(1,128)S(1)} %get-tuple-element.145), channel_id=1, source_target_pairs={{0,2},{1,3},{4,6},{5,7},{8,10},{9,11},{12,14},{13,15},{16,18},{17,... | collective-permute-start | bytes 3848 | tf_op jit(solution)/shard_map/ppermute | solution.py:39
  21.1 5.5 %collective-permute-start.9 = (f32[10,1,32]{2,1,0:T(1,128)S(1)}, f32[10,1,32]{2,1,0:T(1,128)S(1)}, u32[]{:S(2)}, u32[]{:S(2)}) collective-permute-start(f32[10,1,32]{2,1,0:T(1,128)S(1)} %get-tuple-element.146), channel_id=1, source_target_pairs={{2,0},{3,1},{6,4},{7,5},{10,8},{11,9},{14,12},{15,13},{18,16},{19,... | collective-permute-start | bytes 3848 | tf_op jit(solution)/shard_map/ppermute | solution.py:42
  26.8 2.6 %collective-permute-start.10 = (f32[10,4,1]{2,1,0:T(4,128)S(1)}, f32[10,4,1]{2,1,0:T(4,128)S(1)}, u32[]{:S(2)}, u32[]{:S(2)}) collective-permute-start(f32[10,4,1]{2,1,0:T(4,128)S(1)} %get-tuple-element.143), channel_id=1, source_target_pairs={{0,1},{2,3},{4,5},{6,7},{8,9},{10,11},{12,13},{14,15},{16,17},{18,... | collective-permute-start | bytes 488 | tf_op jit(solution)/shard_map/ppermute | solution.py:39
  28.1 3.1 %collective-permute-start.11 = (f32[10,4,1]{2,1,0:T(4,128)S(1)}, f32[10,4,1]{2,1,0:T(4,128)S(1)}, u32[]{:S(2)}, u32[]{:S(2)}) collective-permute-start(f32[10,4,1]{2,1,0:T(4,128)S(1)} %get-tuple-element.144), channel_id=1, source_target_pairs={{1,0},{3,2},{5,4},{7,6},{9,8},{11,10},{13,12},{15,14},{17,16},{19,... | collective-permute-start | bytes 488 | tf_op jit(solution)/shard_map/ppermute | solution.py:42
  33.2 3.8 %collective-permute-start.2 = (bf16[10,32,1,128]{3,1,2,0:T(8,128)(2,1)S(1)}, bf16[10,32,1,128]{3,1,2,0:T(8,128)(2,1)S(1)}, u32[]{:S(2)}, u32[]{:S(2)}) collective-permute-start(bf16[10,32,1,128]{3,1,2,0:T(8,128)(2,1)S(1)} %get-tuple-element.116), channel_id=1, source_target_pairs={{0,2},{1,3},{4,6},{5,7},{8,10},{9,11},{12,14},{13,15},{16,18},{17,... | collective-permute-start | bytes 245768 | tf_op jit(solution)/shard_map/ppermute | solution.py:39
  34.8 6.3 %collective-permute-start.3 = (bf16[10,32,1,128]{3,1,2,0:T(8,128)(2,1)S(1)}, bf16[10,32,1,128]{3,1,2,0:T(8,128)(2,1)S(1)}, u32[]{:S(2)}, u32[]{:S(2)}) collective-permute-start(bf16[10,32,1,128]{3,1,2,0:T(8,128)(2,1)S(1)} %get-tuple-element.117), channel_id=1, source_target_pairs={{2,0},{3,1},{6,4},{7,5},{10,8},{11,9},{14,12},{15,13},{18,16},{19,... | collective-permute-start | bytes 245768 | tf_op jit(solution)/shard_map/ppermute | solution.py:42
  47.9 10.6 %collective-permute-start.5 = (bf16[10,32,8,1]{1,2,3,0:T(8,128)(2,1)}, bf16[10,32,8,1]{1,2,3,0:T(8,128)(2,1)}, u32[]{:S(2)}, u32[]{:S(2)}) collective-permute-start(bf16[10,32,8,1]{1,2,3,0:T(8,128)(2,1)} %copy.27), channel_id=1, source_target_pairs={{1,0},{3,2},{5,4},{7,6},{9,8},{11,10},{13,12},{15,14},{17,16},{19,... | collective-permute-start | bytes 15368 | tf_op jit(solution)/shard_map/ppermute | solution.py:42
  49.2 7.2 %collective-permute-start.4 = (bf16[10,32,8,1]{1,2,3,0:T(8,128)(2,1)}, bf16[10,32,8,1]{1,2,3,0:T(8,128)(2,1)}, u32[]{:S(2)}, u32[]{:S(2)}) collective-permute-start(bf16[10,32,8,1]{1,2,3,0:T(8,128)(2,1)} %copy.26), channel_id=1, source_target_pairs={{0,1},{2,3},{4,5},{6,7},{8,9},{10,11},{12,13},{14,15},{16,17},{18,... | collective-permute-start | bytes 15368 | tf_op jit(solution)/shard_map/ppermute | solution.py:39
  60.6 2.3 %copy-start = (bf16[19,32,8,128]{3,1,2,0:T(8,128)(2,1)S(1)}, bf16[19,32,8,128]{3,1,2,0:T(8,128)(2,1)}, u32[]{:S(2)}) copy-start(bf16[19,32,8,128]{3,1,2,0:T(8,128)(2,1)} %constant_dynamic-update-slice_fusion.26) | copy-start | bytes 3735556
  60.6 2.4 %copy-start.3 = (bf16[32,10,128]{2,0,1:T(8,128)(2,1)S(1)}, bf16[32,10,128]{2,0,1:T(8,128)(2,1)}, u32[]{:S(2)}) copy-start(bf16[32,10,128]{2,0,1:T(8,128)(2,1)} %get-tuple-element.97) | copy-start | bytes 245764
  60.6 2.4 %copy-start.2 = (bf16[32,10,128]{2,0,1:T(8,128)(2,1)S(1)}, bf16[32,10,128]{2,0,1:T(8,128)(2,1)}, u32[]{:S(2)}) copy-start(bf16[32,10,128]{2,0,1:T(8,128)(2,1)} %get-tuple-element.96) | copy-start | bytes 245764
  64.7 0.8 copy-start.5
  71.2 6.2 %collective-permute-start.12 = (f32[1,4,34]{2,0,1:T(1,128)S(1)}, f32[1,4,34]{2,0,1:T(1,128)S(1)}, u32[]{:S(2)}, u32[]{:S(2)}) collective-permute-start(f32[1,4,34]{2,0,1:T(1,128)S(1)} %get-tuple-element.141), channel_id=1, source_target_pairs={{0,4},{4,8},{8,12},{1,5},{5,9},{9,13},{2,6},{6,10},{10,14},{3,7},{... | collective-permute-start | bytes 1640 | tf_op jit(solution)/shard_map/ppermute | solution.py:39
  75.7 5.5 %collective-permute-start.13 = (f32[1,4,34]{2,0,1:T(1,128)S(1)}, f32[1,4,34]{2,0,1:T(1,128)S(1)}, u32[]{:S(2)}, u32[]{:S(2)}) collective-permute-start(f32[1,4,34]{2,0,1:T(1,128)S(1)} %get-tuple-element.142), channel_id=1, source_target_pairs={{4,0},{8,4},{12,8},{5,1},{9,5},{13,9},{6,2},{10,6},{14,10},{7,3},{... | collective-permute-start | bytes 1640 | tf_op jit(solution)/shard_map/ppermute | solution.py:42
  77.0 14.0 %copy-start.10 = (pred[19]{0:T(512)(128)(4,1)S(1)}, pred[19]{0:T(512)(128)(4,1)}, u32[]{:S(2)}) copy-start(pred[19]{0:T(512)(128)(4,1)} %constant.77.clone.1) | copy-start | bytes 61
  81.2 2.9 %collective-permute-start.14 = (f32[12,1,34]{2,0,1:T(8,128)S(1)}, f32[12,1,34]{2,0,1:T(8,128)S(1)}, u32[]{:S(2)}, u32[]{:S(2)}) collective-permute-start(f32[12,1,34]{2,0,1:T(8,128)S(1)} %get-tuple-element.139), channel_id=1, source_target_pairs={{0,2},{1,3},{4,6},{5,7},{8,10},{9,11},{12,14},{13,15},{16,18},{17,... | collective-permute-start | bytes 4904 | tf_op jit(solution)/shard_map/ppermute | solution.py:39
  82.8 5.5 %collective-permute-start.15 = (f32[12,1,34]{2,0,1:T(8,128)S(1)}, f32[12,1,34]{2,0,1:T(8,128)S(1)}, u32[]{:S(2)}, u32[]{:S(2)}) collective-permute-start(f32[12,1,34]{2,0,1:T(8,128)S(1)} %get-tuple-element.140), channel_id=1, source_target_pairs={{2,0},{3,1},{6,4},{7,5},{10,8},{11,9},{14,12},{15,13},{18,16},{19,... | collective-permute-start | bytes 4904 | tf_op jit(solution)/shard_map/ppermute | solution.py:42
  88.4 5.5 %collective-permute-start.16 = (f32[12,6,1]{2,0,1:T(8,128)S(1)}, f32[12,6,1]{2,0,1:T(8,128)S(1)}, u32[]{:S(2)}, u32[]{:S(2)}) collective-permute-start(f32[12,6,1]{2,0,1:T(8,128)S(1)} %get-tuple-element.137), channel_id=1, source_target_pairs={{0,1},{2,3},{4,5},{6,7},{8,9},{10,11},{12,13},{14,15},{16,17},{18,... | collective-permute-start | bytes 872 | tf_op jit(solution)/shard_map/ppermute | solution.py:39
  89.7 4.2 %collective-permute-start.17 = (f32[12,6,1]{2,0,1:T(8,128)S(1)}, f32[12,6,1]{2,0,1:T(8,128)S(1)}, u32[]{:S(2)}, u32[]{:S(2)}) collective-permute-start(f32[12,6,1]{2,0,1:T(8,128)S(1)} %get-tuple-element.138), channel_id=1, source_target_pairs={{1,0},{3,2},{5,4},{7,6},{9,8},{11,10},{13,12},{15,14},{17,16},{19,... | collective-permute-start | bytes 872 | tf_op jit(solution)/shard_map/ppermute | solution.py:42
  92.3 1.7 %copy-start.9 = (pred[8]{0:T(512)(128)(4,1)S(1)}, pred[8]{0:T(512)(128)(4,1)}, u32[]{:S(2)}) copy-start(pred[8]{0:T(512)(128)(4,1)} %constant.95.clone.1) | copy-start | bytes 28
  92.3 1.8 %copy-start.8 = (pred[2]{0:T(512)(128)(4,1)S(1)}, pred[2]{0:T(512)(128)(4,1)}, u32[]{:S(2)}) copy-start(pred[2]{0:T(512)(128)(4,1)} %constant.96.clone.1) | copy-start | bytes 10
  92.3 2.0 %copy-start.7 = (pred[32]{0:T(512)(128)(4,1)S(1)}, pred[32]{0:T(512)(128)(4,1)}, u32[]{:S(2)}) copy-start(pred[32]{0:T(512)(128)(4,1)} %constant.97.clone.1) | copy-start | bytes 100
where the time goes:
time: 96.6 us; the launch traced here: 95 us
  starting transfers between devices  39 us (40%)
  local copies, waits for them, and re-layouts  22.3 us (23%)
  waiting for transfers between devices  18.2 us (19%)
  other arithmetic  11.9 us (12%)
  matrix products  2.35 us (2%)
  between operations  1.35 us (1%)
    ppermute x9, starting transfers between devices, padded(): lax.ppermute(lax.slice_in_dim(block, block.shape[dim] - width, None, axis...  27.4 us
    ppermute x9, waiting for transfers between devices, padded(): lax.ppermute(lax.slice_in_dim(block, 0, width, axis=dim), axis, backward)  18.1 us
    ppermute x9, starting transfers between devices, padded(): lax.ppermute(lax.slice_in_dim(block, 0, width, axis=dim), axis, backward)  11.6 us
    unnamed x47, local copies, waits for them, and re-layouts  7.38 us
    slice x8, local copies, waits for them, and re-layouts, padded(): lax.slice_in_dim(block, block.shape[dim] - width, None, axis=dim)  3.82 us
    slice x2, local copies, waits for them, and re-layouts, padded(): lax.slice_in_dim(block, 0, width, axis=dim)  3.02 us
    add_any x1, other arithmetic, collide(): flow_x = moment(populations, 0) / density  2.81 us
    concatenate x6, other arithmetic, padded(): block = jnp.concatenate([low, block, high], axis=dim)  2.48 us
  transfers between devices with their start and end apart: 18, of which 5 were waited for; matrix products, arithmetic and copies ran while one was open for 14% of the time, Pallas kernels for 0%

commit v1 on v0

--- a/solution.py
+++ b/solution.py
@@ -31,17 +31,55 @@
 highest = lax.Precision.HIGHEST
 
 
-def padded(block, sides, width):
-    for axis, dim in sides:
-        count = lax.axis_size(axis)
+def exchange(low_parts, high_parts, axis):
+    count = lax.axis_size(axis)
+    shapes = [part.shape for part in high_parts]
+    types = [part.dtype for part in high_parts]
+    sizes = [part.size for part in high_parts]
+    wire = jnp.result_type(*types)
+    low = jnp.concatenate([part.astype(wire).reshape(-1) for part in low_parts])
+    high = jnp.concatenate([part.astype(wire).reshape(-1) for part in high_parts])
+    if count == 1:
+        from_prev = jnp.zeros_like(high)
+        from_next = jnp.zeros_like(low)
+    elif count == 2:
+        index = lax.axis_index(axis)
+        received = lax.ppermute(jnp.where(index == 0, high, low), axis, [(0, 1), (1, 0)])
+        from_prev = jnp.where(index == 1, received, jnp.zeros_like(received))
+        from_next = jnp.where(index == 0, received, jnp.zeros_like(received))
+    else:
         forward = [(i, i + 1) for i in range(count - 1)]
         backward = [(target, source) for source, target in forward]
-        low = lax.ppermute(
-            lax.slice_in_dim(block, block.shape[dim] - width, None, axis=dim), axis, forward
-        )
-        high = lax.ppermute(lax.slice_in_dim(block, 0, width, axis=dim), axis, backward)
-        block = jnp.concatenate([low, block, high], axis=dim)
-    return block
+        from_prev = lax.ppermute(high, axis, forward)
+        from_next = lax.ppermute(low, axis, backward)
+
+    def split(flat):
+        pieces = []
+        offset = 0
+        for shape, dtype, size in zip(shapes, types, sizes):
+            pieces.append(flat[offset : offset + size].reshape(shape).astype(dtype))
+            offset += size
+        return pieces
+
+    return split(from_prev), split(from_next)
+
+
+def faces(block, dim):
+    length = block.shape[dim]
+    return (
+        lax.slice_in_dim(block, 0, 1, axis=dim),
+        lax.slice_in_dim(block, length - 1, length, axis=dim),
+    )
+
+
+def padded_pair(coef, coef_dim, pops, pops_dim, axis):
+    coef_low, coef_high = faces(coef, coef_dim)
+    pops_low, pops_high = faces(pops, pops_dim)
+    coef_prev, coef_next = exchange([coef_low], [coef_high], axis)
+    pops_prev, pops_next = exchange([pops_low], [pops_high], axis)
+    coef = jnp.concatenate([coef_prev[0], coef, coef_next[0]], axis=coef_dim)
+    pops = jnp.concatenate([pops_prev[0], pops, pops_next[0]], axis=pops_dim)
+    return coef, pops
 
 
 def equilibrium(density, flow_x, flow_y, flow_z):
@@ -113,39 +151,37 @@
     return result
 
 
-def fold_rim(bordered, dimension):
-    length_here = bordered.shape[dimension]
-    middle = lax.slice_in_dim(bordered, 2, length_here - 2, axis=dimension)
-    head_slice = lax.slice_in_dim(bordered, 0, 1, axis=dimension)
-    tail_slice = lax.slice_in_dim(bordered, length_here - 1, length_here, axis=dimension)
-    middle_count = length_here - 4
+def fold_rim(partial, dimension, axis):
+    length_here = partial.shape[dimension]
+    low, high = faces(partial, dimension)
+    from_prev, from_next = exchange([low], [high], axis)
+    middle = lax.slice_in_dim(partial, 1, length_here - 1, axis=dimension)
+    middle_count = length_here - 2
     head_pads = [(0, 0)] * 3
     tail_pads = [(0, 0)] * 3
     head_pads[dimension] = (0, middle_count - 1)
     tail_pads[dimension] = (middle_count - 1, 0)
-    return middle + jnp.pad(head_slice, head_pads) + jnp.pad(tail_slice, tail_pads)
+    return middle + jnp.pad(from_prev[0], head_pads) + jnp.pad(from_next[0], tail_pads)
 
 
 def per_device(forward_pops, adjoint_pops, coefficients, node_kind):
     cells_x, cells_y, cells_z = node_kind.shape
     coarse_x, coarse_y, coarse_z = coefficients.shape
-    window = padded(coefficients, (("gx", 0), ("gy", 1), ("gz", 2)), 1)
     basis_x = basis_matrix(cells_x, coarse_x + 2, 0, -1)
     basis_y = basis_matrix(cells_y, coarse_y + 2, 0, -1)
     basis_z = basis_matrix(cells_z, coarse_z + 2, 0, -1)
+    lane_list = [adjoint_pops[component] for component in range(19)]
+    window = coefficients
+    for dimension, axis in ((0, "gx"), (1, "gy"), (2, "gz")):
+        stacked = jnp.stack([lane_list[component] for component in moving(dimension)])
+        window, extended = padded_pair(window, dimension, stacked, dimension + 1, axis)
+        lane_list = pull_along(lane_list, dimension, extended)
     partway = jnp.einsum("ijk,zk->ijz", window, basis_z, precision=highest)
     partway = jnp.einsum("ijz,yj->iyz", partway, basis_y, precision=highest)
     level_set = jnp.einsum("iyz,xi->xyz", partway, basis_x, precision=highest)
     bent = jnp.tanh(4.0 * level_set)
     porosity = 0.45 * (1.0 - bent)
     slope_phi = -1.8 * (1.0 - bent * bent)
-    lane_list = [adjoint_pops[component] for component in range(19)]
-    extended = padded(jnp.stack([lane_list[component] for component in moving(0)]), (("gx", 1),), 1)
-    lane_list = pull_along(lane_list, 0, extended)
-    extended = padded(jnp.stack([lane_list[component] for component in moving(1)]), (("gy", 2),), 1)
-    lane_list = pull_along(lane_list, 1, extended)
-    extended = padded(jnp.stack([lane_list[component] for component in moving(2)]), (("gz", 3),), 1)
-    lane_list = pull_along(lane_list, 2, extended)
     pulled = jnp.stack(lane_list).astype(jnp.float32)
     forward = forward_pops.astype(jnp.float32)
 
@@ -159,8 +195,7 @@
     partial_value = jnp.einsum("xyz,xi->iyz", sensitivity, basis_x, precision=highest)
     partial_value = jnp.einsum("iyz,yj->ijz", partial_value, basis_y, precision=highest)
     partial_value = jnp.einsum("ijz,zk->ijk", partial_value, basis_z, precision=highest)
-    bordered = padded(partial_value, (("gx", 0), ("gy", 1), ("gz", 2)), 1)
-    gradient = fold_rim(fold_rim(fold_rim(bordered, 0), 1), 2)
+    gradient = fold_rim(fold_rim(fold_rim(partial_value, 0, "gx"), 1, "gy"), 2, "gz")
     return (prior_adjoint, gradient)
 
 

time: 96.6 us -> 99.3 us (1.028)
  local copies, waits for them, and re-layouts: 22.3 us -> 38.4 us
  other arithmetic: 11.9 us -> 27.8 us
  waiting for transfers between devices: 18.2 us -> 2.55 us
  starting transfers between devices: 39 us -> 23.9 us
  matrix products: 2.35 us -> 3.52 us
    ppermute x18 -> x12, waiting for transfers between devices: 18.2 us -> 2.55 us  [the longest x6 2.27 us: exchange(): lax.ppermute(jnp.where(index == 0, high, low), axis, [(0, 1), (1, 0)])]
    ppermute x18 -> x12, starting transfers between devices: 39 us -> 23.9 us  [the longest x3 15.3 us: exchange(): from_prev = lax.ppermute(high, axis, forward)]
    reshape x0 -> x24, local copies, waits for them, and re-layouts: none -> 14.3 us  [the longest x20 13.4 us: split(): pieces.append(flat[offset:offset + size].reshape(shape).astype(dtype))]
    select_n x0 -> x12, other arithmetic: none -> 5.29 us  [the longest x6 3.5 us: exchange(): jnp.where(index == 0, high, low)]
    slice x12 -> x3, local copies, waits for them, and re-layouts: 6.92 us -> 1.66 us  [the longest x2 0.86 us: faces(): lax.slice_in_dim(block, length - 1, length, axis=dim)]
    select_n x0 -> x7, local copies, waits for them, and re-layouts: none -> 5.02 us  [exchange(): jnp.where(index == 0, high, low)]
    ppermute x2 -> x0, local copies, waits for them, and re-layouts: 4.24 us -> none  [the longest x1 2.13 us: padded(): lax.ppermute(lax.slice_in_dim(block, block.shape[dim] - width, None, axis...]
    convert_element_type x1, other arithmetic: 1.27 us -> 5.13 us  [per_device(): prior_adjoint = prior.astype(jnp.bfloat16)]
  transfers between devices with their start and end apart: 18 -> 12, of which waited for: 5 -> 3; matrix products, arithmetic and copies ran while one was open for 14% -> 38% of each run, Pallas kernels for 0% -> 0%
where the time goes in v1:
time: 99.3 us; the launch traced here: 97.4 us
  local copies, waits for them, and re-layouts  38.4 us (39%)
  other arithmetic  27.8 us (28%)
  starting transfers between devices  23.9 us (24%)
  matrix products  3.52 us (4%)
  waiting for transfers between devices  2.55 us (3%)
  between operations  1.2 us (1%)
    ppermute x3, starting transfers between devices, exchange(): from_prev = lax.ppermute(high, axis, forward)  15.3 us
    reshape x20, local copies, waits for them, and re-layouts, split(): pieces.append(flat[offset:offset + size].reshape(shape).astype(dtype))  13.4 us
    unnamed x61, local copies, waits for them, and re-layouts  8 us
    convert_element_type x1, other arithmetic, per_device(): prior_adjoint = prior.astype(jnp.bfloat16)  5.13 us
    select_n x7, local copies, waits for them, and re-layouts, exchange(): jnp.where(index == 0, high, low)  5.02 us
    ppermute x6, starting transfers between devices, exchange(): lax.ppermute(jnp.where(index == 0, high, low), axis, [(0, 1), (1, 0)])  4.68 us
    ppermute x3, starting transfers between devices, exchange(): from_next = lax.ppermute(low, axis, backward)  3.98 us
    select_n x6, other arithmetic, exchange(): jnp.where(index == 0, high, low)  3.5 us
  transfers between devices with their start and end apart: 12, of which 3 were waited for; matrix products, arithmetic and copies ran while one was open for 38% of the time, Pallas kernels for 0%

profile of v1, /device:TPU:0, one launch (start us, length us, event | category | flops | bytes accessed | tf_op | source)
XLA Modules:
  0.0 97.4 jit_solution(12207354664616205301)
XLA Ops:
  0.6 0.8 fusion.379
  1.5 4.9 %collective-permute-start.4 = (f32[64]{0:T(128)S(1)}, f32[64]{0:T(128)S(1)}, u32[]{:S(2)}, u32[]{:S(2)}) collective-permute-start(f32[64]{0:T(128)S(1)} %reshape.243), channel_id=1, source_target_pairs={{0,4},{4,8},{8,12},{1,5},{5,9},{9,13},{2,6},{6,10},{10,14},{3,7},{... | collective-permute-start | bytes 776 | tf_op jit(solution)/shard_map/ppermute | solution.py:53
  6.5 0.6 reshape.245
  7.1 1.4 %collective-permute-start.5 = (f32[64]{0:T(128)}, f32[64]{0:T(128)}, u32[]{:S(2)}, u32[]{:S(2)}) collective-permute-start(f32[64]{0:T(128)} %reshape.245), channel_id=1, source_target_pairs={{4,0},{8,4},{12,8},{5,1},{9,5},{13,9},{6,2},{10,6},{14,10},{7,3},{... | collective-permute-start | bytes 776 | tf_op jit(solution)/shard_map/ppermute | solution.py:54
  8.5 1.1 %fusion.378 = (bf16[2,32,8,128]{3,2,1,0:T(8,128)(2,1)S(1)}, bf16[2,32,8,128]{3,2,1,0:T(8,128)(2,1)S(1)}, bf16[2,32,8,128]{3,2,1,0:T(8,128)(2,1)S(1)}) fusion(bf16[19,32,8,128]{3,2,1,0:T(8,128)(2,1)} %param.5), kind=kLoop, calls=%fused_computation.695 | loop fusion | bytes 786432 | tf_op jit(solution)/shard_map/slice | solution.py:173
  9.6 1.1 %slice.358 = bf16[8,32,8,128]{3,2,1,0:T(8,128)(2,1)S(1)} slice(bf16[19,32,8,128]{3,2,1,0:T(8,128)(2,1)} %param.5), slice={[7:15], [0:32], [0:8], [0:128]} | slice | bytes 1048576 | tf_op jit(solution)/shard_map/slice | solution.py:173
  10.8 0.8 slice_reduce_fusion
  11.7 1.3 %collective-permute-start = (bf16[10240]{0:T(1024)(128)(2,1)}, bf16[10240]{0:T(1024)(128)(2,1)}, u32[]{:S(2)}, u32[]{:S(2)}) collective-permute-start(bf16[10240]{0:T(1024)(128)(2,1)} %bitcast.117), channel_id=1, source_target_pairs={{4,0},{8,4},{12,8},{5,1},{9,5},{13,9},{6,2},{10,6},{14,10},{7,3},{... | collective-permute-start | bytes 61448 | tf_op jit(solution)/shard_map/ppermute | solution.py:54
  12.9 5.8 %collective-permute-start.1 = (bf16[10240]{0:T(1024)(128)(2,1)}, bf16[10240]{0:T(1024)(128)(2,1)}, u32[]{:S(2)}, u32[]{:S(2)}) collective-permute-start(bf16[10240]{0:T(1024)(128)(2,1)} %bitcast.118), channel_id=1, source_target_pairs={{0,4},{4,8},{8,12},{1,5},{5,9},{9,13},{2,6},{6,10},{10,14},{3,7},{... | collective-permute-start | bytes 61448 | tf_op jit(solution)/shard_map/ppermute | solution.py:53
  18.7 0.5 add_multiply_fusion.4
  20.7 0.7 broadcast_compare_fusion.2
  21.4 0.6 constant_dynamic-update-slice_fusion.30
  22.0 0.8 copy_dynamic-update-slice_fusion.2
  22.9 0.7 constant_dynamic-update-slice_fusion.32
  23.6 0.7 reshape.246
  24.3 0.6 fusion.332
  24.9 0.8 select_n.200
  25.7 1.5 %collective-permute-start.6 = (f32[320]{0:T(512)S(1)}, f32[320]{0:T(512)}, u32[]{:S(2)}, u32[]{:S(2)}) collective-permute-start(f32[320]{0:T(512)S(1)} %select_n.200), channel_id=1, source_target_pairs={{0,2},{2,0},{1,3},{3,1},{4,6},{6,4},{5,7},{7,5},{8,10},{10,8},{9,1... | collective-permute-start | bytes 3848 | tf_op jit(solution)/shard_map/ppermute | solution.py:47
  27.2 0.5 add_multiply_fusion.2
  27.7 1.4 %copy.23 = pred[32,8,128]{2,0,1:T(8,128)(4,1)} copy(pred[32,8,128]{2,1,0:T(8,128)(4,1)} %get-tuple-element.132) | data formatting | bytes 65536 | tf_op jit(solution)/shard_map/jvp()/eq | solution.py:127
  29.4 1.2 %broadcast_select_fusion.8 = (f32[320]{0:T(512)}, f32[320]{0:T(512)S(1)}) fusion(f32[320]{0:T(512)} %collective-permute-done.6, pred[]{:T(512)S(6)} %eq.51, pred[]{:T(512)S(6)} %eq.52), kind=kLoop, calls=%fused_computation.652 | loop fusion | flops 640 | bytes 3842 | tf_op jit(solution)/shard_map/jit(_where)/select_n | solution.py:48
  30.6 1.4 %reshape.289 = f32[10,1,32]{2,1,0:T(1,128)} reshape(f32[320]{0:T(512)} %get-tuple-element.143) | data formatting | bytes 2560 | tf_op jit(solution)/shard_map/reshape | solution.py:60
  32.0 0.7 reshape.290
  32.6 0.7 pad_maximum_fusion.4
  33.4 0.8 fusion.315
  34.1 0.8 select_n.205
  35.0 1.4 %copy.24 = pred[32,8,128]{2,0,1:T(8,128)(4,1)} copy(pred[32,8,128]{2,1,0:T(8,128)(4,1)} %get-tuple-element.134) | data formatting | bytes 65536 | tf_op jit(solution)/shard_map/jvp()/eq | solution.py:125
  36.4 1.4 %copy.37 = pred[32,8,128]{2,0,1:T(8,128)(4,1)} copy(pred[32,8,128]{2,1,0:T(8,128)(4,1)} %get-tuple-element.133) | data formatting | bytes 65536 | tf_op jit(solution)/shard_map/jvp()/eq | solution.py:127
  38.3 1.4 %reshape.291 = f32[10,4,1]{2,1,0:T(4,128)} reshape(f32[40]{0:T(128)} %get-tuple-element.147) | data formatting | bytes 320 | tf_op jit(solution)/shard_map/reshape | solution.py:60
  39.7 0.7 reshape.292
  40.4 0.9 pad_maximum_fusion.5
  41.3 0.9 fusion.313
  42.2 0.8 copy.28
  42.9 0.8 copy.29
  43.7 0.7 constant_dynamic-update-slice_fusion.11
  44.4 0.7 constant_dynamic-update-slice_fusion.10
  45.1 0.7 constant_dynamic-update-slice_fusion.9
  45.8 0.7 constant_dynamic-update-slice_fusion.8
  46.5 0.7 copy_dynamic-update-slice_fusion.1
  47.3 0.9 slice_select_fusion.1
  48.2 1.6 %collective-permute-start.2 = (bf16[40960]{0:T(1024)(128)(2,1)S(1)}, bf16[40960]{0:T(1024)(128)(2,1)S(1)}, u32[]{:S(2)}, u32[]{:S(2)}) collective-permute-start(bf16[40960]{0:T(1024)(128)(2,1)S(1)} %bitcast.758), channel_id=1, source_target_pairs={{0,2},{2,0},{1,3},{3,1},{4,6},{6,4},{5,7},{7,5},{8,10},{10,8},{9,1... | collective-permute-start | bytes 245768 | tf_op jit(solution)/shard_map/ppermute | solution.py:47
  49.8 1.4 %fusion.318 = f32[8,10,128]{2,0,1:T(8,128)} fusion(f32[10,4,128]{2,0,1:T(8,128)S(1)} %fusion.313, f32[4]{0:T(128)} %add_multiply_fusion.3), kind=kOutput, calls=%fused_computation.614 | convolution fusion | flops 491904 | bytes 61456 | tf_op jit(solution)/shard_map/ijz,yj->iyz/dot_general | solution.py:180
  51.1 2.0 %collective-permute-done.2 = bf16[40960]{0:T(1024)(128)(2,1)S(1)} collective-permute-done((bf16[40960]{0:T(1024)(128)(2,1)S(1)}, bf16[40960]{0:T(1024)(128)(2,1)S(1)}, u32[]{:S(2)}, u32[]{:S(2)}) %collective-permute-start.2) | collective-permute-done | bytes 81952 | tf_op jit(solution)/shard_map/ppermute | solution.py:47
  53.2 1.2 %pad_maximum_fusion.1 = bf16[10,32,10,128]{3,1,2,0:T(8,128)(2,1)S(1)} fusion(bf16[10,32,1,128]{3,1,2,0:T(8,128)(2,1)S(1)} %bitcast.757, bf16[10,32,8,128]{3,1,2,0:T(8,128)(2,1)} %copy_dynamic-update-slice_fusion.1, bf16[10,32,1,128]{3,1,2,0:T(8,128)(2,1)S(1)} %bitcast.756), kind=kLoop, calls=%fused_computation.38 | loop fusion | flops 819200 | bytes 1638400 | tf_op jit(solution)/shard_map/concatenate | solution.py:81
  54.3 0.8 slice_bitcast_fusion.31
  55.2 1.1 %slice_select_fusion = bf16[10,32,8,1]{3,1,2,0:T(8,128)(2,1)} fusion(bf16[10,32,8,128]{3,1,2,0:T(8,128)(2,1)S(1)} %constant_dynamic-update-slice_fusion.4, pred[]{:T(512)S(6)} %eq.54), kind=kLoop, calls=%fused_computation.39 | loop fusion | flops 2560 | bytes 15361 | tf_op jit(solution)/shard_map/jit(_where)/select_n | solution.py:47
  56.3 3.0 %copy.33 = bf16[10,32,8,1]{2,1,0,3:T(8,128)(2,1)S(1)} copy(bf16[10,32,8,1]{3,1,2,0:T(8,128)(2,1)} %slice_select_fusion) | data formatting | bytes 10240 | tf_op jit(solution)/shard_map/jit(_where)/select_n | solution.py:47
  59.5 1.5 %constant_dynamic-update-slice_fusion.27 = bf16[19,32,8,128]{3,1,2,0:T(8,128)(2,1)} fusion(bf16[19,32,8,128]{3,1,2,0:T(8,128)(2,1)} %get-tuple-element.110, bf16[32,10,128]{2,0,1:T(8,128)(2,1)} %get-tuple-element.107), kind=kLoop, calls=%fused_computation.549 | loop fusion | bytes 131072
  61.0 0.6 constant_dynamic-update-slice_fusion.26
  61.9 3.0 %copy.35 = bf16[10,32,8,1]{3,1,2,0:T(8,128)(2,1)} copy(bf16[10,32,8,1]{2,1,0,3:T(8,128)(2,1)S(1)} %reshape.242) | data formatting | bytes 10240 | tf_op jit(solution)/shard_map/reshape | solution.py:60
  64.9 3.0 %copy.34 = bf16[10,32,8,1]{3,1,2,0:T(8,128)(2,1)} copy(bf16[10,32,8,1]{2,1,0,3:T(8,128)(2,1)S(1)} %reshape.241) | data formatting | bytes 10240 | tf_op jit(solution)/shard_map/reshape | solution.py:60
  67.9 2.1 %pad_maximum_fusion = bf16[10,32,8,130]{3,1,2,0:T(8,128)(2,1)S(1)} fusion(bf16[10,32,8,1]{3,1,2,0:T(8,128)(2,1)} %copy.35, bf16[10,32,8,128]{3,1,2,0:T(8,128)(2,1)S(1)} %constant_dynamic-update-slice_fusion.4, bf16[10,32,8,1]{3,1,2,0:T(8,128)(2,1)} %copy.34), kind=kLoop, calls=%fused_computation.34 | loop fusion | flops 1996800 | bytes 1331200 | tf_op jit(solution)/shard_map/concatenate | solution.py:81
  71.1 1.1 %fusion.1 = (f32[19,32,8,128]{3,1,2,0:T(8,128)S(1)}, f32[19,32,8,128]{3,1,2,0:T(8,128)S(1)}, f32[19,32,8,128]{3,1,2,0:T(8,128)S(1)}) fusion(bf16[19,32,8,128]{3,1,2,0:T(8,128)(2,1)S(1)} %constant_dynamic-update-slice_fusion.12, pred[32,8,128]{2,0,1:T(8,128)(4,1)S(1)} %copy-done.7, pred[32,8,128]{2,0,1:T(8,128)(4,1)S(1)} %copy-done.6, ...), kind=kLoop, calls=%fused_computation.3 | loop fusion | flops 5603328 | bytes 8814592 | tf_op jit(solution)/shard_map/transpose(jvp(jit(_where)))/select_n | solution.py:127
  73.6 0.7 fusion.60
  74.3 0.7 bitcast_add_fusion.16
  75.0 1.2 %fusion.377 = (f32[1,32,8,128]{3,1,2,0:T(8,128)S(1)}, f32[1,32,8,128]{3,1,2,0:T(8,128)S(1)}, f32[1,32,8,128]{3,1,2,0:T(8,128)S(1)}, f32[1,32,8,128]{3,1,2,0:T(8,...) fusion(f32[19,32,8,128]{3,1,2,0:T(8,128)S(1)} %get-tuple-element.82), kind=kLoop, calls=%fused_computation.694 | loop fusion | bytes 4718592 | tf_op jit(solution)/shard_map/transpose(jvp())/unstack | solution.py:117
  76.2 3.0 %negate_add_fusion = (f32[32,8,128]{2,0,1:T(8,128)S(1)}, f32[32,8,128]{2,0,1:T(8,128)S(1)}, f32[32,8,128]{2,0,1:T(8,128)S(1)}, f32[32,8,128]{2,0,1:T(8,128)S(1)}...) fusion(f32[32,8,128]{2,0,1:T(8,128)S(1)} %get-tuple-element.19, ...), kind=kLoop, calls=%fused_computation.453 | loop fusion | flops 17006592 | bytes 12320768 | tf_op jit(solution)/shard_map/transpose(jvp())/add_any | solution.py:110
  80.2 1.3 %collective-permute-start.9 = (f32[136]{0:T(256)S(1)}, f32[136]{0:T(256)S(1)}, u32[]{:S(2)}, u32[]{:S(2)}) collective-permute-start(f32[136]{0:T(256)S(1)} %reshape.253), channel_id=1, source_target_pairs={{4,0},{8,4},{12,8},{5,1},{9,5},{13,9},{6,2},{10,6},{14,10},{7,3},{... | collective-permute-start | bytes 1640 | tf_op jit(solution)/shard_map/ppermute | solution.py:54
  81.5 4.5 %collective-permute-start.8 = (f32[136]{0:T(256)S(1)}, f32[136]{0:T(256)S(1)}, u32[]{:S(2)}, u32[]{:S(2)}) collective-permute-start(f32[136]{0:T(256)S(1)} %reshape.251), channel_id=1, source_target_pairs={{0,4},{4,8},{8,12},{1,5},{5,9},{9,13},{2,6},{6,10},{10,14},{3,7},{... | collective-permute-start | bytes 1640 | tf_op jit(solution)/shard_map/ppermute | solution.py:53
  86.1 0.9 multiply_bitcast_fusion.2
  87.5 1.5 %collective-permute-start.10 = (f32[272]{0:T(512)S(1)}, f32[272]{0:T(512)S(1)}, u32[]{:S(2)}, u32[]{:S(2)}) collective-permute-start(f32[272]{0:T(512)S(1)} %select_n.213), channel_id=1, source_target_pairs={{0,2},{2,0},{1,3},{3,1},{4,6},{6,4},{5,7},{7,5},{8,10},{10,8},{9,1... | collective-permute-start | bytes 3272 | tf_op jit(solution)/shard_map/ppermute | solution.py:47
  89.0 5.1 %add_convert_fusion = bf16[19,32,8,128]{3,1,2,0:T(8,128)(2,1)S(1)} fusion(f32[1,32,8,128]{3,1,2,0:T(8,128)} %get-tuple-element.128, f32[1,32,8,128]{3,1,2,0:T(8,128)} %get-tuple-element.129, bf16[19,32,8,128]{3,1,2,0:T(8,128)(2,1)S(1)} %copy-done.3, f32[1,32,8,128]{3,1,2,0:T(8,128)} %get-tuple-element.130, f32[1,32,8,128]{3,1,2,0:T(8,128)} %get-tuple-element.131, ...), kind=kLoop, calls=%fused_computation.33 | loop fusion | flops 36732928 | bytes 5832723 | tf_op jit(solution)/shard_map/convert_element_type | solution.py:193
  94.7 1.6 %copy.45 = bf16[19,32,8,128]{3,2,1,0:T(8,128)(2,1)} copy(bf16[19,32,8,128]{3,1,2,0:T(8,128)(2,1)S(1)} %add_convert_fusion) | data formatting | bytes 2490368
  96.8 0.6 copy.46
  (115 shorter events, 7.9 us)
Async XLA Ops:
  0.6 19.1 %copy-start.4 = (bf16[19,32,8,128]{3,2,1,0:T(8,128)(2,1)S(1)}, bf16[19,32,8,128]{3,2,1,0:T(8,128)(2,1)}, u32[]{:S(2)}) copy-start(bf16[19,32,8,128]{3,2,1,0:T(8,128)(2,1)} %param.4) | copy-start | bytes 3735556
  1.5 21.3 %collective-permute-start.4 = (f32[64]{0:T(128)S(1)}, f32[64]{0:T(128)S(1)}, u32[]{:S(2)}, u32[]{:S(2)}) collective-permute-start(f32[64]{0:T(128)S(1)} %reshape.243), channel_id=1, source_target_pairs={{0,4},{4,8},{8,12},{1,5},{5,9},{9,13},{2,6},{6,10},{10,14},{3,7},{... | collective-permute-start | bytes 776 | tf_op jit(solution)/shard_map/ppermute | solution.py:53
  7.1 12.8 %copy-start.5 = (bf16[19,32,8,128]{3,2,1,0:T(8,128)(2,1)S(1)}, bf16[19,32,8,128]{3,2,1,0:T(8,128)(2,1)}, u32[]{:S(2)}) copy-start(bf16[19,32,8,128]{3,2,1,0:T(8,128)(2,1)} %param.4) | copy-start | bytes 3735556
  7.1 16.5 %collective-permute-start.5 = (f32[64]{0:T(128)}, f32[64]{0:T(128)}, u32[]{:S(2)}, u32[]{:S(2)}) collective-permute-start(f32[64]{0:T(128)} %reshape.245), channel_id=1, source_target_pairs={{4,0},{8,4},{12,8},{5,1},{9,5},{13,9},{6,2},{10,6},{14,10},{7,3},{... | collective-permute-start | bytes 776 | tf_op jit(solution)/shard_map/ppermute | solution.py:54
  11.7 30.5 %collective-permute-start = (bf16[10240]{0:T(1024)(128)(2,1)}, bf16[10240]{0:T(1024)(128)(2,1)}, u32[]{:S(2)}, u32[]{:S(2)}) collective-permute-start(bf16[10240]{0:T(1024)(128)(2,1)} %bitcast.117), channel_id=1, source_target_pairs={{4,0},{8,4},{12,8},{5,1},{9,5},{13,9},{6,2},{10,6},{14,10},{7,3},{... | collective-permute-start | bytes 61448 | tf_op jit(solution)/shard_map/ppermute | solution.py:54
  12.9 30.0 %collective-permute-start.1 = (bf16[10240]{0:T(1024)(128)(2,1)}, bf16[10240]{0:T(1024)(128)(2,1)}, u32[]{:S(2)}, u32[]{:S(2)}) collective-permute-start(bf16[10240]{0:T(1024)(128)(2,1)} %bitcast.118), channel_id=1, source_target_pairs={{0,4},{4,8},{8,12},{1,5},{5,9},{9,13},{2,6},{6,10},{10,14},{3,7},{... | collective-permute-start | bytes 61448 | tf_op jit(solution)/shard_map/ppermute | solution.py:53
  19.8 0.9 copy-start.12
  19.8 1.6 %slice-start = ((bf16[19,32,8,128]{3,2,1,0:T(8,128)(2,1)}), bf16[1,32,8,128]{3,2,1,0:T(8,128)(2,1)S(1)}, s32[]{:S(2)}) async-start(bf16[19,32,8,128]{3,2,1,0:T(8,128)(2,1)} %param.5), calls=%async_computation | async-start | bytes 131072 | tf_op jit(solution)/shard_map/slice | solution.py:173
  22.8 23.8 %slice-start.1 = ((bf16[19,32,8,128]{3,2,1,0:T(8,128)(2,1)}), bf16[4,32,8,128]{3,2,1,0:T(8,128)(2,1)S(1)}, s32[]{:S(2)}) async-start(bf16[19,32,8,128]{3,2,1,0:T(8,128)(2,1)} %param.5), calls=%async_computation.1 | async-start | bytes 524288 | tf_op jit(solution)/shard_map/slice | solution.py:173
  25.7 3.7 %collective-permute-start.6 = (f32[320]{0:T(512)S(1)}, f32[320]{0:T(512)}, u32[]{:S(2)}, u32[]{:S(2)}) collective-permute-start(f32[320]{0:T(512)S(1)} %select_n.200), channel_id=1, source_target_pairs={{0,2},{2,0},{1,3},{3,1},{4,6},{6,4},{5,7},{7,5},{8,10},{10,8},{9,1... | collective-permute-start | bytes 3848 | tf_op jit(solution)/shard_map/ppermute | solution.py:47
  34.9 2.8 %collective-permute-start.7 = (f32[40]{0:T(128)S(1)}, f32[40]{0:T(128)S(1)}, u32[]{:S(2)}, u32[]{:S(2)}) collective-permute-start(f32[40]{0:T(128)S(1)} %select_n.205), channel_id=1, source_target_pairs={{0,1},{1,0},{2,3},{3,2},{4,5},{5,4},{6,7},{7,6},{8,9},{9,8},{10,11... | collective-permute-start | bytes 488 | tf_op jit(solution)/shard_map/ppermute | solution.py:47
  46.5 8.6 %copy-start = (bf16[10,32,8,128]{3,1,2,0:T(8,128)(2,1)S(1)}, bf16[10,32,8,128]{3,1,2,0:T(8,128)(2,1)}, u32[]{:S(2)}) copy-start(bf16[10,32,8,128]{3,1,2,0:T(8,128)(2,1)} %get-tuple-element.108) | copy-start | bytes 1966084
  48.2 4.9 %collective-permute-start.2 = (bf16[40960]{0:T(1024)(128)(2,1)S(1)}, bf16[40960]{0:T(1024)(128)(2,1)S(1)}, u32[]{:S(2)}, u32[]{:S(2)}) collective-permute-start(bf16[40960]{0:T(1024)(128)(2,1)S(1)} %bitcast.758), channel_id=1, source_target_pairs={{0,2},{2,0},{1,3},{3,1},{4,6},{6,4},{5,7},{7,5},{8,10},{10,8},{9,1... | collective-permute-start | bytes 245768 | tf_op jit(solution)/shard_map/ppermute | solution.py:47
  59.5 2.2 %collective-permute-start.3 = (bf16[2560]{0:T(1024)(128)(2,1)S(1)}, bf16[2560]{0:T(1024)(128)(2,1)S(1)}, u32[]{:S(2)}, u32[]{:S(2)}) collective-permute-start(bf16[2560]{0:T(1024)(128)(2,1)S(1)} %select_n.184), channel_id=1, source_target_pairs={{0,1},{1,0},{2,3},{3,2},{4,5},{5,4},{6,7},{7,6},{8,9},{9,8},{10,11... | collective-permute-start | bytes 15368 | tf_op jit(solution)/shard_map/ppermute | solution.py:47
  67.9 2.3 %copy-start.1 = (bf16[19,32,8,128]{3,1,2,0:T(8,128)(2,1)S(1)}, bf16[19,32,8,128]{3,1,2,0:T(8,128)(2,1)}, u32[]{:S(2)}) copy-start(bf16[19,32,8,128]{3,1,2,0:T(8,128)(2,1)} %constant_dynamic-update-slice_fusion.26) | copy-start | bytes 3735556
  67.9 2.5 %copy-start.10 = (bf16[32,10,128]{2,0,1:T(8,128)(2,1)S(1)}, bf16[32,10,128]{2,0,1:T(8,128)(2,1)}, u32[]{:S(2)}) copy-start(bf16[32,10,128]{2,0,1:T(8,128)(2,1)} %get-tuple-element.101) | copy-start | bytes 245764
  67.9 2.5 %copy-start.9 = (bf16[32,10,128]{2,0,1:T(8,128)(2,1)S(1)}, bf16[32,10,128]{2,0,1:T(8,128)(2,1)}, u32[]{:S(2)}) copy-start(bf16[32,10,128]{2,0,1:T(8,128)(2,1)} %get-tuple-element.100) | copy-start | bytes 245764
  67.9 2.5 %copy-start.8 = (bf16[32,10,128]{2,0,1:T(8,128)(2,1)S(1)}, bf16[32,10,128]{2,0,1:T(8,128)(2,1)}, u32[]{:S(2)}) copy-start(bf16[32,10,128]{2,0,1:T(8,128)(2,1)} %get-tuple-element.99) | copy-start | bytes 245764
  70.1 0.9 copy-start.6
  70.1 0.9 copy-start.7
  70.1 0.9 copy-start.11
  71.1 1.1 %copy-start.2 = (bf16[19,32,8,128]{3,1,2,0:T(8,128)(2,1)}, bf16[19,32,8,128]{3,1,2,0:T(8,128)(2,1)S(1)}, u32[]{:S(2)}) copy-start(bf16[19,32,8,128]{3,1,2,0:T(8,128)(2,1)S(1)} %constant_dynamic-update-slice_fusion.12) | copy-start | bytes 3735556
  72.2 0.8 copy-start.13
  72.2 0.8 copy-start.15
  76.2 3.3 %copy-start.14 = (f32[4]{0:T(128)S(1)}, f32[4]{0:T(128)}, u32[]{:S(2)}) copy-start(f32[4]{0:T(128)} %add_multiply_fusion.3) | copy-start | bytes 52
  76.2 3.6 %copy-start.17 = (f32[34]{0:T(128)S(1)}, f32[34]{0:T(128)}, u32[]{:S(2)}) copy-start(f32[34]{0:T(128)} %add_multiply_fusion.2) | copy-start | bytes 412
  79.2 9.8 %copy-start.3 = (bf16[19,32,8,128]{3,1,2,0:T(8,128)(2,1)S(1)}, bf16[19,32,8,128]{3,1,2,0:T(8,128)(2,1)}, u32[]{:S(2)}) copy-start(bf16[19,32,8,128]{3,1,2,0:T(8,128)(2,1)} %copy-done.2) | copy-start | bytes 3735556
  79.2 9.8 %copy-start.16 = (pred[19]{0:T(512)(128)(4,1)S(1)}, pred[19]{0:T(512)(128)(4,1)}, u32[]{:S(2)}) copy-start(pred[19]{0:T(512)(128)(4,1)} %constant.41.clone.1) | copy-start | bytes 61
  80.2 6.8 %collective-permute-start.9 = (f32[136]{0:T(256)S(1)}, f32[136]{0:T(256)S(1)}, u32[]{:S(2)}, u32[]{:S(2)}) collective-permute-start(f32[136]{0:T(256)S(1)} %reshape.253), channel_id=1, source_target_pairs={{4,0},{8,4},{12,8},{5,1},{9,5},{13,9},{6,2},{10,6},{14,10},{7,3},{... | collective-permute-start | bytes 1640 | tf_op jit(solution)/shard_map/ppermute | solution.py:54
  81.5 5.8 %collective-permute-start.8 = (f32[136]{0:T(256)S(1)}, f32[136]{0:T(256)S(1)}, u32[]{:S(2)}, u32[]{:S(2)}) collective-permute-start(f32[136]{0:T(256)S(1)} %reshape.251), channel_id=1, source_target_pairs={{0,4},{4,8},{8,12},{1,5},{5,9},{9,13},{2,6},{6,10},{10,14},{3,7},{... | collective-permute-start | bytes 1640 | tf_op jit(solution)/shard_map/ppermute | solution.py:53
  87.5 6.7 %collective-permute-start.10 = (f32[272]{0:T(512)S(1)}, f32[272]{0:T(512)S(1)}, u32[]{:S(2)}, u32[]{:S(2)}) collective-permute-start(f32[272]{0:T(512)S(1)} %select_n.213), channel_id=1, source_target_pairs={{0,2},{2,0},{1,3},{3,1},{4,6},{6,4},{5,7},{7,5},{8,10},{10,8},{9,1... | collective-permute-start | bytes 3272 | tf_op jit(solution)/shard_map/ppermute | solution.py:47
  94.7 1.6 %collective-permute-start.11 = (f32[16]{0:T(128)S(1)}, f32[16]{0:T(128)S(1)}, u32[]{:S(2)}, u32[]{:S(2)}) collective-permute-start(f32[16]{0:T(128)S(1)} %select_n.220), channel_id=1, source_target_pairs={{0,1},{1,0},{2,3},{3,2},{4,5},{5,4},{6,7},{7,6},{8,9},{9,8},{10,11... | collective-permute-start | bytes 200 | tf_op jit(solution)/shard_map/ppermute | solution.py:47

commit v2 on v1

--- a/solution.py
+++ b/solution.py
@@ -33,6 +33,8 @@
 
 def exchange(low_parts, high_parts, axis):
     count = lax.axis_size(axis)
+    if len(high_parts) == 1:
+        return exchange_one(low_parts[0], high_parts[0], axis, count)
     shapes = [part.shape for part in high_parts]
     types = [part.dtype for part in high_parts]
     sizes = [part.size for part in high_parts]
@@ -64,6 +66,19 @@
     return split(from_prev), split(from_next)
 
 
+def exchange_one(low, high, axis, count):
+    if count == 1:
+        return [jnp.zeros_like(high)], [jnp.zeros_like(low)]
+    if count == 2:
+        index = lax.axis_index(axis)
+        received = lax.ppermute(jnp.where(index == 0, high, low), axis, [(0, 1), (1, 0)])
+        zero = jnp.zeros_like(received)
+        return [jnp.where(index == 1, received, zero)], [jnp.where(index == 0, received, zero)]
+    forward = [(i, i + 1) for i in range(count - 1)]
+    backward = [(target, source) for source, target in forward]
+    return [lax.ppermute(high, axis, forward)], [lax.ppermute(low, axis, backward)]
+
+
 def faces(block, dim):
     length = block.shape[dim]
     return (
@@ -170,12 +185,26 @@
     basis_x = basis_matrix(cells_x, coarse_x + 2, 0, -1)
     basis_y = basis_matrix(cells_y, coarse_y + 2, 0, -1)
     basis_z = basis_matrix(cells_z, coarse_z + 2, 0, -1)
-    lane_list = [adjoint_pops[component] for component in range(19)]
     window = coefficients
+    extended = adjoint_pops
     for dimension, axis in ((0, "gx"), (1, "gy"), (2, "gz")):
-        stacked = jnp.stack([lane_list[component] for component in moving(dimension)])
-        window, extended = padded_pair(window, dimension, stacked, dimension + 1, axis)
-        lane_list = pull_along(lane_list, dimension, extended)
+        coef_low, coef_high = faces(window, dimension)
+        coef_prev, coef_next = exchange([coef_low], [coef_high], axis)
+        window = jnp.concatenate([coef_prev[0], window, coef_next[0]], axis=dimension)
+        pops_low, pops_high = faces(extended, dimension + 1)
+        pops_prev, pops_next = exchange([pops_low], [pops_high], axis)
+        extended = jnp.concatenate([pops_prev[0], extended, pops_next[0]], axis=dimension + 1)
+    lane_list = []
+    for component in range(19):
+        step_x, step_y, step_z = VELOCITY[component]
+        lane_list.append(
+            extended[
+                component,
+                1 + step_x : 1 + step_x + cells_x,
+                1 + step_y : 1 + step_y + cells_y,
+                1 + step_z : 1 + step_z + cells_z,
+            ]
+        )
     partway = jnp.einsum("ijk,zk->ijz", window, basis_z, precision=highest)
     partway = jnp.einsum("ijz,yj->iyz", partway, basis_y, precision=highest)
     level_set = jnp.einsum("iyz,xi->xyz", partway, basis_x, precision=highest)

time: 99.3 us -> 116 us (1.17); the launches traced: 97.4 us -> 115 us
  other arithmetic: 27.8 us -> 38.3 us
  waiting for transfers between devices: 2.55 us -> 9.22 us
  local copies, waits for them, and re-layouts: 38.4 us -> 41.6 us
  starting transfers between devices: 23.9 us -> 22.6 us
    concatenate x1 -> x4, local copies, waits for them, and re-layouts: 0.01 us -> 19.1 us  [per_device(): jnp.concatenate([pops_prev[0], extended, pops_next[0]], axis=dimension + 1)]
    reshape x24 -> x0, local copies, waits for them, and re-layouts: 14.3 us -> none  [the longest x20 13.4 us: split(): pieces.append(flat[offset:offset + size].reshape(shape).astype(dtype))]
    unnamed x4 -> x15, other arithmetic: 2.85 us -> 12 us
    ppermute x12, waiting for transfers between devices: 2.55 us -> 9.22 us  [the longest x6 5.46 us: exchange_one(): lax.ppermute(jnp.where(index == 0, high, low), axis, [(0, 1), (1, 0)])]
    select_n x7 -> x5, local copies, waits for them, and re-layouts: 5.02 us -> 8.84 us  [the longest x2 3.63 us: exchange_one(): jnp.where(index == 0, received, zero)]
    slice x7 -> x0, local copies, waits for them, and re-layouts: 2.95 us -> none  [the longest x6 2.15 us: per_device(): lane_list = [adjoint_pops[component] for component in range(19)]]
    convert_element_type x1, other arithmetic: 0.35 us -> 3.18 us  [per_device(): forward = forward_pops.astype(jnp.float32)]
    convert_element_type x1, other arithmetic: 5.13 us -> 2.97 us  [per_device(): prior_adjoint = prior.astype(jnp.bfloat16)]
  transfers between devices with their start and end apart: 12 -> 12, of which waited for: 3 -> 3; matrix products, arithmetic and copies ran while one was open for 38% -> 26% of each run, Pallas kernels for 0% -> 0%
where the time goes in v2:
time: 116 us; the launch traced here: 115 us
  local copies, waits for them, and re-layouts  41.6 us (36%)
  other arithmetic  38.3 us (33%)
  starting transfers between devices  22.6 us (19%)
  waiting for transfers between devices  9.22 us (8%)
  matrix products  2.48 us (2%)
    concatenate x4, local copies, waits for them, and re-layouts, per_device(): jnp.concatenate([pops_prev[0], extended, pops_next[0]], axis=dimension + 1)  19.1 us
    ppermute x3, starting transfers between devices, exchange_one(): lax.ppermute(high, axis, forward)  14 us
    unnamed x15, other arithmetic  12 us
    unnamed x46, local copies, waits for them, and re-layouts  9.29 us
    ppermute x6, waiting for transfers between devices, exchange_one(): lax.ppermute(jnp.where(index == 0, high, low), axis, [(0, 1), (1, 0)])  5.46 us
    ppermute x6, starting transfers between devices, exchange_one(): lax.ppermute(jnp.where(index == 0, high, low), axis, [(0, 1), (1, 0)])  4.7 us
    concatenate x2, other arithmetic, per_device(): jnp.concatenate([pops_prev[0], extended, pops_next[0]], axis=dimension + 1)  4.56 us
    ppermute x3, starting transfers between devices, exchange_one(): lax.ppermute(low, axis, backward)  3.88 us
  transfers between devices with their start and end apart: 12, of which 3 were waited for; matrix products, arithmetic and copies ran while one was open for 26% of the time, Pallas kernels for 0%

profile of v2, /device:TPU:0, one launch (start us, length us, event | category | flops | bytes accessed | tf_op | source)
XLA Modules:
  0.0 115.3 jit_solution(7524090857701342635)
XLA Ops:
  0.6 0.9 fusion.389
  1.5 4.9 %collective-permute-start.1 = (bf16[19,1,8,128]{3,2,1,0:T(8,128)(2,1)S(1)}, bf16[19,1,8,128]{3,2,1,0:T(8,128)(2,1)S(1)}, u32[]{:S(2)}, u32[]{:S(2)}) collective-permute-start(bf16[19,1,8,128]{3,2,1,0:T(8,128)(2,1)S(1)} %get-tuple-element.90), channel_id=1, source_target_pairs={{0,4},{4,8},{8,12},{1,5},{5,9},{9,13},{2,6},{6,10},{10,14},{3,7},{... | collective-permute-start | bytes 116744 | tf_op jit(solution)/shard_map/ppermute | solution.py:79
  6.5 1.3 %collective-permute-start = (bf16[19,1,8,128]{3,2,1,0:T(8,128)(2,1)S(1)}, bf16[19,1,8,128]{3,2,1,0:T(8,128)(2,1)S(1)}, u32[]{:S(2)}, u32[]{:S(2)}) collective-permute-start(bf16[19,1,8,128]{3,2,1,0:T(8,128)(2,1)S(1)} %get-tuple-element.91), channel_id=1, source_target_pairs={{4,0},{8,4},{12,8},{5,1},{9,5},{13,9},{6,2},{10,6},{14,10},{7,3},{... | collective-permute-start | bytes 116744 | tf_op jit(solution)/shard_map/ppermute | solution.py:79
  7.8 0.7 fusion.391
  8.5 4.5 %collective-permute-start.4 = (f32[1,2,32]{2,0,1:T(1,128)S(1)}, f32[1,2,32]{2,0,1:T(1,128)S(1)}, u32[]{:S(2)}, u32[]{:S(2)}) collective-permute-start(f32[1,2,32]{2,0,1:T(1,128)S(1)} %bitcast.620), channel_id=1, source_target_pairs={{0,4},{4,8},{8,12},{1,5},{5,9},{9,13},{2,6},{6,10},{10,14},{3,7},{... | collective-permute-start | bytes 776 | tf_op jit(solution)/shard_map/ppermute | solution.py:79
  13.0 1.3 %collective-permute-start.5 = (f32[1,2,32]{2,0,1:T(1,128)S(1)}, f32[1,2,32]{2,0,1:T(1,128)S(1)}, u32[]{:S(2)}, u32[]{:S(2)}) collective-permute-start(f32[1,2,32]{2,0,1:T(1,128)S(1)} %bitcast.619), channel_id=1, source_target_pairs={{4,0},{8,4},{12,8},{5,1},{9,5},{13,9},{6,2},{10,6},{14,10},{7,3},{... | collective-permute-start | bytes 776 | tf_op jit(solution)/shard_map/ppermute | solution.py:79
  14.3 0.7 copy.143
  15.1 1.0 broadcast_compare_fusion.2
  16.0 3.2 %copy_convert_fusion = f32[19,32,8,128]{3,1,2,0:T(8,128)} fusion(bf16[19,32,8,128]{3,2,1,0:T(8,128)(2,1)} %param.4), kind=kLoop, calls=%fused_computation.35 | loop fusion | flops 622592 | bytes 3735552 | tf_op jit(solution)/shard_map/convert_element_type | solution.py:215
  19.3 1.6 %collective-permute-start.6 = (f32[10,1,32]{2,0,1:T(8,128)S(1)}, f32[10,1,32]{2,0,1:T(8,128)S(1)}, u32[]{:S(2)}, u32[]{:S(2)}) collective-permute-start(f32[10,1,32]{2,0,1:T(8,128)S(1)} %slice_select_fusion.4), channel_id=1, source_target_pairs={{0,2},{2,0},{1,3},{3,1},{4,6},{6,4},{5,7},{7,5},{8,10},{10,8},{9,1... | collective-permute-start | bytes 3848 | tf_op jit(solution)/shard_map/ppermute | solution.py:74
  21.4 1.6 %collective-permute-done.6 = f32[10,1,32]{2,0,1:T(8,128)S(1)} collective-permute-done((f32[10,1,32]{2,0,1:T(8,128)S(1)}, f32[10,1,32]{2,0,1:T(8,128)S(1)}, u32[]{:S(2)}, u32[]{:S(2)}) %collective-permute-start.6) | collective-permute-done | bytes 1312 | tf_op jit(solution)/shard_map/ppermute | solution.py:74
  23.1 0.6 copy.121
  23.7 0.6 copy.140
  24.6 0.9 convolution_bitcast_fusion
  25.5 0.6 constant_dynamic-update-slice_fusion.2
  26.1 1.3 %constant_dynamic-update-slice_fusion.1 = bf16[19,34,8,128]{3,2,1,0:T(8,128)(2,1)} fusion(bf16[19,34,8,128]{3,2,1,0:T(8,128)(2,1)} %constant_dynamic-update-slice_fusion.2, bf16[19,32,8,128]{3,2,1,0:T(8,128)(2,1)S(1)} %copy-done.4), kind=kLoop, calls=%fused_computation.546 | loop fusion | bytes 2490368
  27.5 0.6 constant_dynamic-update-slice_fusion
  28.1 5.9 %copy.125 = bf16[19,34,8,128]{1,0,3,2:T(8,128)(2,1)} copy(bf16[19,34,8,128]{3,2,1,0:T(8,128)(2,1)} %constant_dynamic-update-slice_fusion) | data formatting | bytes 2646016 | tf_op jit(solution)/shard_map/concatenate | solution.py:196
  34.0 1.6 %copy.129 = bf16[19,34,8,128]{3,1,2,0:T(8,128)(2,1)S(1)} copy(bf16[19,34,8,128]{3,2,1,0:T(8,128)(2,1)} %constant_dynamic-update-slice_fusion) | data formatting | bytes 2646016 | tf_op jit(solution)/shard_map/concatenate | solution.py:196
  35.7 2.3 %slice_select_fusion = bf16[19,34,1,128]{1,0,3,2:T(8,128)(2,1)} fusion(bf16[19,34,8,128]{1,0,3,2:T(8,128)(2,1)} %copy.125, pred[]{:T(512)S(6)} %eq.51), kind=kLoop, calls=%fused_computation.40 | loop fusion | flops 82688 | bytes 496129 | tf_op jit(solution)/shard_map/jit(_where)/select_n | solution.py:74
  38.0 1.6 %copy.127 = bf16[19,34,1,128]{3,1,2,0:T(8,128)(2,1)S(1)} copy(bf16[19,34,1,128]{1,0,3,2:T(8,128)(2,1)} %slice_select_fusion) | data formatting | bytes 330752 | tf_op jit(solution)/shard_map/jit(_where)/select_n | solution.py:74
  39.6 1.5 %collective-permute-start.2 = (bf16[19,34,1,128]{3,1,2,0:T(8,128)(2,1)S(1)}, bf16[19,34,1,128]{3,1,2,0:T(8,128)(2,1)S(1)}, u32[]{:S(2)}, u32[]{:S(2)}) collective-permute-start(bf16[19,34,1,128]{3,1,2,0:T(8,128)(2,1)S(1)} %copy.127), channel_id=1, source_target_pairs={{0,2},{2,0},{1,3},{3,1},{4,6},{6,4},{5,7},{7,5},{8,10},{10,8},{9,1... | collective-permute-start | bytes 496136 | tf_op jit(solution)/shard_map/ppermute | solution.py:74
  41.2 0.6 copy_dynamic-update-slice_fusion.2
  41.8 0.6 copy_dynamic-update-slice_fusion.1
  42.5 0.6 copy_dynamic-update-slice_fusion
  43.1 3.8 %collective-permute-done.2 = bf16[19,34,1,128]{3,1,2,0:T(8,128)(2,1)S(1)} collective-permute-done((bf16[19,34,1,128]{3,1,2,0:T(8,128)(2,1)S(1)}, bf16[19,34,1,128]{3,1,2,0:T(8,128)(2,1)S(1)}, u32[]{:S(2)}, u32[]{:S(2)}) %collective-permute-start.2) | collective-permute-done | bytes 165408 | tf_op jit(solution)/shard_map/ppermute | solution.py:74
  46.9 1.3 %copy.128 = bf16[19,34,1,128]{1,0,3,2:T(8,128)(2,1)} copy(bf16[19,34,1,128]{3,1,2,0:T(8,128)(2,1)S(1)} %collective-permute-done.2) | data formatting | bytes 330752 | tf_op jit(solution)/shard_map/ppermute | solution.py:74
  48.2 1.2 %broadcast_select_fusion = (bf16[19,34,1,128]{1,0,3,2:T(8,128)(2,1)S(1)}, bf16[19,34,1,128]{1,0,3,2:T(8,128)(2,1)S(1)}) fusion(bf16[19,34,1,128]{1,0,3,2:T(8,128)(2,1)} %copy.128, pred[]{:T(512)S(6)} %eq.52, pred[]{:T(512)S(6)} %eq.51), kind=kLoop, calls=%fused_computation.41 | loop fusion | flops 165376 | bytes 496130 | tf_op jit(solution)/shard_map/jit(_where)/select_n | solution.py:76
  50.4 4.5 %pad_maximum_fusion = bf16[19,34,10,128]{1,0,3,2:T(8,128)(2,1)S(1)} fusion(bf16[19,34,1,128]{1,0,3,2:T(8,128)(2,1)S(1)} %get-tuple-element.93, bf16[19,34,8,128]{1,0,3,2:T(8,128)(2,1)} %copy.125, bf16[19,34,1,128]{1,0,3,2:T(8,128)(2,1)S(1)} %get-tuple-element.92), kind=kLoop, calls=%fused_computation | loop fusion | flops 1653760 | bytes 3307520 | tf_op jit(solution)/shard_map/concatenate | solution.py:196
  55.0 0.7 slice_select_fusion.1
  55.7 1.1 maximum_dynamic-update-slice_fusion.11
  56.8 1.3 %copy-done.2 = bf16[19,34,10,128]{1,0,3,2:T(8,128)(2,1)} copy-done((bf16[19,34,10,128]{1,0,3,2:T(8,128)(2,1)}, bf16[19,34,10,128]{1,0,3,2:T(8,128)(2,1)S(1)}, u32[]{:S(2)}) %copy-start.2) | copy-done | bytes 1653784
  58.1 0.7 maximum_dynamic-update-slice_fusion.10
  58.7 10.9 %copy.135 = bf16[19,34,10,128]{3,1,2,0:T(8,128)(2,1)S(1)} copy(bf16[19,34,10,128]{1,0,3,2:T(8,128)(2,1)} %copy-done.2) | data formatting | bytes 3307520 | tf_op jit(solution)/shard_map/concatenate | solution.py:196
  69.6 1.5 %broadcast_select_fusion.2 = (bf16[19,34,10,1]{1,0,3,2:T(8,128)(2,1)}, bf16[19,34,10,1]{1,0,3,2:T(8,128)(2,1)}) fusion(bf16[19,34,10,1]{1,0,3,2:T(8,128)(2,1)} %collective-permute-done.3, pred[]{:T(512)S(6)} %eq.54, pred[]{:T(512)S(6)} %eq.53), kind=kLoop, calls=%fused_computation.543 | loop fusion | flops 12920 | bytes 38762 | tf_op jit(solution)/shard_map/jit(_where)/select_n | solution.py:76
  71.1 3.2 %copy.136 = bf16[19,34,10,1]{3,1,2,0:T(8,128)(2,1)} copy(bf16[19,34,10,1]{1,0,3,2:T(8,128)(2,1)} %get-tuple-element.112) | data formatting | bytes 25840 | tf_op jit(solution)/shard_map/jit(_where)/select_n | solution.py:76
  74.3 3.1 %copy.137 = bf16[19,34,10,1]{3,1,2,0:T(8,128)(2,1)} copy(bf16[19,34,10,1]{1,0,3,2:T(8,128)(2,1)} %get-tuple-element.111) | data formatting | bytes 25840 | tf_op jit(solution)/shard_map/jit(_where)/select_n | solution.py:76
  77.4 1.8 %maximum_dynamic-update-slice_fusion.9 = bf16[19,32,8,128]{3,1,2,0:T(8,128)(2,1)} fusion(bf16[19,32,8,128]{3,1,2,0:T(8,128)(2,1)} %maximum_dynamic-update-slice_fusion.10, bf16[19,34,10,1]{3,1,2,0:T(8,128)(2,1)} %copy.136, bf16[19,34,10,128]{3,1,2,0:T(8,128)(2,1)S(1)} %copy.135), kind=kLoop, calls=%fused_computation.527 | loop fusion | flops 131072 | bytes 3664896
  79.2 0.7 maximum_dynamic-update-slice_fusion.8
  80.1 0.7 maximum_dynamic-update-slice_fusion.7
  80.8 0.6 maximum_dynamic-update-slice_fusion.6
  81.4 0.7 fusion.307
  82.1 0.6 fusion.306
  82.7 0.8 maximum_dynamic-update-slice_fusion.5
  83.5 0.7 maximum_dynamic-update-slice_fusion.4
  84.2 0.7 maximum_dynamic-update-slice_fusion.3
  84.9 0.7 maximum_dynamic-update-slice_fusion.2
  85.7 0.8 maximum_dynamic-update-slice_fusion.1
  86.4 0.7 maximum_dynamic-update-slice_fusion
  87.1 0.7 fusion.305
  87.9 0.8 fusion.304
  88.6 0.6 copy-done.5
  89.2 2.6 %fusion.1 = (f32[19,32,8,128]{3,1,2,0:T(8,128)S(1)}, f32[19,32,8,128]{3,1,2,0:T(8,128)S(1)}, f32[19,32,8,128]{3,1,2,0:T(8,128)S(1)}, f32[32,8,128]{2,0,1:T(8,128)S(1)}) fusion(bf16[19,32,8,128]{3,1,2,0:T(8,128)(2,1)} %fusion.304, pred[32,8,128]{2,0,1:T(8,128)(4,1)S(1)} %copy-done.10, pred[32,8,128]{2,0,1:T(8,128)(4,1)S(1)} %copy.120, ...), kind=kLoop, calls=%fused_computation.4 | loop fusion | flops 6815744 | bytes 10190848 | tf_op jit(solution)/shard_map/transpose(jvp(jit(_where)))/select_n | solution.py:142
  92.6 0.5 bitcast_add_fusion.17
  93.3 0.7 fusion.60
  94.0 0.7 bitcast_add_fusion.16
  94.7 2.8 %negate_add_fusion = (f32[32,8,128]{2,0,1:T(8,128)S(1)}, f32[32,8,128]{2,0,1:T(8,128)S(1)}, f32[32,8,128]{2,0,1:T(8,128)S(1)}, f32[32,8,128]{2,0,1:T(8,128)S(1)}...) fusion(f32[32,8,128]{2,0,1:T(8,128)S(1)} %get-tuple-element.21, ...), kind=kLoop, calls=%fused_computation.441 | loop fusion | flops 17006592 | bytes 12320768 | tf_op jit(solution)/shard_map/transpose(jvp())/add_any | solution.py:125
  98.3 4.5 %collective-permute-start.8 = (f32[1,4,34]{2,0,1:T(1,128)S(1)}, f32[1,4,34]{2,0,1:T(1,128)S(1)}, u32[]{:S(2)}, u32[]{:S(2)}) collective-permute-start(f32[1,4,34]{2,0,1:T(1,128)S(1)} %get-tuple-element.113), channel_id=1, source_target_pairs={{0,4},{4,8},{8,12},{1,5},{5,9},{9,13},{2,6},{6,10},{10,14},{3,7},{... | collective-permute-start | bytes 1640 | tf_op jit(solution)/shard_map/ppermute | solution.py:79
  102.9 1.3 %collective-permute-start.9 = (f32[1,4,34]{2,0,1:T(1,128)S(1)}, f32[1,4,34]{2,0,1:T(1,128)S(1)}, u32[]{:S(2)}, u32[]{:S(2)}) collective-permute-start(f32[1,4,34]{2,0,1:T(1,128)S(1)} %get-tuple-element.114), channel_id=1, source_target_pairs={{4,0},{8,4},{12,8},{5,1},{9,5},{13,9},{6,2},{10,6},{14,10},{7,3},{... | collective-permute-start | bytes 1640 | tf_op jit(solution)/shard_map/ppermute | solution.py:79
  104.6 3.7 %collective-permute-done.9 = f32[1,4,34]{2,0,1:T(1,128)S(1)} collective-permute-done((f32[1,4,34]{2,0,1:T(1,128)S(1)}, f32[1,4,34]{2,0,1:T(1,128)S(1)}, u32[]{:S(2)}, u32[]{:S(2)}) %collective-permute-start.9) | collective-permute-done | bytes 576 | tf_op jit(solution)/shard_map/ppermute | solution.py:79
  108.4 1.6 %collective-permute-start.10 = (f32[8,1,34]{2,0,1:T(8,128)S(1)}, f32[8,1,34]{2,0,1:T(8,128)S(1)}, u32[]{:S(2)}, u32[]{:S(2)}) collective-permute-start(f32[8,1,34]{2,0,1:T(8,128)S(1)} %slice_select_fusion.5), channel_id=1, source_target_pairs={{0,2},{2,0},{1,3},{3,1},{4,6},{6,4},{5,7},{7,5},{8,10},{10,8},{9,1... | collective-permute-start | bytes 3272 | tf_op jit(solution)/shard_map/ppermute | solution.py:74
  109.9 3.0 %add_convert_fusion = bf16[19,32,8,128]{3,1,2,0:T(8,128)(2,1)S(1)} fusion(f32[1,32,8,128]{3,1,2,0:T(8,128)S(1)} %get-tuple-element.104, f32[1,32,8,128]{3,1,2,0:T(8,128)S(1)} %get-tuple-element.105, bf16[19,32,8,128]{3,1,2,0:T(8,128)(2,1)} %fusion.304, f32[1,32,8,128]{3,1,2,0:T(8,128)S(1)} %get-tuple-element.106, ...), kind=kLoop, calls=%fused_computation.34 | loop fusion | flops 36732928 | bytes 5832723 | tf_op jit(solution)/shard_map/convert_element_type | solution.py:222
  113.0 1.6 %copy.148 = bf16[19,32,8,128]{3,2,1,0:T(8,128)(2,1)} copy(bf16[19,32,8,128]{3,1,2,0:T(8,128)(2,1)S(1)} %add_convert_fusion) | data formatting | bytes 2490368
  114.7 0.6 copy.149
  (77 shorter events, 4.4 us)
Async XLA Ops:
  0.6 25.5 %copy-start.4 = (bf16[19,32,8,128]{3,2,1,0:T(8,128)(2,1)S(1)}, bf16[19,32,8,128]{3,2,1,0:T(8,128)(2,1)}, u32[]{:S(2)}) copy-start(bf16[19,32,8,128]{3,2,1,0:T(8,128)(2,1)} %param.5) | copy-start | bytes 3735556
  1.5 24.0 %collective-permute-start.1 = (bf16[19,1,8,128]{3,2,1,0:T(8,128)(2,1)S(1)}, bf16[19,1,8,128]{3,2,1,0:T(8,128)(2,1)S(1)}, u32[]{:S(2)}, u32[]{:S(2)}) collective-permute-start(bf16[19,1,8,128]{3,2,1,0:T(8,128)(2,1)S(1)} %get-tuple-element.90), channel_id=1, source_target_pairs={{0,4},{4,8},{8,12},{1,5},{5,9},{9,13},{2,6},{6,10},{10,14},{3,7},{... | collective-permute-start | bytes 116744 | tf_op jit(solution)/shard_map/ppermute | solution.py:79
  6.5 21.0 %collective-permute-start = (bf16[19,1,8,128]{3,2,1,0:T(8,128)(2,1)S(1)}, bf16[19,1,8,128]{3,2,1,0:T(8,128)(2,1)S(1)}, u32[]{:S(2)}, u32[]{:S(2)}) collective-permute-start(bf16[19,1,8,128]{3,2,1,0:T(8,128)(2,1)S(1)} %get-tuple-element.91), channel_id=1, source_target_pairs={{4,0},{8,4},{12,8},{5,1},{9,5},{13,9},{6,2},{10,6},{14,10},{7,3},{... | collective-permute-start | bytes 116744 | tf_op jit(solution)/shard_map/ppermute | solution.py:79
  8.5 10.7 %collective-permute-start.4 = (f32[1,2,32]{2,0,1:T(1,128)S(1)}, f32[1,2,32]{2,0,1:T(1,128)S(1)}, u32[]{:S(2)}, u32[]{:S(2)}) collective-permute-start(f32[1,2,32]{2,0,1:T(1,128)S(1)} %bitcast.620), channel_id=1, source_target_pairs={{0,4},{4,8},{8,12},{1,5},{5,9},{9,13},{2,6},{6,10},{10,14},{3,7},{... | collective-permute-start | bytes 776 | tf_op jit(solution)/shard_map/ppermute | solution.py:79
  13.0 6.2 %collective-permute-start.5 = (f32[1,2,32]{2,0,1:T(1,128)S(1)}, f32[1,2,32]{2,0,1:T(1,128)S(1)}, u32[]{:S(2)}, u32[]{:S(2)}) collective-permute-start(f32[1,2,32]{2,0,1:T(1,128)S(1)} %bitcast.619), channel_id=1, source_target_pairs={{4,0},{8,4},{12,8},{5,1},{9,5},{13,9},{6,2},{10,6},{14,10},{7,3},{... | collective-permute-start | bytes 776 | tf_op jit(solution)/shard_map/ppermute | solution.py:79
  15.1 12.4 %copy-start.17 = (f32[34]{0:T(128)}, f32[34]{0:T(128)S(1)}, u32[]{:S(2)}) copy-start(f32[34]{0:T(128)S(1)} %add_multiply_fusion.2) | copy-start | bytes 412
  15.1 12.4 %copy-start.15 = (f32[4]{0:T(128)}, f32[4]{0:T(128)S(1)}, u32[]{:S(2)}) copy-start(f32[4]{0:T(128)S(1)} %add_multiply_fusion.3) | copy-start | bytes 52
  19.3 3.7 %collective-permute-start.6 = (f32[10,1,32]{2,0,1:T(8,128)S(1)}, f32[10,1,32]{2,0,1:T(8,128)S(1)}, u32[]{:S(2)}, u32[]{:S(2)}) collective-permute-start(f32[10,1,32]{2,0,1:T(8,128)S(1)} %slice_select_fusion.4), channel_id=1, source_target_pairs={{0,2},{2,0},{1,3},{3,1},{4,6},{6,4},{5,7},{7,5},{8,10},{10,8},{9,1... | collective-permute-start | bytes 3848 | tf_op jit(solution)/shard_map/ppermute | solution.py:74
  23.1 1.3 %collective-permute-start.7 = (f32[10,4,1]{2,0,1:T(8,128)S(1)}, f32[10,4,1]{2,0,1:T(8,128)S(1)}, u32[]{:S(2)}, u32[]{:S(2)}) collective-permute-start(f32[10,4,1]{2,0,1:T(8,128)S(1)} %slice_select_fusion.2), channel_id=1, source_target_pairs={{0,1},{1,0},{2,3},{3,2},{4,5},{5,4},{6,7},{7,6},{8,9},{9,8},{10,11... | collective-permute-start | bytes 488 | tf_op jit(solution)/shard_map/ppermute | solution.py:74
  39.6 7.3 %collective-permute-start.2 = (bf16[19,34,1,128]{3,1,2,0:T(8,128)(2,1)S(1)}, bf16[19,34,1,128]{3,1,2,0:T(8,128)(2,1)S(1)}, u32[]{:S(2)}, u32[]{:S(2)}) collective-permute-start(bf16[19,34,1,128]{3,1,2,0:T(8,128)(2,1)S(1)} %copy.127), channel_id=1, source_target_pairs={{0,2},{2,0},{1,3},{3,1},{4,6},{6,4},{5,7},{7,5},{8,10},{10,8},{9,1... | collective-permute-start | bytes 496136 | tf_op jit(solution)/shard_map/ppermute | solution.py:74
  49.9 5.7 %copy-start.6 = (bf16[19,34,1,128]{3,1,2,0:T(8,128)(2,1)}, bf16[19,34,1,128]{3,1,2,0:T(8,128)(2,1)S(1)}, u32[]{:S(2)}) copy-start(bf16[19,34,1,128]{3,1,2,0:T(8,128)(2,1)S(1)} %copy.130) | copy-start | bytes 496132
  50.4 6.4 %copy-start.8 = (bf16[19,34,1,128]{3,1,2,0:T(8,128)(2,1)}, bf16[19,34,1,128]{3,1,2,0:T(8,128)(2,1)S(1)}, u32[]{:S(2)}) copy-start(bf16[19,34,1,128]{3,1,2,0:T(8,128)(2,1)S(1)} %copy.132) | copy-start | bytes 496132
  55.0 3.1 %copy-start.2 = (bf16[19,34,10,128]{1,0,3,2:T(8,128)(2,1)}, bf16[19,34,10,128]{1,0,3,2:T(8,128)(2,1)S(1)}, u32[]{:S(2)}) copy-start(bf16[19,34,10,128]{1,0,3,2:T(8,128)(2,1)S(1)} %pad_maximum_fusion) | copy-start | bytes 4961284
  55.7 14.0 %collective-permute-start.3 = (bf16[19,34,10,1]{1,0,3,2:T(8,128)(2,1)}, bf16[19,34,10,1]{1,0,3,2:T(8,128)(2,1)}, u32[]{:S(2)}, u32[]{:S(2)}) collective-permute-start(bf16[19,34,10,1]{1,0,3,2:T(8,128)(2,1)} %slice_select_fusion.1), channel_id=1, source_target_pairs={{0,1},{1,0},{2,3},{3,2},{4,5},{5,4},{6,7},{7,6},{8,9},{9,8},{10,11... | collective-permute-start | bytes 38768 | tf_op jit(solution)/shard_map/ppermute | solution.py:74
  77.4 1.8 %copy-start.1 = (bf16[19,34,10,1]{3,1,2,0:T(8,128)(2,1)S(1)}, bf16[19,34,10,1]{3,1,2,0:T(8,128)(2,1)}, u32[]{:S(2)}) copy-start(bf16[19,34,10,1]{3,1,2,0:T(8,128)(2,1)} %copy.137) | copy-start | bytes 38764
  79.2 0.9 copy-start.7
  79.2 1.6 %copy-start.9 = (bf16[19,34,1,128]{3,1,2,0:T(8,128)(2,1)S(1)}, bf16[19,34,1,128]{3,1,2,0:T(8,128)(2,1)}, u32[]{:S(2)}) copy-start(bf16[19,34,1,128]{3,1,2,0:T(8,128)(2,1)} %copy-done.8) | copy-start | bytes 496132
  80.8 1.9 %copy-start = (bf16[19,34,10,1]{3,1,2,0:T(8,128)(2,1)S(1)}, bf16[19,34,10,1]{3,1,2,0:T(8,128)(2,1)}, u32[]{:S(2)}) copy-start(bf16[19,34,10,1]{3,1,2,0:T(8,128)(2,1)} %copy.136) | copy-start | bytes 38764
  87.9 1.3 %copy-start.5 = (bf16[19,32,8,128]{3,2,1,0:T(8,128)(2,1)S(1)}, bf16[19,32,8,128]{3,2,1,0:T(8,128)(2,1)}, u32[]{:S(2)}) copy-start(bf16[19,32,8,128]{3,2,1,0:T(8,128)(2,1)} %param.4) | copy-start | bytes 3735556
  87.9 1.3 %copy-start.10 = (pred[32,8,128]{2,0,1:T(8,128)(4,1)S(1)}, pred[32,8,128]{2,0,1:T(8,128)(4,1)}, u32[]{:S(2)}) copy-start(pred[32,8,128]{2,0,1:T(8,128)(4,1)} %copy.121) | copy-start | bytes 98308
  87.9 1.3 %copy-start.11 = (pred[32,8,128]{2,0,1:T(8,128)(4,1)S(1)}, pred[32,8,128]{2,0,1:T(8,128)(4,1)}, u32[]{:S(2)}) copy-start(pred[32,8,128]{2,0,1:T(8,128)(4,1)} %copy.140) | copy-start | bytes 98308
  89.2 2.6 %copy-start.3 = (f32[19,32,8,128]{3,1,2,0:T(8,128)S(1)}, f32[19,32,8,128]{3,1,2,0:T(8,128)}, u32[]{:S(2)}) copy-start(f32[19,32,8,128]{3,1,2,0:T(8,128)} %copy_convert_fusion) | copy-start | bytes 7471108
  91.8 0.7 copy-start.12
  91.8 0.8 copy-start.14
  94.7 3.1 %copy-start.16 = (f32[4]{0:T(128)S(1)}, f32[4]{0:T(128)}, u32[]{:S(2)}) copy-start(f32[4]{0:T(128)} %copy-done.15) | copy-start | bytes 52
  94.7 3.4 %copy-start.18 = (f32[34]{0:T(128)S(1)}, f32[34]{0:T(128)}, u32[]{:S(2)}) copy-start(f32[34]{0:T(128)} %copy-done.17) | copy-start | bytes 412
  98.3 6.3 %collective-permute-start.8 = (f32[1,4,34]{2,0,1:T(1,128)S(1)}, f32[1,4,34]{2,0,1:T(1,128)S(1)}, u32[]{:S(2)}, u32[]{:S(2)}) collective-permute-start(f32[1,4,34]{2,0,1:T(1,128)S(1)} %get-tuple-element.113), channel_id=1, source_target_pairs={{0,4},{4,8},{8,12},{1,5},{5,9},{9,13},{2,6},{6,10},{10,14},{3,7},{... | collective-permute-start | bytes 1640 | tf_op jit(solution)/shard_map/ppermute | solution.py:79
  102.9 5.5 %collective-permute-start.9 = (f32[1,4,34]{2,0,1:T(1,128)S(1)}, f32[1,4,34]{2,0,1:T(1,128)S(1)}, u32[]{:S(2)}, u32[]{:S(2)}) collective-permute-start(f32[1,4,34]{2,0,1:T(1,128)S(1)} %get-tuple-element.114), channel_id=1, source_target_pairs={{4,0},{8,4},{12,8},{5,1},{9,5},{13,9},{6,2},{10,6},{14,10},{7,3},{... | collective-permute-start | bytes 1640 | tf_op jit(solution)/shard_map/ppermute | solution.py:79
  104.2 5.8 %copy-start.13 = (pred[19]{0:T(512)(128)(4,1)S(1)}, pred[19]{0:T(512)(128)(4,1)}, u32[]{:S(2)}) copy-start(pred[19]{0:T(512)(128)(4,1)} %constant.41.clone.1) | copy-start | bytes 61
  108.4 4.5 %collective-permute-start.10 = (f32[8,1,34]{2,0,1:T(8,128)S(1)}, f32[8,1,34]{2,0,1:T(8,128)S(1)}, u32[]{:S(2)}, u32[]{:S(2)}) collective-permute-start(f32[8,1,34]{2,0,1:T(8,128)S(1)} %slice_select_fusion.5), channel_id=1, source_target_pairs={{0,2},{2,0},{1,3},{3,1},{4,6},{6,4},{5,7},{7,5},{8,10},{10,8},{9,1... | collective-permute-start | bytes 3272 | tf_op jit(solution)/shard_map/ppermute | solution.py:74
  113.0 1.6 %collective-permute-start.11 = (f32[8,2,1]{2,0,1:T(8,128)S(1)}, f32[8,2,1]{2,0,1:T(8,128)S(1)}, u32[]{:S(2)}, u32[]{:S(2)}) collective-permute-start(f32[8,2,1]{2,0,1:T(8,128)S(1)} %slice_select_fusion.3), channel_id=1, source_target_pairs={{0,1},{1,0},{2,3},{3,2},{4,5},{5,4},{6,7},{7,6},{8,9},{9,8},{10,11... | collective-permute-start | bytes 200 | tf_op jit(solution)/shard_map/ppermute | solution.py:74

commit v3 on v0

--- a/solution.py
+++ b/solution.py
@@ -31,6 +31,29 @@
 highest = lax.Precision.HIGHEST
 
 
+def exchange_one(low, high, axis, count):
+    if count == 1:
+        return [jnp.zeros_like(high)], [jnp.zeros_like(low)]
+    if count == 2:
+        index = lax.axis_index(axis)
+        received = lax.ppermute(jnp.where(index == 0, high, low), axis, [(0, 1), (1, 0)])
+        zero = jnp.zeros_like(received)
+        return [jnp.where(index == 1, received, zero)], [jnp.where(index == 0, received, zero)]
+    forward = [(i, i + 1) for i in range(count - 1)]
+    backward = [(target, source) for source, target in forward]
+    return [lax.ppermute(high, axis, forward)], [lax.ppermute(low, axis, backward)]
+
+
+def padded_swap(block, sides):
+    for axis, dim in sides:
+        length = block.shape[dim]
+        low = lax.slice_in_dim(block, 0, 1, axis=dim)
+        high = lax.slice_in_dim(block, length - 1, length, axis=dim)
+        from_prev, from_next = exchange_one(low, high, axis, lax.axis_size(axis))
+        block = jnp.concatenate([from_prev[0], block, from_next[0]], axis=dim)
+    return block
+
+
 def padded(block, sides, width):
     for axis, dim in sides:
         count = lax.axis_size(axis)
@@ -129,7 +152,7 @@
 def per_device(forward_pops, adjoint_pops, coefficients, node_kind):
     cells_x, cells_y, cells_z = node_kind.shape
     coarse_x, coarse_y, coarse_z = coefficients.shape
-    window = padded(coefficients, (("gx", 0), ("gy", 1), ("gz", 2)), 1)
+    window = padded_swap(coefficients, (("gx", 0), ("gy", 1), ("gz", 2)))
     basis_x = basis_matrix(cells_x, coarse_x + 2, 0, -1)
     basis_y = basis_matrix(cells_y, coarse_y + 2, 0, -1)
     basis_z = basis_matrix(cells_z, coarse_z + 2, 0, -1)
@@ -159,7 +182,7 @@
     partial_value = jnp.einsum("xyz,xi->iyz", sensitivity, basis_x, precision=highest)
     partial_value = jnp.einsum("iyz,yj->ijz", partial_value, basis_y, precision=highest)
     partial_value = jnp.einsum("ijz,zk->ijk", partial_value, basis_z, precision=highest)
-    bordered = padded(partial_value, (("gx", 0), ("gy", 1), ("gz", 2)), 1)
+    bordered = padded_swap(partial_value, (("gx", 0), ("gy", 1), ("gz", 2)))
     gradient = fold_rim(fold_rim(fold_rim(bordered, 0), 1), 2)
     return (prior_adjoint, gradient)
 

time: 96.6 us -> 99.4 us (1.029)
  local copies, waits for them, and re-layouts: 22.3 us -> 31 us
  starting transfers between devices: 39 us -> 30.4 us
  other arithmetic: 11.9 us -> 20.2 us
  waiting for transfers between devices: 18.2 us -> 12.3 us
    ppermute x9 -> x3, starting transfers between devices: 27.4 us -> 11.6 us  [padded(): lax.ppermute(lax.slice_in_dim(block, block.shape[dim] - width, None, axis...]
    ppermute x0 -> x8, starting transfers between devices: none -> 15 us  [the longest x2 10.7 us: exchange_one(): lax.ppermute(high, axis, forward)]
    ppermute x9 -> x3, waiting for transfers between devices: 18.1 us -> 4.12 us  [padded(): lax.ppermute(lax.slice_in_dim(block, 0, width, axis=dim), axis, backward)]
    ppermute x0 -> x8, waiting for transfers between devices: none -> 7.91 us  [the longest x4 4.03 us: exchange_one(): lax.ppermute(jnp.where(index == 0, high, low), axis, [(0, 1), (1, 0)])]
    ppermute x9 -> x3, starting transfers between devices: 11.6 us -> 3.87 us  [padded(): lax.ppermute(lax.slice_in_dim(block, 0, width, axis=dim), axis, backward)]
    unnamed x4, other arithmetic: 1.56 us -> 5.58 us
    unnamed x47 -> x55, local copies, waits for them, and re-layouts: 7.38 us -> 9.44 us
    select_n x0 -> x8, other arithmetic: none -> 1.48 us  [the longest x4 0.76 us: exchange_one(): jnp.where(index == 0, high, low)]
  transfers between devices with their start and end apart: 18 -> 14, of which waited for: 5 -> 5; matrix products, arithmetic and copies ran while one was open for 14% -> 26% of each run, Pallas kernels for 0% -> 0%
where the time goes in v3:
time: 99.4 us; the launch traced here: 98.1 us
  local copies, waits for them, and re-layouts  31 us (31%)
  starting transfers between devices  30.4 us (31%)
  other arithmetic  20.2 us (20%)
  waiting for transfers between devices  12.3 us (12%)
  matrix products  3 us (3%)
  between operations  1.21 us (1%)
    ppermute x3, starting transfers between devices, padded(): lax.ppermute(lax.slice_in_dim(block, block.shape[dim] - width, None, axis...  11.6 us
    ppermute x2, starting transfers between devices, exchange_one(): lax.ppermute(high, axis, forward)  10.7 us
    unnamed x55, local copies, waits for them, and re-layouts  9.44 us
    unnamed x4, other arithmetic  5.58 us
    slice x4, local copies, waits for them, and re-layouts, padded(): lax.slice_in_dim(block, block.shape[dim] - width, None, axis=dim)  5.18 us
    ppermute x3, waiting for transfers between devices, padded(): lax.ppermute(lax.slice_in_dim(block, 0, width, axis=dim), axis, backward)  4.12 us
    ppermute x4, waiting for transfers between devices, exchange_one(): lax.ppermute(jnp.where(index == 0, high, low), axis, [(0, 1), (1, 0)])  4.03 us
    ppermute x3, starting transfers between devices, padded(): lax.ppermute(lax.slice_in_dim(block, 0, width, axis=dim), axis, backward)  3.87 us
  transfers between devices with their start and end apart: 14, of which 5 were waited for; matrix products, arithmetic and copies ran while one was open for 26% of the time, Pallas kernels for 0%

profile of v3, /device:TPU:0, one launch (start us, length us, event | category | flops | bytes accessed | tf_op | source)
XLA Modules:
  0.0 98.1 jit_solution(15415451851936665589)
XLA Ops:
  0.6 1.4 %fusion.394 = (f32[1,2,32]{2,1,0:T(2,128)}, f32[1,2,32]{2,1,0:T(2,128)S(1)}) fusion(f32[8,2,32]{2,1,0:T(2,128)} %param.6), kind=kLoop, calls=%fused_computation.707 | loop fusion | bytes 1024 | tf_op jit(solution)/shard_map/slice | solution.py:50
  2.0 1.3 %collective-permute-start.7 = (f32[1,2,32]{2,1,0:T(2,128)}, f32[1,2,32]{2,1,0:T(2,128)}, u32[]{:S(2)}, u32[]{:S(2)}) collective-permute-start(f32[1,2,32]{2,1,0:T(2,128)} %get-tuple-element.145), channel_id=1, source_target_pairs={{4,0},{8,4},{12,8},{5,1},{9,5},{13,9},{6,2},{10,6},{14,10},{7,3},{... | collective-permute-start | bytes 776 | tf_op jit(solution)/shard_map/ppermute | solution.py:44
  3.3 6.2 %collective-permute-start.6 = (f32[1,2,32]{2,1,0:T(2,128)S(1)}, f32[1,2,32]{2,1,0:T(2,128)}, u32[]{:S(2)}, u32[]{:S(2)}) collective-permute-start(f32[1,2,32]{2,1,0:T(2,128)S(1)} %get-tuple-element.146), channel_id=1, source_target_pairs={{0,4},{4,8},{8,12},{1,5},{5,9},{9,13},{2,6},{6,10},{10,14},{3,7},{... | collective-permute-start | bytes 776 | tf_op jit(solution)/shard_map/ppermute | solution.py:44
  9.4 1.1 %fusion.389 = (bf16[2,32,8,128]{3,2,1,0:T(8,128)(2,1)S(1)}, bf16[2,32,8,128]{3,2,1,0:T(8,128)(2,1)S(1)}, bf16[2,32,8,128]{3,2,1,0:T(8,128)(2,1)S(1)}) fusion(bf16[19,32,8,128]{3,2,1,0:T(8,128)(2,1)} %param.5), kind=kLoop, calls=%fused_computation.702 | loop fusion | bytes 786432 | tf_op jit(solution)/shard_map/slice | solution.py:165
  10.5 1.1 %slice.379 = bf16[8,32,8,128]{3,2,1,0:T(8,128)(2,1)S(1)} slice(bf16[19,32,8,128]{3,2,1,0:T(8,128)(2,1)} %param.5), slice={[7:15], [0:32], [0:8], [0:128]} | slice | bytes 1048576 | tf_op jit(solution)/shard_map/slice | solution.py:165
  11.8 0.7 fusion.392
  12.5 4.0 %collective-permute-start.1 = (bf16[10,1,8,128]{3,1,2,0:T(2,128)(2,1)}, bf16[10,1,8,128]{3,1,2,0:T(2,128)(2,1)}, u32[]{:S(2)}, u32[]{:S(2)}) collective-permute-start(bf16[10,1,8,128]{3,1,2,0:T(2,128)(2,1)} %get-tuple-element.118), channel_id=1, source_target_pairs={{0,4},{4,8},{8,12},{1,5},{5,9},{9,13},{2,6},{6,10},{10,14},{3,7},{... | collective-permute-start | bytes 61448 | tf_op jit(solution)/shard_map/ppermute | solution.py:62
  16.4 1.3 %collective-permute-start = (bf16[10,1,8,128]{3,1,2,0:T(2,128)(2,1)}, bf16[10,1,8,128]{3,1,2,0:T(2,128)(2,1)}, u32[]{:S(2)}, u32[]{:S(2)}) collective-permute-start(bf16[10,1,8,128]{3,1,2,0:T(2,128)(2,1)} %get-tuple-element.119), channel_id=1, source_target_pairs={{4,0},{8,4},{12,8},{5,1},{9,5},{13,9},{6,2},{10,6},{14,10},{7,3},{... | collective-permute-start | bytes 61448 | tf_op jit(solution)/shard_map/ppermute | solution.py:65
  17.7 0.6 add_multiply_fusion.4
  18.4 0.3 copy_convert_fusion
  18.8 0.4 copy-done.7
  19.2 0.7 broadcast_compare_fusion.2
  19.9 0.6 constant_dynamic-update-slice_fusion.30
  20.5 0.7 copy_dynamic-update-slice_fusion.2
  21.3 0.7 constant_dynamic-update-slice_fusion.33
  21.9 0.7 constant_dynamic-update-slice_fusion.32
  22.7 0.6 constant_dynamic-update-slice_fusion.31
  23.3 0.6 broadcast_select_fusion.5
  23.9 1.5 %collective-permute-start.8 = (f32[10,1,32]{2,1,0:T(1,128)}, f32[10,1,32]{2,1,0:T(1,128)}, u32[]{:S(2)}, u32[]{:S(2)}) collective-permute-start(f32[10,1,32]{2,1,0:T(1,128)} %broadcast_select_fusion.5), channel_id=1, source_target_pairs={{0,2},{2,0},{1,3},{3,1},{4,6},{6,4},{5,7},{7,5},{8,10},{10,8},{9,1... | collective-permute-start | bytes 3848 | tf_op jit(solution)/shard_map/ppermute | solution.py:39
  25.4 0.6 add_multiply_fusion.2
  26.0 1.4 %copy.18 = pred[32,8,128]{2,0,1:T(8,128)(4,1)} copy(pred[32,8,128]{2,1,0:T(8,128)(4,1)} %get-tuple-element.134) | data formatting | bytes 65536 | tf_op jit(solution)/shard_map/jvp()/eq | solution.py:112
  27.4 0.5 collective-permute-done.8
  27.8 0.7 broadcast_select_fusion.6
  28.7 1.4 %copy.19 = pred[32,8,128]{2,0,1:T(8,128)(4,1)} copy(pred[32,8,128]{2,1,0:T(8,128)(4,1)} %get-tuple-element.136) | data formatting | bytes 65536 | tf_op jit(solution)/shard_map/jvp()/eq | solution.py:110
  30.1 1.4 %copy.31 = pred[32,8,128]{2,0,1:T(8,128)(4,1)} copy(pred[32,8,128]{2,1,0:T(8,128)(4,1)} %get-tuple-element.135) | data formatting | bytes 65536 | tf_op jit(solution)/shard_map/jvp()/eq | solution.py:112
  31.6 0.9 fusion.313
  32.5 1.4 %constant_dynamic-update-slice_fusion.11 = (bf16[10,32,8,128]{3,1,2,0:T(8,128)(2,1)}, bf16[10,32,8,128]{3,1,2,0:T(8,128)(2,1)}) fusion(bf16[10,32,8,128]{3,1,2,0:T(8,128)(2,1)} %get-tuple-element.150, bf16[10,1,8,128]{3,1,2,0:T(2,128)(2,1)} %collective-permute-done, bf16[10,32,8,128]{3,1,2,0:T(8,128)(2,1)S(1)} %copy_dynamic-update-slice_fusion, ...), kind=kLoop, calls=%fused_computation.532 | loop fusion | flops 262144 | bytes 827392
  33.9 1.4 %constant_dynamic-update-slice_fusion.10 = (bf16[10,32,8,128]{3,1,2,0:T(8,128)(2,1)}, bf16[10,32,8,128]{3,1,2,0:T(8,128)(2,1)}) fusion(bf16[10,32,8,128]{3,1,2,0:T(8,128)(2,1)} %get-tuple-element.112, bf16[10,32,8,128]{3,1,2,0:T(8,128)(2,1)S(1)} %copy_dynamic-update-slice_fusion, bf16[10,1,8,128]{3,1,2,0:T(2,128)(2,1)} %collective-permute-done.1, ...), kind=kLoop, calls=%fused_computation.531 | loop fusion | flops 262144 | bytes 827392
  35.3 1.4 %constant_dynamic-update-slice_fusion.9 = (bf16[10,32,8,128]{3,1,2,0:T(8,128)(2,1)}, bf16[10,32,8,128]{3,1,2,0:T(8,128)(2,1)}, bf16[19,32,8,128]{3,1,2,0:T(8,128)(2,1)}) fusion(bf16[10,32,8,128]{3,1,2,0:T(8,128)(2,1)} %get-tuple-element.110, bf16[10,1,8,128]{3,1,2,0:T(2,128)(2,1)} %collective-permute-done, ...), kind=kLoop, calls=%fused_computation.530 | loop fusion | flops 393216 | bytes 892928
  36.7 1.4 %constant_dynamic-update-slice_fusion.8 = (bf16[10,32,8,128]{3,1,2,0:T(8,128)(2,1)}, bf16[10,32,8,128]{3,1,2,0:T(8,128)(2,1)}, bf16[19,32,8,128]{3,1,2,0:T(8,128)(2,1)}) fusion(bf16[10,32,8,128]{3,1,2,0:T(8,128)(2,1)} %get-tuple-element.107, bf16[10,32,8,128]{3,1,2,0:T(8,128)(2,1)S(1)} %copy_dynamic-update-slice_fusion, ...), kind=kLoop, calls=%fused_computation.529 | loop fusion | flops 393216 | bytes 892928
  38.1 0.7 copy_dynamic-update-slice_fusion.1
  38.8 0.9 fusion.391
  39.8 3.4 %collective-permute-start.2 = (bf16[10,32,1,128]{3,1,2,0:T(8,128)(2,1)S(1)}, bf16[10,32,1,128]{3,1,2,0:T(8,128)(2,1)S(1)}, u32[]{:S(2)}, u32[]{:S(2)}) collective-permute-start(bf16[10,32,1,128]{3,1,2,0:T(8,128)(2,1)S(1)} %get-tuple-element.116), channel_id=1, source_target_pairs={{0,2},{1,3},{4,6},{5,7},{8,10},{9,11},{12,14},{13,15},{16,18},{17,... | collective-permute-start | bytes 245768 | tf_op jit(solution)/shard_map/ppermute | solution.py:62
  43.2 1.3 %collective-permute-start.3 = (bf16[10,32,1,128]{3,1,2,0:T(8,128)(2,1)S(1)}, bf16[10,32,1,128]{3,1,2,0:T(8,128)(2,1)S(1)}, u32[]{:S(2)}, u32[]{:S(2)}) collective-permute-start(bf16[10,32,1,128]{3,1,2,0:T(8,128)(2,1)S(1)} %get-tuple-element.117), channel_id=1, source_target_pairs={{2,0},{3,1},{6,4},{7,5},{10,8},{11,9},{14,12},{15,13},{18,16},{19,... | collective-permute-start | bytes 245768 | tf_op jit(solution)/shard_map/ppermute | solution.py:65
  44.5 0.8 fusion.328
  45.5 4.1 %collective-permute-done.3 = bf16[10,32,1,128]{3,1,2,0:T(8,128)(2,1)S(1)} collective-permute-done((bf16[10,32,1,128]{3,1,2,0:T(8,128)(2,1)S(1)}, bf16[10,32,1,128]{3,1,2,0:T(8,128)(2,1)S(1)}, u32[]{:S(2)}, u32[]{:S(2)}) %collective-permute-start.3) | collective-permute-done | bytes 81952 | tf_op jit(solution)/shard_map/ppermute | solution.py:65
  49.6 1.2 %pad_maximum_fusion.1 = bf16[10,32,10,128]{3,1,2,0:T(8,128)(2,1)S(1)} fusion(bf16[10,32,1,128]{3,1,2,0:T(8,128)(2,1)S(1)} %collective-permute-done.3, bf16[10,32,8,128]{3,1,2,0:T(8,128)(2,1)} %copy_dynamic-update-slice_fusion.1, bf16[10,32,1,128]{3,1,2,0:T(8,128)(2,1)S(1)} %collective-permute-done.2), kind=kLoop, calls=%fused_computation.38 | loop fusion | flops 819200 | bytes 1638400 | tf_op jit(solution)/shard_map/concatenate | solution.py:66
  50.8 0.7 slice_bitcast_fusion.31
  51.7 1.3 %fusion.390 = (bf16[10,32,8,1]{3,1,2,0:T(8,128)(2,1)}, bf16[10,32,8,1]{3,1,2,0:T(8,128)(2,1)}) fusion(bf16[10,32,8,128]{3,1,2,0:T(8,128)(2,1)S(1)} %constant_dynamic-update-slice_fusion.4), kind=kLoop, calls=%fused_computation.703 | loop fusion | bytes 20480 | tf_op jit(solution)/shard_map/slice | solution.py:63
  53.0 2.2 %copy.26 = bf16[10,32,8,1]{1,2,3,0:T(8,128)(2,1)} copy(bf16[10,32,8,1]{3,1,2,0:T(8,128)(2,1)} %get-tuple-element.114) | data formatting | bytes 10240 | tf_op jit(solution)/shard_map/slice | solution.py:63
  55.2 1.6 %copy.27 = bf16[10,32,8,1]{1,2,3,0:T(8,128)(2,1)S(1)} copy(bf16[10,32,8,1]{3,1,2,0:T(8,128)(2,1)} %get-tuple-element.115) | data formatting | bytes 10240 | tf_op jit(solution)/shard_map/slice | solution.py:65
  56.8 1.3 %collective-permute-start.5 = (bf16[10,32,8,1]{1,2,3,0:T(8,128)(2,1)S(1)}, bf16[10,32,8,1]{1,2,3,0:T(8,128)(2,1)}, u32[]{:S(2)}, u32[]{:S(2)}) collective-permute-start(bf16[10,32,8,1]{1,2,3,0:T(8,128)(2,1)S(1)} %copy.27), channel_id=1, source_target_pairs={{1,0},{3,2},{5,4},{7,6},{9,8},{11,10},{13,12},{15,14},{17,16},{19,... | collective-permute-start | bytes 15368 | tf_op jit(solution)/shard_map/ppermute | solution.py:65
  58.1 4.2 %collective-permute-start.4 = (bf16[10,32,8,1]{1,2,3,0:T(8,128)(2,1)}, bf16[10,32,8,1]{1,2,3,0:T(8,128)(2,1)}, u32[]{:S(2)}, u32[]{:S(2)}) collective-permute-start(bf16[10,32,8,1]{1,2,3,0:T(8,128)(2,1)} %copy.26), channel_id=1, source_target_pairs={{0,1},{2,3},{4,5},{6,7},{8,9},{10,11},{12,13},{14,15},{16,17},{18,... | collective-permute-start | bytes 15368 | tf_op jit(solution)/shard_map/ppermute | solution.py:62
  62.3 1.5 %constant_dynamic-update-slice_fusion.27 = bf16[19,32,8,128]{3,1,2,0:T(8,128)(2,1)} fusion(bf16[19,32,8,128]{3,1,2,0:T(8,128)(2,1)} %get-tuple-element.106, bf16[32,10,128]{2,0,1:T(8,128)(2,1)} %get-tuple-element.103), kind=kLoop, calls=%fused_computation.548 | loop fusion | bytes 131072
  63.8 1.5 %constant_dynamic-update-slice_fusion.26 = bf16[19,32,8,128]{3,1,2,0:T(8,128)(2,1)} fusion(bf16[19,32,8,128]{3,1,2,0:T(8,128)(2,1)} %constant_dynamic-update-slice_fusion.27, bf16[32,10,128]{2,0,1:T(8,128)(2,1)} %get-tuple-element.102), kind=kLoop, calls=%fused_computation.547 | loop fusion | bytes 131072
  65.3 2.1 %copy.28 = bf16[10,32,8,1]{3,1,2,0:T(8,128)(2,1)} copy(bf16[10,32,8,1]{1,2,3,0:T(8,128)(2,1)} %collective-permute-done.4) | data formatting | bytes 10240 | tf_op jit(solution)/shard_map/ppermute | solution.py:62
  67.4 2.1 %copy.29 = bf16[10,32,8,1]{3,1,2,0:T(8,128)(2,1)} copy(bf16[10,32,8,1]{1,2,3,0:T(8,128)(2,1)} %collective-permute-done.5) | data formatting | bytes 10240 | tf_op jit(solution)/shard_map/ppermute | solution.py:65
  69.5 2.1 %pad_maximum_fusion = bf16[10,32,8,130]{3,1,2,0:T(8,128)(2,1)S(1)} fusion(bf16[10,32,8,1]{3,1,2,0:T(8,128)(2,1)} %copy.29, bf16[10,32,8,128]{3,1,2,0:T(8,128)(2,1)S(1)} %constant_dynamic-update-slice_fusion.4, bf16[10,32,8,1]{3,1,2,0:T(8,128)(2,1)} %copy.28), kind=kLoop, calls=%fused_computation.34 | loop fusion | flops 1996800 | bytes 1331200 | tf_op jit(solution)/shard_map/concatenate | solution.py:66
  72.6 1.1 %fusion.1 = (f32[19,32,8,128]{3,1,2,0:T(8,128)S(1)}, f32[19,32,8,128]{3,1,2,0:T(8,128)S(1)}, f32[19,32,8,128]{3,1,2,0:T(8,128)S(1)}) fusion(bf16[19,32,8,128]{3,1,2,0:T(8,128)(2,1)S(1)} %constant_dynamic-update-slice_fusion.12, pred[32,8,128]{2,0,1:T(8,128)(4,1)S(1)} %copy-done.4, pred[32,8,128]{2,0,1:T(8,128)(4,1)S(1)} %copy-done.3, ...), kind=kLoop, calls=%fused_computation.3 | loop fusion | flops 5603328 | bytes 8814592 | tf_op jit(solution)/shard_map/transpose(jvp(jit(_where)))/select_n | solution.py:112
  73.7 0.3 bitcast_add_fusion.11
  74.0 0.4 copy-done.8
  74.5 0.5 bitcast_add_fusion.17
  75.2 0.7 fusion.60
  75.8 0.7 bitcast_add_fusion.16
  76.5 2.8 %negate_add_fusion = (f32[32,8,128]{2,0,1:T(8,128)S(1)}, f32[32,8,128]{2,0,1:T(8,128)S(1)}, f32[32,8,128]{2,0,1:T(8,128)S(1)}, f32[32,8,128]{2,0,1:T(8,128)S(1)}...) fusion(f32[32,8,128]{2,0,1:T(8,128)S(1)} %get-tuple-element.15, ...), kind=kLoop, calls=%fused_computation.452 | loop fusion | flops 17006592 | bytes 12320768 | tf_op jit(solution)/shard_map/transpose(jvp())/add_any | solution.py:95
  79.3 0.3 fusion.273
  80.2 4.6 %collective-permute-start.10 = (f32[1,4,34]{2,0,1:T(1,128)S(1)}, f32[1,4,34]{2,0,1:T(1,128)S(1)}, u32[]{:S(2)}, u32[]{:S(2)}) collective-permute-start(f32[1,4,34]{2,0,1:T(1,128)S(1)} %get-tuple-element.139), channel_id=1, source_target_pairs={{0,4},{4,8},{8,12},{1,5},{5,9},{9,13},{2,6},{6,10},{10,14},{3,7},{... | collective-permute-start | bytes 1640 | tf_op jit(solution)/shard_map/ppermute | solution.py:44
  84.7 1.3 %collective-permute-start.11 = (f32[1,4,34]{2,0,1:T(1,128)S(1)}, f32[1,4,34]{2,0,1:T(1,128)S(1)}, u32[]{:S(2)}, u32[]{:S(2)}) collective-permute-start(f32[1,4,34]{2,0,1:T(1,128)S(1)} %get-tuple-element.140), channel_id=1, source_target_pairs={{4,0},{8,4},{12,8},{5,1},{9,5},{13,9},{6,2},{10,6},{14,10},{7,3},{... | collective-permute-start | bytes 1640 | tf_op jit(solution)/shard_map/ppermute | solution.py:44
  86.0 0.3 fusion.388
  86.3 3.9 %collective-permute-done.11 = f32[1,4,34]{2,0,1:T(1,128)S(1)} collective-permute-done((f32[1,4,34]{2,0,1:T(1,128)S(1)}, f32[1,4,34]{2,0,1:T(1,128)S(1)}, u32[]{:S(2)}, u32[]{:S(2)}) %collective-permute-start.11) | collective-permute-done | bytes 576 | tf_op jit(solution)/shard_map/ppermute | solution.py:44
  90.4 3.6 %collective-permute-done.12 = f32[12,1,34]{2,0,1:T(8,128)S(1)} collective-permute-done((f32[12,1,34]{2,0,1:T(8,128)S(1)}, f32[12,1,34]{2,0,1:T(8,128)S(1)}, u32[]{:S(2)}, u32[]{:S(2)}) %collective-permute-start.12) | collective-permute-done | bytes 1664 | tf_op jit(solution)/shard_map/ppermute | solution.py:39
  94.1 1.3 %add_convert_fusion = bf16[19,32,8,128]{3,1,2,0:T(8,128)(2,1)S(1)} fusion(f32[1,32,8,128]{3,1,2,0:T(8,128)S(1)} %get-tuple-element.130, f32[1,32,8,128]{3,1,2,0:T(8,128)S(1)} %get-tuple-element.131, bf16[19,32,8,128]{3,1,2,0:T(8,128)(2,1)S(1)} %constant_dynamic-update-slice_fusion.12, f32[1,32,8,128]{3,1,2,0:T(8,128)S(1)} %get-tuple-element.132, ...), kind=kLoop, calls=%fused_computation.33 | loop fusion | flops 36732928 | bytes 5832723 | tf_op jit(solution)/shard_map/convert_element_type | solution.py:180
  95.4 1.6 %copy.32 = bf16[19,32,8,128]{3,2,1,0:T(8,128)(2,1)} copy(bf16[19,32,8,128]{3,1,2,0:T(8,128)(2,1)S(1)} %add_convert_fusion) | data formatting | bytes 2490368
  97.5 0.6 copy.33
  (88 shorter events, 3.1 us)
Async XLA Ops:
  0.6 17.7 %copy-start.2 = (bf16[19,32,8,128]{3,2,1,0:T(8,128)(2,1)S(1)}, bf16[19,32,8,128]{3,2,1,0:T(8,128)(2,1)}, u32[]{:S(2)}) copy-start(bf16[19,32,8,128]{3,2,1,0:T(8,128)(2,1)} %param.4) | copy-start | bytes 3735556
  2.0 20.7 %collective-permute-start.7 = (f32[1,2,32]{2,1,0:T(2,128)}, f32[1,2,32]{2,1,0:T(2,128)}, u32[]{:S(2)}, u32[]{:S(2)}) collective-permute-start(f32[1,2,32]{2,1,0:T(2,128)} %get-tuple-element.145), channel_id=1, source_target_pairs={{4,0},{8,4},{12,8},{5,1},{9,5},{13,9},{6,2},{10,6},{14,10},{7,3},{... | collective-permute-start | bytes 776 | tf_op jit(solution)/shard_map/ppermute | solution.py:44
  3.3 18.0 %collective-permute-start.6 = (f32[1,2,32]{2,1,0:T(2,128)S(1)}, f32[1,2,32]{2,1,0:T(2,128)}, u32[]{:S(2)}, u32[]{:S(2)}) collective-permute-start(f32[1,2,32]{2,1,0:T(2,128)S(1)} %get-tuple-element.146), channel_id=1, source_target_pairs={{0,4},{4,8},{8,12},{1,5},{5,9},{9,13},{2,6},{6,10},{10,14},{3,7},{... | collective-permute-start | bytes 776 | tf_op jit(solution)/shard_map/ppermute | solution.py:44
  12.5 21.4 %collective-permute-start.1 = (bf16[10,1,8,128]{3,1,2,0:T(2,128)(2,1)}, bf16[10,1,8,128]{3,1,2,0:T(2,128)(2,1)}, u32[]{:S(2)}, u32[]{:S(2)}) collective-permute-start(bf16[10,1,8,128]{3,1,2,0:T(2,128)(2,1)} %get-tuple-element.118), channel_id=1, source_target_pairs={{0,4},{4,8},{8,12},{1,5},{5,9},{9,13},{2,6},{6,10},{10,14},{3,7},{... | collective-permute-start | bytes 61448 | tf_op jit(solution)/shard_map/ppermute | solution.py:62
  16.4 16.1 %collective-permute-start = (bf16[10,1,8,128]{3,1,2,0:T(2,128)(2,1)}, bf16[10,1,8,128]{3,1,2,0:T(2,128)(2,1)}, u32[]{:S(2)}, u32[]{:S(2)}) collective-permute-start(bf16[10,1,8,128]{3,1,2,0:T(2,128)(2,1)} %get-tuple-element.119), channel_id=1, source_target_pairs={{4,0},{8,4},{12,8},{5,1},{9,5},{13,9},{6,2},{10,6},{14,10},{7,3},{... | collective-permute-start | bytes 61448 | tf_op jit(solution)/shard_map/ppermute | solution.py:65
  18.3 0.9 copy-start.7
  18.3 1.6 %slice-start = ((bf16[19,32,8,128]{3,2,1,0:T(8,128)(2,1)}), bf16[1,32,8,128]{3,2,1,0:T(8,128)(2,1)S(1)}, s32[]{:S(2)}) async-start(bf16[19,32,8,128]{3,2,1,0:T(8,128)(2,1)} %param.5), calls=%async_computation | async-start | bytes 131072 | tf_op jit(solution)/shard_map/slice | solution.py:165
  20.5 17.5 %slice-start.1 = ((bf16[19,32,8,128]{3,2,1,0:T(8,128)(2,1)}), bf16[4,32,8,128]{3,2,1,0:T(8,128)(2,1)S(1)}, s32[]{:S(2)}) async-start(bf16[19,32,8,128]{3,2,1,0:T(8,128)(2,1)} %param.5), calls=%async_computation.1 | async-start | bytes 524288 | tf_op jit(solution)/shard_map/slice | solution.py:165
  23.9 3.9 %collective-permute-start.8 = (f32[10,1,32]{2,1,0:T(1,128)}, f32[10,1,32]{2,1,0:T(1,128)}, u32[]{:S(2)}, u32[]{:S(2)}) collective-permute-start(f32[10,1,32]{2,1,0:T(1,128)} %broadcast_select_fusion.5), channel_id=1, source_target_pairs={{0,2},{2,0},{1,3},{3,1},{4,6},{6,4},{5,7},{7,5},{8,10},{10,8},{9,1... | collective-permute-start | bytes 3848 | tf_op jit(solution)/shard_map/ppermute | solution.py:39
  28.6 2.8 %collective-permute-start.9 = (f32[10,4,1]{2,1,0:T(4,128)S(1)}, f32[10,4,1]{2,1,0:T(4,128)S(1)}, u32[]{:S(2)}, u32[]{:S(2)}) collective-permute-start(f32[10,4,1]{2,1,0:T(4,128)S(1)} %slice_select_fusion.2), channel_id=1, source_target_pairs={{0,1},{1,0},{2,3},{3,2},{4,5},{5,4},{6,7},{7,6},{8,9},{9,8},{10,11... | collective-permute-start | bytes 488 | tf_op jit(solution)/shard_map/ppermute | solution.py:39
  38.1 13.5 %copy-start = (bf16[10,32,8,128]{3,1,2,0:T(8,128)(2,1)S(1)}, bf16[10,32,8,128]{3,1,2,0:T(8,128)(2,1)}, u32[]{:S(2)}) copy-start(bf16[10,32,8,128]{3,1,2,0:T(8,128)(2,1)} %get-tuple-element.104) | copy-start | bytes 1966084
  39.8 5.7 %collective-permute-start.2 = (bf16[10,32,1,128]{3,1,2,0:T(8,128)(2,1)S(1)}, bf16[10,32,1,128]{3,1,2,0:T(8,128)(2,1)S(1)}, u32[]{:S(2)}, u32[]{:S(2)}) collective-permute-start(bf16[10,32,1,128]{3,1,2,0:T(8,128)(2,1)S(1)} %get-tuple-element.116), channel_id=1, source_target_pairs={{0,2},{1,3},{4,6},{5,7},{8,10},{9,11},{12,14},{13,15},{16,18},{17,... | collective-permute-start | bytes 245768 | tf_op jit(solution)/shard_map/ppermute | solution.py:62
  43.2 6.5 %collective-permute-start.3 = (bf16[10,32,1,128]{3,1,2,0:T(8,128)(2,1)S(1)}, bf16[10,32,1,128]{3,1,2,0:T(8,128)(2,1)S(1)}, u32[]{:S(2)}, u32[]{:S(2)}) collective-permute-start(bf16[10,32,1,128]{3,1,2,0:T(8,128)(2,1)S(1)} %get-tuple-element.117), channel_id=1, source_target_pairs={{2,0},{3,1},{6,4},{7,5},{10,8},{11,9},{14,12},{15,13},{18,16},{19,... | collective-permute-start | bytes 245768 | tf_op jit(solution)/shard_map/ppermute | solution.py:65
  56.8 10.6 %collective-permute-start.5 = (bf16[10,32,8,1]{1,2,3,0:T(8,128)(2,1)S(1)}, bf16[10,32,8,1]{1,2,3,0:T(8,128)(2,1)}, u32[]{:S(2)}, u32[]{:S(2)}) collective-permute-start(bf16[10,32,8,1]{1,2,3,0:T(8,128)(2,1)S(1)} %copy.27), channel_id=1, source_target_pairs={{1,0},{3,2},{5,4},{7,6},{9,8},{11,10},{13,12},{15,14},{17,16},{19,... | collective-permute-start | bytes 15368 | tf_op jit(solution)/shard_map/ppermute | solution.py:65
  58.1 7.2 %collective-permute-start.4 = (bf16[10,32,8,1]{1,2,3,0:T(8,128)(2,1)}, bf16[10,32,8,1]{1,2,3,0:T(8,128)(2,1)}, u32[]{:S(2)}, u32[]{:S(2)}) collective-permute-start(bf16[10,32,8,1]{1,2,3,0:T(8,128)(2,1)} %copy.26), channel_id=1, source_target_pairs={{0,1},{2,3},{4,5},{6,7},{8,9},{10,11},{12,13},{14,15},{16,17},{18,... | collective-permute-start | bytes 15368 | tf_op jit(solution)/shard_map/ppermute | solution.py:62
  69.5 2.3 %copy-start.1 = (bf16[19,32,8,128]{3,1,2,0:T(8,128)(2,1)S(1)}, bf16[19,32,8,128]{3,1,2,0:T(8,128)(2,1)}, u32[]{:S(2)}) copy-start(bf16[19,32,8,128]{3,1,2,0:T(8,128)(2,1)} %constant_dynamic-update-slice_fusion.26) | copy-start | bytes 3735556
  69.5 2.4 %copy-start.5 = (bf16[32,10,128]{2,0,1:T(8,128)(2,1)S(1)}, bf16[32,10,128]{2,0,1:T(8,128)(2,1)}, u32[]{:S(2)}) copy-start(bf16[32,10,128]{2,0,1:T(8,128)(2,1)} %get-tuple-element.97) | copy-start | bytes 245764
  71.7 0.9 copy-start.3
  71.7 0.9 copy-start.4
  71.7 0.9 copy-start.6
  73.7 0.8 copy-start.8
  73.7 0.8 copy-start.9
  76.5 3.4 %copy-start.14 = (f32[34]{0:T(128)S(1)}, f32[34]{0:T(128)}, u32[]{:S(2)}) copy-start(f32[34]{0:T(128)} %add_multiply_fusion.2) | copy-start | bytes 412
  80.2 6.2 %collective-permute-start.10 = (f32[1,4,34]{2,0,1:T(1,128)S(1)}, f32[1,4,34]{2,0,1:T(1,128)S(1)}, u32[]{:S(2)}, u32[]{:S(2)}) collective-permute-start(f32[1,4,34]{2,0,1:T(1,128)S(1)} %get-tuple-element.139), channel_id=1, source_target_pairs={{0,4},{4,8},{8,12},{1,5},{5,9},{9,13},{2,6},{6,10},{10,14},{3,7},{... | collective-permute-start | bytes 1640 | tf_op jit(solution)/shard_map/ppermute | solution.py:44
  84.7 5.5 %collective-permute-start.11 = (f32[1,4,34]{2,0,1:T(1,128)S(1)}, f32[1,4,34]{2,0,1:T(1,128)S(1)}, u32[]{:S(2)}, u32[]{:S(2)}) collective-permute-start(f32[1,4,34]{2,0,1:T(1,128)S(1)} %get-tuple-element.140), channel_id=1, source_target_pairs={{4,0},{8,4},{12,8},{5,1},{9,5},{13,9},{6,2},{10,6},{14,10},{7,3},{... | collective-permute-start | bytes 1640 | tf_op jit(solution)/shard_map/ppermute | solution.py:44
  86.0 8.1 %copy-start.13 = (pred[19]{0:T(512)(128)(4,1)S(1)}, pred[19]{0:T(512)(128)(4,1)}, u32[]{:S(2)}) copy-start(pred[19]{0:T(512)(128)(4,1)} %constant.42.clone.1) | copy-start | bytes 61
  90.2 3.7 %collective-permute-start.12 = (f32[12,1,34]{2,0,1:T(8,128)S(1)}, f32[12,1,34]{2,0,1:T(8,128)S(1)}, u32[]{:S(2)}, u32[]{:S(2)}) collective-permute-start(f32[12,1,34]{2,0,1:T(8,128)S(1)} %fusion.339), channel_id=1, source_target_pairs={{0,2},{2,0},{1,3},{3,1},{4,6},{6,4},{5,7},{7,5},{8,10},{10,8},{9,1... | collective-permute-start | bytes 4904 | tf_op jit(solution)/shard_map/ppermute | solution.py:39
  94.0 3.0 %collective-permute-start.13 = (f32[12,6,1]{2,0,1:T(8,128)S(1)}, f32[12,6,1]{2,0,1:T(8,128)S(1)}, u32[]{:S(2)}, u32[]{:S(2)}) collective-permute-start(f32[12,6,1]{2,0,1:T(8,128)S(1)} %slice_select_fusion), channel_id=1, source_target_pairs={{0,1},{1,0},{2,3},{3,2},{4,5},{5,4},{6,7},{7,6},{8,9},{9,8},{10,11... | collective-permute-start | bytes 872 | tf_op jit(solution)/shard_map/ppermute | solution.py:39
  95.4 1.7 %copy-start.12 = (pred[8]{0:T(512)(128)(4,1)S(1)}, pred[8]{0:T(512)(128)(4,1)}, u32[]{:S(2)}) copy-start(pred[8]{0:T(512)(128)(4,1)} %constant.106.clone.1) | copy-start | bytes 28
  95.4 1.9 %copy-start.11 = (pred[2]{0:T(512)(128)(4,1)S(1)}, pred[2]{0:T(512)(128)(4,1)}, u32[]{:S(2)}) copy-start(pred[2]{0:T(512)(128)(4,1)} %constant.107.clone.1) | copy-start | bytes 10
  95.4 2.0 %copy-start.10 = (pred[32]{0:T(512)(128)(4,1)S(1)}, pred[32]{0:T(512)(128)(4,1)}, u32[]{:S(2)}) copy-start(pred[32]{0:T(512)(128)(4,1)} %constant.108.clone.1) | copy-start | bytes 100

commit v4 on v0

--- a/solution.py
+++ b/solution.py
@@ -129,13 +129,25 @@
 def per_device(forward_pops, adjoint_pops, coefficients, node_kind):
     cells_x, cells_y, cells_z = node_kind.shape
     coarse_x, coarse_y, coarse_z = coefficients.shape
-    window = padded(coefficients, (("gx", 0), ("gy", 1), ("gz", 2)), 1)
+    count_x, count_y, count_z = (lax.axis_size(axis) for axis in ("gx", "gy", "gz"))
+    gathered = lax.all_gather(coefficients, ("gx", "gy", "gz"))
+    gathered = gathered.reshape(count_x, count_y, count_z, coarse_x, coarse_y, coarse_z)
+    gathered = gathered.transpose(0, 3, 1, 4, 2, 5).reshape(
+        count_x * coarse_x, count_y * coarse_y, count_z * coarse_z
+    )
+    start_x, start_y, start_z = (
+        (lax.axis_index(axis) * cells).astype(jnp.float32)
+        for axis, cells in (("gx", cells_x), ("gy", cells_y), ("gz", cells_z))
+    )
+    full_x = basis_matrix(cells_x, count_x * coarse_x, start_x, 0)
+    full_y = basis_matrix(cells_y, count_y * coarse_y, start_y, 0)
+    full_z = basis_matrix(cells_z, count_z * coarse_z, start_z, 0)
+    partway = jnp.einsum("ijk,zk->ijz", gathered, full_z, precision=highest)
+    partway = jnp.einsum("ijz,yj->iyz", partway, full_y, precision=highest)
+    level_set = jnp.einsum("iyz,xi->xyz", partway, full_x, precision=highest)
     basis_x = basis_matrix(cells_x, coarse_x + 2, 0, -1)
     basis_y = basis_matrix(cells_y, coarse_y + 2, 0, -1)
     basis_z = basis_matrix(cells_z, coarse_z + 2, 0, -1)
-    partway = jnp.einsum("ijk,zk->ijz", window, basis_z, precision=highest)
-    partway = jnp.einsum("ijz,yj->iyz", partway, basis_y, precision=highest)
-    level_set = jnp.einsum("iyz,xi->xyz", partway, basis_x, precision=highest)
     bent = jnp.tanh(4.0 * level_set)
     porosity = 0.45 * (1.0 - bent)
     slope_phi = -1.8 * (1.0 - bent * bent)

time: 96.6 us -> 109 us (1.13)
  blocking collectives: 0 us -> 23 us
  starting transfers between devices: 39 us -> 22.8 us
  other arithmetic: 11.9 us -> 17.6 us
  waiting for transfers between devices: 18.2 us -> 13.3 us
  local copies, waits for them, and re-layouts: 22.3 us -> 26.8 us
    all_gather x0 -> x1, blocking collectives: none -> 23 us  [per_device(): gathered = lax.all_gather(coefficients, ('gx', 'gy', 'gz'))]
    ppermute x9 -> x6, starting transfers between devices: 27.4 us -> 15.1 us  [padded(): lax.ppermute(lax.slice_in_dim(block, block.shape[dim] - width, None, axis...]
    ppermute x9 -> x6, waiting for transfers between devices: 18.1 us -> 12.1 us  [padded(): lax.ppermute(lax.slice_in_dim(block, 0, width, axis=dim), axis, backward)]
    ppermute x9 -> x6, starting transfers between devices: 11.6 us -> 7.73 us  [padded(): lax.ppermute(lax.slice_in_dim(block, 0, width, axis=dim), axis, backward)]
    unnamed x4, other arithmetic: 1.56 us -> 4.3 us
    unnamed x47 -> x55, local copies, waits for them, and re-layouts: 7.38 us -> 8.92 us
    convert_element_type x1, other arithmetic: 0.35 us -> 1.67 us  [per_device(): forward = forward_pops.astype(jnp.float32)]
    ppermute x9 -> x6, waiting for transfers between devices: 0.02 us -> 1.17 us  [padded(): lax.ppermute(lax.slice_in_dim(block, block.shape[dim] - width, None, axis...]
  transfers between devices with their start and end apart: 18 -> 12, of which waited for: 5 -> 4; matrix products, arithmetic and copies ran while one was open for 14% -> 17% of each run, Pallas kernels for 0% -> 0%
where the time goes in v4:
time: 109 us; the launch traced here: 107 us
  local copies, waits for them, and re-layouts  26.8 us (25%)
  blocking collectives  23 us (21%)
  starting transfers between devices  22.8 us (21%)
  other arithmetic  17.6 us (16%)
  waiting for transfers between devices  13.3 us (12%)
  matrix products  2.53 us (2%)
  between operations  1.24 us (1%)
    all_gather x1, blocking collectives, per_device(): gathered = lax.all_gather(coefficients, ('gx', 'gy', 'gz'))  23 us
    ppermute x6, starting transfers between devices, padded(): lax.ppermute(lax.slice_in_dim(block, block.shape[dim] - width, None, axis...  15.1 us
    ppermute x6, waiting for transfers between devices, padded(): lax.ppermute(lax.slice_in_dim(block, 0, width, axis=dim), axis, backward)  12.1 us
    unnamed x55, local copies, waits for them, and re-layouts  8.92 us
    ppermute x6, starting transfers between devices, padded(): lax.ppermute(lax.slice_in_dim(block, 0, width, axis=dim), axis, backward)  7.73 us
    slice x6, local copies, waits for them, and re-layouts, padded(): lax.slice_in_dim(block, block.shape[dim] - width, None, axis=dim)  4.41 us
    unnamed x4, other arithmetic  4.3 us
    slice x6, local copies, waits for them, and re-layouts, per_device(): lane_list = [adjoint_pops[component] for component in range(19)]  2.94 us
  transfers between devices with their start and end apart: 12, of which 4 were waited for; matrix products, arithmetic and copies ran while one was open for 17% of the time, Pallas kernels for 0%

profile of v4, /device:TPU:0, one launch (start us, length us, event | category | flops | bytes accessed | tf_op | source)
XLA Modules:
  0.0 107.3 jit_solution(4096841538462601859)
XLA Ops:
  0.6 1.9 %fusion.481 = (bf16[2,32,8,128]{3,2,1,0:T(8,128)(2,1)}, bf16[2,32,8,128]{3,2,1,0:T(8,128)(2,1)}, bf16[2,32,8,128]{3,2,1,0:T(8,128)(2,1)S(1)}) fusion(bf16[19,32,8,128]{3,2,1,0:T(8,128)(2,1)} %param.5), kind=kLoop, calls=%fused_computation.777 | loop fusion | bytes 786432 | tf_op jit(solution)/shard_map/slice | solution.py:154
  2.5 1.1 %slice.361 = bf16[8,32,8,128]{3,2,1,0:T(8,128)(2,1)S(1)} slice(bf16[19,32,8,128]{3,2,1,0:T(8,128)(2,1)} %param.5), slice={[7:15], [0:32], [0:8], [0:128]} | slice | bytes 1048576 | tf_op jit(solution)/shard_map/slice | solution.py:154
  3.6 0.1 copy_dynamic-update-slice_fusion
  3.8 0.7 fusion.484
  4.5 5.6 %collective-permute-start.1 = (bf16[10,1,8,128]{3,1,2,0:T(2,128)(2,1)}, bf16[10,1,8,128]{3,1,2,0:T(2,128)(2,1)}, u32[]{:S(2)}, u32[]{:S(2)}) collective-permute-start(bf16[10,1,8,128]{3,1,2,0:T(2,128)(2,1)} %get-tuple-element.120), channel_id=1, source_target_pairs={{0,4},{4,8},{8,12},{1,5},{5,9},{9,13},{2,6},{6,10},{10,14},{3,7},{... | collective-permute-start | bytes 61448 | tf_op jit(solution)/shard_map/ppermute | solution.py:39
  10.0 1.3 %collective-permute-start = (bf16[10,1,8,128]{3,1,2,0:T(2,128)(2,1)}, bf16[10,1,8,128]{3,1,2,0:T(2,128)(2,1)}, u32[]{:S(2)}, u32[]{:S(2)}) collective-permute-start(bf16[10,1,8,128]{3,1,2,0:T(2,128)(2,1)} %get-tuple-element.121), channel_id=1, source_target_pairs={{4,0},{8,4},{12,8},{5,1},{9,5},{13,9},{6,2},{10,6},{14,10},{7,3},{... | collective-permute-start | bytes 61448 | tf_op jit(solution)/shard_map/ppermute | solution.py:42
  11.4 0.6 add_multiply_fusion.4
  12.0 1.7 %copy_convert_fusion = f32[19,32,8,128]{3,1,2,0:T(8,128)S(1)} fusion(bf16[19,32,8,128]{3,2,1,0:T(8,128)(2,1)} %param.4), kind=kLoop, calls=%fused_computation.35 | loop fusion | flops 622592 | bytes 3735552 | tf_op jit(solution)/shard_map/convert_element_type | solution.py:162
  13.8 0.5 iota_multiply_fusion.2
  14.3 0.7 broadcast_compare_fusion.2
  15.0 23.0 %all-gather = f32[128,2,32]{2,1,0:T(2,128)S(1)} all-gather(f32[8,2,32]{2,1,0:T(2,128)S(1)} %copy-done.8), channel_id=2, replica_groups=mesh['parts'=2,'gx'=4,'gy'=2,'gz'=2] {'gx','gy','gz'}, dimensions={0}, use_global_device_ids=true | all-gather | bytes 34816 | tf_op jit(solution)/shard_map/all_gather | solution.py:133
  38.0 0.1 reshape.173
  38.2 0.6 constant_dynamic-update-slice_fusion.30
  38.8 1.0 copy_dynamic-update-slice_fusion.2
  39.9 0.3 convolution_bitcast_fusion.1
  40.2 1.0 convolution_bitcast_fusion
  41.2 0.8 copy.31
  42.0 0.8 copy.32
  42.7 0.8 copy.44
  43.5 0.8 constant_dynamic-update-slice_fusion.11
  44.3 0.7 constant_dynamic-update-slice_fusion.10
  45.0 1.4 %constant_dynamic-update-slice_fusion.9 = (bf16[10,32,8,128]{3,1,2,0:T(8,128)(2,1)S(1)}, bf16[10,32,8,128]{3,1,2,0:T(8,128)(2,1)S(1)}, bf16[19,32,8,128]{3,1,2,0:T(8,128)(2,1)}) fusion(bf16[10,32,8,128]{3,1,2,0:T(8,128)(2,1)S(1)} %get-tuple-element.112, bf16[10,1,8,128]{3,1,2,0:T(2,128)(2,1)} %collective-permute-done, ...), kind=kLoop, calls=%fused_computation.545 | loop fusion | flops 393216 | bytes 892928
  46.5 1.4 %constant_dynamic-update-slice_fusion.8 = (bf16[10,32,8,128]{3,1,2,0:T(8,128)(2,1)S(1)}, bf16[10,32,8,128]{3,1,2,0:T(8,128)(2,1)S(1)}, bf16[19,32,8,128]{3,1,2,0:T(8,128)(2,1)}) fusion(bf16[10,32,8,128]{3,1,2,0:T(8,128)(2,1)S(1)} %get-tuple-element.109, bf16[10,32,8,128]{3,1,2,0:T(8,128)(2,1)S(1)} %copy_dynamic-update-slice_fusion, ...), kind=kLoop, calls=%fused_computation.544 | loop fusion | flops 393216 | bytes 892928
  47.9 1.3 %collective-permute-start.2 = (bf16[10,32,1,128]{3,1,2,0:T(8,128)(2,1)S(1)}, bf16[10,32,1,128]{3,1,2,0:T(8,128)(2,1)S(1)}, u32[]{:S(2)}, u32[]{:S(2)}) collective-permute-start(bf16[10,32,1,128]{3,1,2,0:T(8,128)(2,1)S(1)} %get-tuple-element.118), channel_id=1, source_target_pairs={{0,2},{1,3},{4,6},{5,7},{8,10},{9,11},{12,14},{13,15},{16,18},{17,... | collective-permute-start | bytes 245768 | tf_op jit(solution)/shard_map/ppermute | solution.py:39
  49.2 1.3 %collective-permute-start.3 = (bf16[10,32,1,128]{3,1,2,0:T(8,128)(2,1)S(1)}, bf16[10,32,1,128]{3,1,2,0:T(8,128)(2,1)S(1)}, u32[]{:S(2)}, u32[]{:S(2)}) collective-permute-start(bf16[10,32,1,128]{3,1,2,0:T(8,128)(2,1)S(1)} %get-tuple-element.119), channel_id=1, source_target_pairs={{2,0},{3,1},{6,4},{7,5},{10,8},{11,9},{14,12},{15,13},{18,16},{19,... | collective-permute-start | bytes 245768 | tf_op jit(solution)/shard_map/ppermute | solution.py:42
  50.6 1.2 %collective-permute-done.2 = bf16[10,32,1,128]{3,1,2,0:T(8,128)(2,1)S(1)} collective-permute-done((bf16[10,32,1,128]{3,1,2,0:T(8,128)(2,1)S(1)}, bf16[10,32,1,128]{3,1,2,0:T(8,128)(2,1)S(1)}, u32[]{:S(2)}, u32[]{:S(2)}) %collective-permute-start.2) | collective-permute-done | bytes 81952 | tf_op jit(solution)/shard_map/ppermute | solution.py:39
  51.7 4.1 %collective-permute-done.3 = bf16[10,32,1,128]{3,1,2,0:T(8,128)(2,1)S(1)} collective-permute-done((bf16[10,32,1,128]{3,1,2,0:T(8,128)(2,1)S(1)}, bf16[10,32,1,128]{3,1,2,0:T(8,128)(2,1)S(1)}, u32[]{:S(2)}, u32[]{:S(2)}) %collective-permute-start.3) | collective-permute-done | bytes 81952 | tf_op jit(solution)/shard_map/ppermute | solution.py:42
  55.9 0.8 slice_bitcast_fusion.31
  56.8 0.8 copy-done
  57.6 1.3 %fusion.482 = (bf16[10,32,8,1]{3,1,2,0:T(8,128)(2,1)}, bf16[10,32,8,1]{3,1,2,0:T(8,128)(2,1)}) fusion(bf16[10,32,8,128]{3,1,2,0:T(8,128)(2,1)S(1)} %constant_dynamic-update-slice_fusion.4), kind=kLoop, calls=%fused_computation.778 | loop fusion | bytes 20480 | tf_op jit(solution)/shard_map/slice | solution.py:40
  58.9 2.3 %copy.39 = bf16[10,32,8,1]{1,2,3,0:T(8,128)(2,1)} copy(bf16[10,32,8,1]{3,1,2,0:T(8,128)(2,1)} %get-tuple-element.116) | data formatting | bytes 10240 | tf_op jit(solution)/shard_map/slice | solution.py:40
  61.2 2.2 %copy.40 = bf16[10,32,8,1]{1,2,3,0:T(8,128)(2,1)} copy(bf16[10,32,8,1]{3,1,2,0:T(8,128)(2,1)} %get-tuple-element.117) | data formatting | bytes 10240 | tf_op jit(solution)/shard_map/slice | solution.py:42
  63.4 1.3 %collective-permute-start.5 = (bf16[10,32,8,1]{1,2,3,0:T(8,128)(2,1)}, bf16[10,32,8,1]{1,2,3,0:T(8,128)(2,1)}, u32[]{:S(2)}, u32[]{:S(2)}) collective-permute-start(bf16[10,32,8,1]{1,2,3,0:T(8,128)(2,1)} %copy.40), channel_id=1, source_target_pairs={{1,0},{3,2},{5,4},{7,6},{9,8},{11,10},{13,12},{15,14},{17,16},{19,... | collective-permute-start | bytes 15368 | tf_op jit(solution)/shard_map/ppermute | solution.py:42
  64.7 4.2 %collective-permute-start.4 = (bf16[10,32,8,1]{1,2,3,0:T(8,128)(2,1)}, bf16[10,32,8,1]{1,2,3,0:T(8,128)(2,1)}, u32[]{:S(2)}, u32[]{:S(2)}) collective-permute-start(bf16[10,32,8,1]{1,2,3,0:T(8,128)(2,1)} %copy.39), channel_id=1, source_target_pairs={{0,1},{2,3},{4,5},{6,7},{8,9},{10,11},{12,13},{14,15},{16,17},{18,... | collective-permute-start | bytes 15368 | tf_op jit(solution)/shard_map/ppermute | solution.py:39
  68.9 1.5 %constant_dynamic-update-slice_fusion.27 = bf16[19,32,8,128]{3,1,2,0:T(8,128)(2,1)} fusion(bf16[19,32,8,128]{3,1,2,0:T(8,128)(2,1)} %get-tuple-element.108, bf16[32,10,128]{2,0,1:T(8,128)(2,1)} %get-tuple-element.105), kind=kLoop, calls=%fused_computation.563 | loop fusion | bytes 131072
  70.4 1.5 %constant_dynamic-update-slice_fusion.26 = bf16[19,32,8,128]{3,1,2,0:T(8,128)(2,1)} fusion(bf16[19,32,8,128]{3,1,2,0:T(8,128)(2,1)} %constant_dynamic-update-slice_fusion.27, bf16[32,10,128]{2,0,1:T(8,128)(2,1)} %get-tuple-element.104), kind=kLoop, calls=%fused_computation.562 | loop fusion | bytes 131072
  71.9 2.1 %copy.41 = bf16[10,32,8,1]{3,1,2,0:T(8,128)(2,1)} copy(bf16[10,32,8,1]{1,2,3,0:T(8,128)(2,1)} %collective-permute-done.4) | data formatting | bytes 10240 | tf_op jit(solution)/shard_map/ppermute | solution.py:39
  74.0 2.1 %copy.42 = bf16[10,32,8,1]{3,1,2,0:T(8,128)(2,1)} copy(bf16[10,32,8,1]{1,2,3,0:T(8,128)(2,1)} %collective-permute-done.5) | data formatting | bytes 10240 | tf_op jit(solution)/shard_map/ppermute | solution.py:42
  76.2 2.1 %pad_maximum_fusion = bf16[10,32,8,130]{3,1,2,0:T(8,128)(2,1)S(1)} fusion(bf16[10,32,8,1]{3,1,2,0:T(8,128)(2,1)} %copy.42, bf16[10,32,8,128]{3,1,2,0:T(8,128)(2,1)S(1)} %copy-done.1, bf16[10,32,8,1]{3,1,2,0:T(8,128)(2,1)} %copy.41), kind=kLoop, calls=%fused_computation.34 | loop fusion | flops 1996800 | bytes 1331200 | tf_op jit(solution)/shard_map/concatenate | solution.py:43
  78.3 0.1 slice_bitcast_fusion.21
  78.4 0.1 constant_dynamic-update-slice_fusion.25
  79.2 1.1 fusion.1
  80.3 0.3 bitcast_add_fusion.11
  80.6 0.6 copy-done.7
  81.2 0.5 bitcast_add_fusion.17
  81.7 0.2 fusion.34
  81.8 0.7 fusion.60
  82.5 0.7 bitcast_add_fusion.16
  83.2 2.8 %negate_add_fusion = (f32[32,8,128]{2,0,1:T(8,128)S(1)}, f32[32,8,128]{2,0,1:T(8,128)S(1)}, f32[32,8,128]{2,0,1:T(8,128)S(1)}, f32[32,8,128]{2,0,1:T(8,128)S(1)}...) fusion(f32[32,8,128]{2,0,1:T(8,128)S(1)} %get-tuple-element.17, ...), kind=kLoop, calls=%fused_computation.457 | loop fusion | flops 17006592 | bytes 12320768 | tf_op jit(solution)/shard_map/transpose(jvp())/add_any | solution.py:72
  86.0 0.3 fusion.274
  86.3 0.2 convolution_bitcast_fusion.2
  86.5 0.2 fusion.310
  86.8 1.3 %collective-permute-start.6 = (f32[1,4,34]{2,0,1:T(1,128)S(1)}, f32[1,4,34]{2,0,1:T(1,128)S(1)}, u32[]{:S(2)}, u32[]{:S(2)}) collective-permute-start(f32[1,4,34]{2,0,1:T(1,128)S(1)} %get-tuple-element.143), channel_id=1, source_target_pairs={{0,4},{4,8},{8,12},{1,5},{5,9},{9,13},{2,6},{6,10},{10,14},{3,7},{... | collective-permute-start | bytes 1640 | tf_op jit(solution)/shard_map/ppermute | solution.py:39
  88.1 1.3 %collective-permute-start.7 = (f32[1,4,34]{2,0,1:T(1,128)S(1)}, f32[1,4,34]{2,0,1:T(1,128)S(1)}, u32[]{:S(2)}, u32[]{:S(2)}) collective-permute-start(f32[1,4,34]{2,0,1:T(1,128)S(1)} %get-tuple-element.144), channel_id=1, source_target_pairs={{4,0},{8,4},{12,8},{5,1},{9,5},{13,9},{6,2},{10,6},{14,10},{7,3},{... | collective-permute-start | bytes 1640 | tf_op jit(solution)/shard_map/ppermute | solution.py:42
  89.4 0.3 fusion.480
  89.7 3.9 %collective-permute-done.7 = f32[1,4,34]{2,0,1:T(1,128)S(1)} collective-permute-done((f32[1,4,34]{2,0,1:T(1,128)S(1)}, f32[1,4,34]{2,0,1:T(1,128)S(1)}, u32[]{:S(2)}, u32[]{:S(2)}) %collective-permute-start.7) | collective-permute-done | bytes 576 | tf_op jit(solution)/shard_map/ppermute | solution.py:42
  93.6 1.5 %collective-permute-start.8 = (f32[12,1,34]{2,0,1:T(8,128)S(1)}, f32[12,1,34]{2,0,1:T(8,128)S(1)}, u32[]{:S(2)}, u32[]{:S(2)}) collective-permute-start(f32[12,1,34]{2,0,1:T(8,128)S(1)} %get-tuple-element.141), channel_id=1, source_target_pairs={{0,2},{1,3},{4,6},{5,7},{8,10},{9,11},{12,14},{13,15},{16,18},{17,... | collective-permute-start | bytes 4904 | tf_op jit(solution)/shard_map/ppermute | solution.py:39
  95.0 1.3 %collective-permute-start.9 = (f32[12,1,34]{2,0,1:T(8,128)S(1)}, f32[12,1,34]{2,0,1:T(8,128)S(1)}, u32[]{:S(2)}, u32[]{:S(2)}) collective-permute-start(f32[12,1,34]{2,0,1:T(8,128)S(1)} %get-tuple-element.142), channel_id=1, source_target_pairs={{2,0},{3,1},{6,4},{7,5},{10,8},{11,9},{14,12},{15,13},{18,16},{19,... | collective-permute-start | bytes 4904 | tf_op jit(solution)/shard_map/ppermute | solution.py:42
  96.5 4.1 %collective-permute-done.9 = f32[12,1,34]{2,0,1:T(8,128)S(1)} collective-permute-done((f32[12,1,34]{2,0,1:T(8,128)S(1)}, f32[12,1,34]{2,0,1:T(8,128)S(1)}, u32[]{:S(2)}, u32[]{:S(2)}) %collective-permute-start.9) | collective-permute-done | bytes 1664 | tf_op jit(solution)/shard_map/ppermute | solution.py:42
  100.7 1.3 %collective-permute-start.10 = (f32[12,6,1]{2,0,1:T(8,128)S(1)}, f32[12,6,1]{2,0,1:T(8,128)S(1)}, u32[]{:S(2)}, u32[]{:S(2)}) collective-permute-start(f32[12,6,1]{2,0,1:T(8,128)S(1)} %get-tuple-element.139), channel_id=1, source_target_pairs={{0,1},{2,3},{4,5},{6,7},{8,9},{10,11},{12,13},{14,15},{16,17},{18,... | collective-permute-start | bytes 872 | tf_op jit(solution)/shard_map/ppermute | solution.py:39
  102.0 1.3 %collective-permute-start.11 = (f32[12,6,1]{2,0,1:T(8,128)S(1)}, f32[12,6,1]{2,0,1:T(8,128)S(1)}, u32[]{:S(2)}, u32[]{:S(2)}) collective-permute-start(f32[12,6,1]{2,0,1:T(8,128)S(1)} %get-tuple-element.140), channel_id=1, source_target_pairs={{1,0},{3,2},{5,4},{7,6},{9,8},{11,10},{13,12},{15,14},{17,16},{19,... | collective-permute-start | bytes 872 | tf_op jit(solution)/shard_map/ppermute | solution.py:42
  103.3 1.3 %add_convert_fusion = bf16[19,32,8,128]{3,1,2,0:T(8,128)(2,1)S(1)} fusion(f32[1,32,8,128]{3,1,2,0:T(8,128)S(1)} %get-tuple-element.132, f32[1,32,8,128]{3,1,2,0:T(8,128)S(1)} %get-tuple-element.133, bf16[19,32,8,128]{3,1,2,0:T(8,128)(2,1)S(1)} %constant_dynamic-update-slice_fusion.12, f32[1,32,8,128]{3,1,2,0:T(8,128)S(1)} %get-tuple-element.134, ...), kind=kLoop, calls=%fused_computation.33 | loop fusion | flops 36732928 | bytes 5832723 | tf_op jit(solution)/shard_map/convert_element_type | solution.py:169
  104.6 1.6 %copy.50 = bf16[19,32,8,128]{3,2,1,0:T(8,128)(2,1)} copy(bf16[19,32,8,128]{3,1,2,0:T(8,128)(2,1)S(1)} %add_convert_fusion) | data formatting | bytes 2490368
  106.7 0.6 copy.51
  (82 shorter events, 1.8 us)
Async XLA Ops:
  0.6 11.3 %copy-start.3 = (bf16[19,32,8,128]{3,2,1,0:T(8,128)(2,1)S(1)}, bf16[19,32,8,128]{3,2,1,0:T(8,128)(2,1)}, u32[]{:S(2)}) copy-start(bf16[19,32,8,128]{3,2,1,0:T(8,128)(2,1)} %param.4) | copy-start | bytes 3735556
  4.5 39.8 %collective-permute-start.1 = (bf16[10,1,8,128]{3,1,2,0:T(2,128)(2,1)}, bf16[10,1,8,128]{3,1,2,0:T(2,128)(2,1)}, u32[]{:S(2)}, u32[]{:S(2)}) collective-permute-start(bf16[10,1,8,128]{3,1,2,0:T(2,128)(2,1)} %get-tuple-element.120), channel_id=1, source_target_pairs={{0,4},{4,8},{8,12},{1,5},{5,9},{9,13},{2,6},{6,10},{10,14},{3,7},{... | collective-permute-start | bytes 61448 | tf_op jit(solution)/shard_map/ppermute | solution.py:39
  10.0 33.5 %collective-permute-start = (bf16[10,1,8,128]{3,1,2,0:T(2,128)(2,1)}, bf16[10,1,8,128]{3,1,2,0:T(2,128)(2,1)}, u32[]{:S(2)}, u32[]{:S(2)}) collective-permute-start(bf16[10,1,8,128]{3,1,2,0:T(2,128)(2,1)} %get-tuple-element.121), channel_id=1, source_target_pairs={{4,0},{8,4},{12,8},{5,1},{9,5},{13,9},{6,2},{10,6},{14,10},{7,3},{... | collective-permute-start | bytes 61448 | tf_op jit(solution)/shard_map/ppermute | solution.py:42
  11.9 2.4 %copy-start.6 = (s32[32,8,128]{2,1,0:T(8,128)S(1)}, s32[32,8,128]{2,1,0:T(8,128)}, u32[]{:S(2)}) copy-start(s32[32,8,128]{2,1,0:T(8,128)} %param.7) | copy-start | bytes 393220
  11.9 3.0 %copy-start.8 = (f32[8,2,32]{2,1,0:T(2,128)S(1)}, f32[8,2,32]{2,1,0:T(2,128)}, u32[]{:S(2)}) copy-start(f32[8,2,32]{2,1,0:T(2,128)} %param.6) | copy-start | bytes 6148
  12.0 26.1 %slice-start = ((bf16[19,32,8,128]{3,2,1,0:T(8,128)(2,1)}), bf16[1,32,8,128]{3,2,1,0:T(8,128)(2,1)S(1)}, s32[]{:S(2)}) async-start(bf16[19,32,8,128]{3,2,1,0:T(8,128)(2,1)} %param.5), calls=%async_computation | async-start | bytes 131072 | tf_op jit(solution)/shard_map/slice | solution.py:154
  38.8 9.0 %slice-start.1 = ((bf16[19,32,8,128]{3,2,1,0:T(8,128)(2,1)}), bf16[4,32,8,128]{3,2,1,0:T(8,128)(2,1)S(1)}, s32[]{:S(2)}) async-start(bf16[19,32,8,128]{3,2,1,0:T(8,128)(2,1)} %param.5), calls=%async_computation.1 | async-start | bytes 524288 | tf_op jit(solution)/shard_map/slice | solution.py:154
  47.9 3.8 %collective-permute-start.2 = (bf16[10,32,1,128]{3,1,2,0:T(8,128)(2,1)S(1)}, bf16[10,32,1,128]{3,1,2,0:T(8,128)(2,1)S(1)}, u32[]{:S(2)}, u32[]{:S(2)}) collective-permute-start(bf16[10,32,1,128]{3,1,2,0:T(8,128)(2,1)S(1)} %get-tuple-element.118), channel_id=1, source_target_pairs={{0,2},{1,3},{4,6},{5,7},{8,10},{9,11},{12,14},{13,15},{16,18},{17,... | collective-permute-start | bytes 245768 | tf_op jit(solution)/shard_map/ppermute | solution.py:39
  49.2 6.6 %collective-permute-start.3 = (bf16[10,32,1,128]{3,1,2,0:T(8,128)(2,1)S(1)}, bf16[10,32,1,128]{3,1,2,0:T(8,128)(2,1)S(1)}, u32[]{:S(2)}, u32[]{:S(2)}) collective-permute-start(bf16[10,32,1,128]{3,1,2,0:T(8,128)(2,1)S(1)} %get-tuple-element.119), channel_id=1, source_target_pairs={{2,0},{3,1},{6,4},{7,5},{10,8},{11,9},{14,12},{15,13},{18,16},{19,... | collective-permute-start | bytes 245768 | tf_op jit(solution)/shard_map/ppermute | solution.py:42
  56.8 0.9 copy-start
  58.9 17.2 %copy-start.1 = (bf16[10,32,8,128]{3,1,2,0:T(8,128)(2,1)S(1)}, bf16[10,32,8,128]{3,1,2,0:T(8,128)(2,1)}, u32[]{:S(2)}) copy-start(bf16[10,32,8,128]{3,1,2,0:T(8,128)(2,1)} %copy-done) | copy-start | bytes 1966084
  63.4 10.6 %collective-permute-start.5 = (bf16[10,32,8,1]{1,2,3,0:T(8,128)(2,1)}, bf16[10,32,8,1]{1,2,3,0:T(8,128)(2,1)}, u32[]{:S(2)}, u32[]{:S(2)}) collective-permute-start(bf16[10,32,8,1]{1,2,3,0:T(8,128)(2,1)} %copy.40), channel_id=1, source_target_pairs={{1,0},{3,2},{5,4},{7,6},{9,8},{11,10},{13,12},{15,14},{17,16},{19,... | collective-permute-start | bytes 15368 | tf_op jit(solution)/shard_map/ppermute | solution.py:42
  64.7 7.2 %collective-permute-start.4 = (bf16[10,32,8,1]{1,2,3,0:T(8,128)(2,1)}, bf16[10,32,8,1]{1,2,3,0:T(8,128)(2,1)}, u32[]{:S(2)}, u32[]{:S(2)}) collective-permute-start(bf16[10,32,8,1]{1,2,3,0:T(8,128)(2,1)} %copy.39), channel_id=1, source_target_pairs={{0,1},{2,3},{4,5},{6,7},{8,9},{10,11},{12,13},{14,15},{16,17},{18,... | collective-permute-start | bytes 15368 | tf_op jit(solution)/shard_map/ppermute | solution.py:39
  76.2 2.3 %copy-start.2 = (bf16[19,32,8,128]{3,1,2,0:T(8,128)(2,1)S(1)}, bf16[19,32,8,128]{3,1,2,0:T(8,128)(2,1)}, u32[]{:S(2)}) copy-start(bf16[19,32,8,128]{3,1,2,0:T(8,128)(2,1)} %constant_dynamic-update-slice_fusion.26) | copy-start | bytes 3735556
  76.2 2.4 %copy-start.5 = (bf16[32,10,128]{2,0,1:T(8,128)(2,1)S(1)}, bf16[32,10,128]{2,0,1:T(8,128)(2,1)}, u32[]{:S(2)}) copy-start(bf16[32,10,128]{2,0,1:T(8,128)(2,1)} %get-tuple-element.99) | copy-start | bytes 245764
  76.2 2.4 %copy-start.4 = (bf16[32,10,128]{2,0,1:T(8,128)(2,1)S(1)}, bf16[32,10,128]{2,0,1:T(8,128)(2,1)}, u32[]{:S(2)}) copy-start(bf16[32,10,128]{2,0,1:T(8,128)(2,1)} %get-tuple-element.98) | copy-start | bytes 245764
  80.3 0.9 copy-start.7
  80.3 0.9 copy-start.14
  80.3 0.9 copy-start.15
  83.2 3.1 %copy-start.13 = (f32[4]{0:T(128)S(1)}, f32[4]{0:T(128)}, u32[]{:S(2)}) copy-start(f32[4]{0:T(128)} %add_multiply_fusion.4) | copy-start | bytes 52
  86.8 2.9 %collective-permute-start.6 = (f32[1,4,34]{2,0,1:T(1,128)S(1)}, f32[1,4,34]{2,0,1:T(1,128)S(1)}, u32[]{:S(2)}, u32[]{:S(2)}) collective-permute-start(f32[1,4,34]{2,0,1:T(1,128)S(1)} %get-tuple-element.143), channel_id=1, source_target_pairs={{0,4},{4,8},{8,12},{1,5},{5,9},{9,13},{2,6},{6,10},{10,14},{3,7},{... | collective-permute-start | bytes 1640 | tf_op jit(solution)/shard_map/ppermute | solution.py:39
  88.1 5.5 %collective-permute-start.7 = (f32[1,4,34]{2,0,1:T(1,128)S(1)}, f32[1,4,34]{2,0,1:T(1,128)S(1)}, u32[]{:S(2)}, u32[]{:S(2)}) collective-permute-start(f32[1,4,34]{2,0,1:T(1,128)S(1)} %get-tuple-element.144), channel_id=1, source_target_pairs={{4,0},{8,4},{12,8},{5,1},{9,5},{13,9},{6,2},{10,6},{14,10},{7,3},{... | collective-permute-start | bytes 1640 | tf_op jit(solution)/shard_map/ppermute | solution.py:42
  89.4 13.9 %copy-start.12 = (pred[19]{0:T(512)(128)(4,1)S(1)}, pred[19]{0:T(512)(128)(4,1)}, u32[]{:S(2)}) copy-start(pred[19]{0:T(512)(128)(4,1)} %constant.54.clone.1) | copy-start | bytes 61
  93.6 2.9 %collective-permute-start.8 = (f32[12,1,34]{2,0,1:T(8,128)S(1)}, f32[12,1,34]{2,0,1:T(8,128)S(1)}, u32[]{:S(2)}, u32[]{:S(2)}) collective-permute-start(f32[12,1,34]{2,0,1:T(8,128)S(1)} %get-tuple-element.141), channel_id=1, source_target_pairs={{0,2},{1,3},{4,6},{5,7},{8,10},{9,11},{12,14},{13,15},{16,18},{17,... | collective-permute-start | bytes 4904 | tf_op jit(solution)/shard_map/ppermute | solution.py:39
  95.0 5.5 %collective-permute-start.9 = (f32[12,1,34]{2,0,1:T(8,128)S(1)}, f32[12,1,34]{2,0,1:T(8,128)S(1)}, u32[]{:S(2)}, u32[]{:S(2)}) collective-permute-start(f32[12,1,34]{2,0,1:T(8,128)S(1)} %get-tuple-element.142), channel_id=1, source_target_pairs={{2,0},{3,1},{6,4},{7,5},{10,8},{11,9},{14,12},{15,13},{18,16},{19,... | collective-permute-start | bytes 4904 | tf_op jit(solution)/shard_map/ppermute | solution.py:42
  100.7 5.5 %collective-permute-start.10 = (f32[12,6,1]{2,0,1:T(8,128)S(1)}, f32[12,6,1]{2,0,1:T(8,128)S(1)}, u32[]{:S(2)}, u32[]{:S(2)}) collective-permute-start(f32[12,6,1]{2,0,1:T(8,128)S(1)} %get-tuple-element.139), channel_id=1, source_target_pairs={{0,1},{2,3},{4,5},{6,7},{8,9},{10,11},{12,13},{14,15},{16,17},{18,... | collective-permute-start | bytes 872 | tf_op jit(solution)/shard_map/ppermute | solution.py:39
  102.0 4.2 %collective-permute-start.11 = (f32[12,6,1]{2,0,1:T(8,128)S(1)}, f32[12,6,1]{2,0,1:T(8,128)S(1)}, u32[]{:S(2)}, u32[]{:S(2)}) collective-permute-start(f32[12,6,1]{2,0,1:T(8,128)S(1)} %get-tuple-element.140), channel_id=1, source_target_pairs={{1,0},{3,2},{5,4},{7,6},{9,8},{11,10},{13,12},{15,14},{17,16},{19,... | collective-permute-start | bytes 872 | tf_op jit(solution)/shard_map/ppermute | solution.py:42
  104.6 1.7 %copy-start.11 = (pred[8]{0:T(512)(128)(4,1)S(1)}, pred[8]{0:T(512)(128)(4,1)}, u32[]{:S(2)}) copy-start(pred[8]{0:T(512)(128)(4,1)} %constant.131.clone.1) | copy-start | bytes 28
  104.6 1.8 %copy-start.10 = (pred[2]{0:T(512)(128)(4,1)S(1)}, pred[2]{0:T(512)(128)(4,1)}, u32[]{:S(2)}) copy-start(pred[2]{0:T(512)(128)(4,1)} %constant.132.clone.1) | copy-start | bytes 10
  104.6 2.0 %copy-start.9 = (pred[32]{0:T(512)(128)(4,1)S(1)}, pred[32]{0:T(512)(128)(4,1)}, u32[]{:S(2)}) copy-start(pred[32]{0:T(512)(128)(4,1)} %constant.133.clone.1) | copy-start | bytes 100

commit v5 on v0

--- a/solution.py
+++ b/solution.py
@@ -129,7 +129,15 @@
 def per_device(forward_pops, adjoint_pops, coefficients, node_kind):
     cells_x, cells_y, cells_z = node_kind.shape
     coarse_x, coarse_y, coarse_z = coefficients.shape
-    window = padded(coefficients, (("gx", 0), ("gy", 1), ("gz", 2)), 1)
+    lane_list = [adjoint_pops[component] for component in range(19)]
+    window = coefficients
+    for dimension, axis in ((0, "gx"), (1, "gy"), (2, "gz")):
+        stacked = jnp.stack([lane_list[component] for component in moving(dimension)])
+        window, stacked = lax.optimization_barrier((window, stacked))
+        window = padded(window, ((axis, dimension),), 1)
+        extended = padded(stacked, ((axis, dimension + 1),), 1)
+        window, extended = lax.optimization_barrier((window, extended))
+        lane_list = pull_along(lane_list, dimension, extended)
     basis_x = basis_matrix(cells_x, coarse_x + 2, 0, -1)
     basis_y = basis_matrix(cells_y, coarse_y + 2, 0, -1)
     basis_z = basis_matrix(cells_z, coarse_z + 2, 0, -1)
@@ -139,13 +147,6 @@
     bent = jnp.tanh(4.0 * level_set)
     porosity = 0.45 * (1.0 - bent)
     slope_phi = -1.8 * (1.0 - bent * bent)
-    lane_list = [adjoint_pops[component] for component in range(19)]
-    extended = padded(jnp.stack([lane_list[component] for component in moving(0)]), (("gx", 1),), 1)
-    lane_list = pull_along(lane_list, 0, extended)
-    extended = padded(jnp.stack([lane_list[component] for component in moving(1)]), (("gy", 2),), 1)
-    lane_list = pull_along(lane_list, 1, extended)
-    extended = padded(jnp.stack([lane_list[component] for component in moving(2)]), (("gz", 3),), 1)
-    lane_list = pull_along(lane_list, 2, extended)
     pulled = jnp.stack(lane_list).astype(jnp.float32)
     forward = forward_pops.astype(jnp.float32)
 

time: 96.6 us -> 97.1 us (level)
  waiting for transfers between devices: 18.2 us -> 14.7 us
  starting transfers between devices: 39 us -> 41.5 us
  local copies, waits for them, and re-layouts: 22.3 us -> 24.3 us
    ppermute x9, waiting for transfers between devices: 18.1 us -> 14 us  [padded(): lax.ppermute(lax.slice_in_dim(block, 0, width, axis=dim), axis, backward)]
    ppermute x9, starting transfers between devices: 27.4 us -> 29.9 us  [padded(): lax.ppermute(lax.slice_in_dim(block, block.shape[dim] - width, None, axis...]
    unnamed x47 -> x54, local copies, waits for them, and re-layouts: 7.38 us -> 9.07 us
    unnamed x4 -> x0, other arithmetic: 1.56 us -> none
    concatenate x6 -> x8, other arithmetic: 2.48 us -> 3.63 us  [padded(): block = jnp.concatenate([low, block, high], axis=dim)]
    slice x2 -> x1, local copies, waits for them, and re-layouts: 3.02 us -> 2.23 us  [padded(): lax.slice_in_dim(block, 0, width, axis=dim)]
    slice x8 -> x9, local copies, waits for them, and re-layouts: 3.82 us -> 4.43 us  [padded(): lax.slice_in_dim(block, block.shape[dim] - width, None, axis=dim)]
  transfers between devices with their start and end apart: 18 -> 18, of which waited for: 5 -> 5; matrix products, arithmetic and copies ran while one was open for 14% -> 18% of each run, Pallas kernels for 0% -> 0%
where the time goes in v5:
time: 97.1 us; the launch traced here: 95.6 us
  starting transfers between devices  41.5 us (43%)
  local copies, waits for them, and re-layouts  24.3 us (25%)
  waiting for transfers between devices  14.7 us (15%)
  other arithmetic  12 us (12%)
  matrix products  1.72 us (2%)
  between operations  1.36 us (1%)
    ppermute x9, starting transfers between devices, padded(): lax.ppermute(lax.slice_in_dim(block, block.shape[dim] - width, None, axis...  29.9 us
    ppermute x9, waiting for transfers between devices, padded(): lax.ppermute(lax.slice_in_dim(block, 0, width, axis=dim), axis, backward)  14 us
    ppermute x9, starting transfers between devices, padded(): lax.ppermute(lax.slice_in_dim(block, 0, width, axis=dim), axis, backward)  11.6 us
    unnamed x54, local copies, waits for them, and re-layouts  9.07 us
    slice x9, local copies, waits for them, and re-layouts, padded(): lax.slice_in_dim(block, block.shape[dim] - width, None, axis=dim)  4.43 us
    concatenate x8, other arithmetic, padded(): block = jnp.concatenate([low, block, high], axis=dim)  3.63 us
    add_any x1, other arithmetic, collide(): flow_x = moment(populations, 0) / density  2.81 us
    slice x6, local copies, waits for them, and re-layouts, per_device(): lane_list = [adjoint_pops[component] for component in range(19)]  2.25 us
  transfers between devices with their start and end apart: 18, of which 5 were waited for; matrix products, arithmetic and copies ran while one was open for 18% of the time, Pallas kernels for 0%

profile of v5, /device:TPU:0, one launch (start us, length us, event | category | flops | bytes accessed | tf_op | source)
XLA Modules:
  0.0 95.6 jit_solution(7636363554438586659)
XLA Ops:
  0.6 1.2 %fusion.388 = (bf16[2,32,8,128]{3,2,1,0:T(8,128)(2,1)S(1)}, bf16[2,32,8,128]{3,2,1,0:T(8,128)(2,1)S(1)}, bf16[2,32,8,128]{3,2,1,0:T(8,128)(2,1)S(1)}) fusion(bf16[19,32,8,128]{3,2,1,0:T(8,128)(2,1)} %param.5), kind=kLoop, calls=%fused_computation.687 | loop fusion | bytes 786432 | tf_op jit(solution)/shard_map/slice | solution.py:132
  1.8 1.1 %slice.369 = bf16[8,32,8,128]{3,2,1,0:T(8,128)(2,1)S(1)} slice(bf16[19,32,8,128]{3,2,1,0:T(8,128)(2,1)} %param.5), slice={[7:15], [0:32], [0:8], [0:128]} | slice | bytes 1048576 | tf_op jit(solution)/shard_map/slice | solution.py:132
  3.1 5.0 %collective-permute-start = (f32[1,2,32]{2,1,0:T(2,128)S(1)}, f32[1,2,32]{2,1,0:T(2,128)S(1)}, u32[]{:S(2)}, u32[]{:S(2)}) collective-permute-start(f32[1,2,32]{2,1,0:T(2,128)S(1)} %get-tuple-element.171), channel_id=1, source_target_pairs={{0,4},{4,8},{8,12},{1,5},{5,9},{9,13},{2,6},{6,10},{10,14},{3,7},{... | collective-permute-start | bytes 776 | tf_op jit(solution)/shard_map/ppermute | solution.py:39
  8.1 1.3 %collective-permute-start.1 = (f32[1,2,32]{2,1,0:T(2,128)S(1)}, f32[1,2,32]{2,1,0:T(2,128)S(1)}, u32[]{:S(2)}, u32[]{:S(2)}) collective-permute-start(f32[1,2,32]{2,1,0:T(2,128)S(1)} %get-tuple-element.172), channel_id=1, source_target_pairs={{4,0},{8,4},{12,8},{5,1},{9,5},{13,9},{6,2},{10,6},{14,10},{7,3},{... | collective-permute-start | bytes 776 | tf_op jit(solution)/shard_map/ppermute | solution.py:42
  9.5 4.5 %collective-permute-start.2 = (bf16[10,1,8,128]{3,1,2,0:T(2,128)(2,1)S(1)}, bf16[10,1,8,128]{3,1,2,0:T(2,128)(2,1)S(1)}, u32[]{:S(2)}, u32[]{:S(2)}) collective-permute-start(bf16[10,1,8,128]{3,1,2,0:T(2,128)(2,1)S(1)} %get-tuple-element.142), channel_id=1, source_target_pairs={{0,4},{4,8},{8,12},{1,5},{5,9},{9,13},{2,6},{6,10},{10,14},{3,7},{... | collective-permute-start | bytes 61448 | tf_op jit(solution)/shard_map/ppermute | solution.py:39
  14.0 1.3 %collective-permute-start.3 = (bf16[10,1,8,128]{3,1,2,0:T(2,128)(2,1)S(1)}, bf16[10,1,8,128]{3,1,2,0:T(2,128)(2,1)S(1)}, u32[]{:S(2)}, u32[]{:S(2)}) collective-permute-start(bf16[10,1,8,128]{3,1,2,0:T(2,128)(2,1)S(1)} %get-tuple-element.143), channel_id=1, source_target_pairs={{4,0},{8,4},{12,8},{5,1},{9,5},{13,9},{6,2},{10,6},{14,10},{7,3},{... | collective-permute-start | bytes 61448 | tf_op jit(solution)/shard_map/ppermute | solution.py:42
  15.3 0.5 add_multiply_fusion.2
  15.9 0.3 copy_convert_fusion
  16.3 0.5 copy-done.5
  16.8 0.6 constant_dynamic-update-slice_fusion.30
  17.6 0.6 copy.31
  18.2 1.7 %collective-permute-done.3 = bf16[10,1,8,128]{3,1,2,0:T(2,128)(2,1)S(1)} collective-permute-done((bf16[10,1,8,128]{3,1,2,0:T(2,128)(2,1)S(1)}, bf16[10,1,8,128]{3,1,2,0:T(2,128)(2,1)S(1)}, u32[]{:S(2)}, u32[]{:S(2)}) %collective-permute-start.3) | collective-permute-done | bytes 20512 | tf_op jit(solution)/shard_map/ppermute | solution.py:42
  19.9 0.4 pad_maximum_fusion.1
  20.4 0.7 constant_dynamic-update-slice_fusion.9
  21.1 0.6 constant_dynamic-update-slice_fusion.8
  21.9 3.4 %collective-permute-start.4 = (f32[10,1,32]{2,1,0:T(1,128)S(1)}, f32[10,1,32]{2,1,0:T(1,128)S(1)}, u32[]{:S(2)}, u32[]{:S(2)}) collective-permute-start(f32[10,1,32]{2,1,0:T(1,128)S(1)} %get-tuple-element.169), channel_id=1, source_target_pairs={{0,2},{1,3},{4,6},{5,7},{8,10},{9,11},{12,14},{13,15},{16,18},{17,... | collective-permute-start | bytes 3848 | tf_op jit(solution)/shard_map/ppermute | solution.py:39
  25.3 1.3 %collective-permute-start.5 = (f32[10,1,32]{2,1,0:T(1,128)S(1)}, f32[10,1,32]{2,1,0:T(1,128)S(1)}, u32[]{:S(2)}, u32[]{:S(2)}) collective-permute-start(f32[10,1,32]{2,1,0:T(1,128)S(1)} %get-tuple-element.170), channel_id=1, source_target_pairs={{2,0},{3,1},{6,4},{7,5},{10,8},{11,9},{14,12},{15,13},{18,16},{19,... | collective-permute-start | bytes 3848 | tf_op jit(solution)/shard_map/ppermute | solution.py:42
  26.6 4.5 %collective-permute-start.6 = (bf16[10,32,1,128]{3,1,2,0:T(8,128)(2,1)S(1)}, bf16[10,32,1,128]{3,1,2,0:T(8,128)(2,1)S(1)}, u32[]{:S(2)}, u32[]{:S(2)}) collective-permute-start(bf16[10,32,1,128]{3,1,2,0:T(8,128)(2,1)S(1)} %get-tuple-element.140), channel_id=1, source_target_pairs={{0,2},{1,3},{4,6},{5,7},{8,10},{9,11},{12,14},{13,15},{16,18},{17,... | collective-permute-start | bytes 245768 | tf_op jit(solution)/shard_map/ppermute | solution.py:39
  31.1 1.3 %collective-permute-start.7 = (bf16[10,32,1,128]{3,1,2,0:T(8,128)(2,1)S(1)}, bf16[10,32,1,128]{3,1,2,0:T(8,128)(2,1)S(1)}, u32[]{:S(2)}, u32[]{:S(2)}) collective-permute-start(bf16[10,32,1,128]{3,1,2,0:T(8,128)(2,1)S(1)} %get-tuple-element.141), channel_id=1, source_target_pairs={{2,0},{3,1},{6,4},{7,5},{10,8},{11,9},{14,12},{15,13},{18,16},{19,... | collective-permute-start | bytes 245768 | tf_op jit(solution)/shard_map/ppermute | solution.py:42
  32.5 0.7 collective-permute-done.6
  33.2 4.3 %collective-permute-done.7 = bf16[10,32,1,128]{3,1,2,0:T(8,128)(2,1)S(1)} collective-permute-done((bf16[10,32,1,128]{3,1,2,0:T(8,128)(2,1)S(1)}, bf16[10,32,1,128]{3,1,2,0:T(8,128)(2,1)S(1)}, u32[]{:S(2)}, u32[]{:S(2)}) %collective-permute-start.7) | collective-permute-done | bytes 81952 | tf_op jit(solution)/shard_map/ppermute | solution.py:42
  37.6 0.8 slice_bitcast_fusion.31
  38.4 0.7 fusion.394
  39.1 1.3 %collective-permute-start.8 = (f32[10,4,1]{2,1,0:T(4,128)}, f32[10,4,1]{2,1,0:T(4,128)S(1)}, u32[]{:S(2)}, u32[]{:S(2)}) collective-permute-start(f32[10,4,1]{2,1,0:T(4,128)} %get-tuple-element.167), channel_id=1, source_target_pairs={{0,1},{2,3},{4,5},{6,7},{8,9},{10,11},{12,13},{14,15},{16,17},{18,... | collective-permute-start | bytes 488 | tf_op jit(solution)/shard_map/ppermute | solution.py:39
  40.4 1.3 %collective-permute-start.9 = (f32[10,4,1]{2,1,0:T(4,128)}, f32[10,4,1]{2,1,0:T(4,128)}, u32[]{:S(2)}, u32[]{:S(2)}) collective-permute-start(f32[10,4,1]{2,1,0:T(4,128)} %get-tuple-element.168), channel_id=1, source_target_pairs={{1,0},{3,2},{5,4},{7,6},{9,8},{11,10},{13,12},{15,14},{17,16},{19,... | collective-permute-start | bytes 488 | tf_op jit(solution)/shard_map/ppermute | solution.py:42
  41.7 1.3 %fusion.389 = (bf16[10,32,8,1]{3,1,2,0:T(8,128)(2,1)}, bf16[10,32,8,1]{3,1,2,0:T(8,128)(2,1)}) fusion(bf16[10,32,8,128]{3,1,2,0:T(8,128)(2,1)S(1)} %constant_dynamic-update-slice_fusion.4), kind=kLoop, calls=%fused_computation.688 | loop fusion | bytes 20480 | tf_op jit(solution)/shard_map/slice | solution.py:40
  43.0 2.2 %copy.26 = bf16[10,32,8,1]{1,2,3,0:T(8,128)(2,1)} copy(bf16[10,32,8,1]{3,1,2,0:T(8,128)(2,1)} %get-tuple-element.138) | data formatting | bytes 10240 | tf_op jit(solution)/shard_map/slice | solution.py:40
  45.2 2.2 %copy.27 = bf16[10,32,8,1]{1,2,3,0:T(8,128)(2,1)} copy(bf16[10,32,8,1]{3,1,2,0:T(8,128)(2,1)} %get-tuple-element.139) | data formatting | bytes 10240 | tf_op jit(solution)/shard_map/slice | solution.py:42
  47.5 1.3 %collective-permute-start.11 = (bf16[10,32,8,1]{1,2,3,0:T(8,128)(2,1)}, bf16[10,32,8,1]{1,2,3,0:T(8,128)(2,1)}, u32[]{:S(2)}, u32[]{:S(2)}) collective-permute-start(bf16[10,32,8,1]{1,2,3,0:T(8,128)(2,1)} %copy.27), channel_id=1, source_target_pairs={{1,0},{3,2},{5,4},{7,6},{9,8},{11,10},{13,12},{15,14},{17,16},{19,... | collective-permute-start | bytes 15368 | tf_op jit(solution)/shard_map/ppermute | solution.py:42
  48.7 4.8 %collective-permute-start.10 = (bf16[10,32,8,1]{1,2,3,0:T(8,128)(2,1)}, bf16[10,32,8,1]{1,2,3,0:T(8,128)(2,1)}, u32[]{:S(2)}, u32[]{:S(2)}) collective-permute-start(bf16[10,32,8,1]{1,2,3,0:T(8,128)(2,1)} %copy.26), channel_id=1, source_target_pairs={{0,1},{2,3},{4,5},{6,7},{8,9},{10,11},{12,13},{14,15},{16,17},{18,... | collective-permute-start | bytes 15368 | tf_op jit(solution)/shard_map/ppermute | solution.py:39
  53.6 1.5 %constant_dynamic-update-slice_fusion.27 = bf16[19,32,8,128]{3,1,2,0:T(8,128)(2,1)} fusion(bf16[19,32,8,128]{3,1,2,0:T(8,128)(2,1)} %get-tuple-element.130, bf16[32,10,128]{2,0,1:T(8,128)(2,1)} %get-tuple-element.127), kind=kLoop, calls=%fused_computation.558 | loop fusion | bytes 131072
  55.0 1.5 %constant_dynamic-update-slice_fusion.26 = bf16[19,32,8,128]{3,1,2,0:T(8,128)(2,1)} fusion(bf16[19,32,8,128]{3,1,2,0:T(8,128)(2,1)} %constant_dynamic-update-slice_fusion.27, bf16[32,10,128]{2,0,1:T(8,128)(2,1)} %get-tuple-element.126), kind=kLoop, calls=%fused_computation.557 | loop fusion | bytes 131072
  56.5 0.6 copy-done.6
  57.1 0.8 pad_maximum_fusion.7
  58.0 2.1 %copy.28 = bf16[10,32,8,1]{3,1,2,0:T(8,128)(2,1)} copy(bf16[10,32,8,1]{1,2,3,0:T(8,128)(2,1)} %collective-permute-done.10) | data formatting | bytes 10240 | tf_op jit(solution)/shard_map/ppermute | solution.py:39
  60.1 2.1 %copy.29 = bf16[10,32,8,1]{3,1,2,0:T(8,128)(2,1)} copy(bf16[10,32,8,1]{1,2,3,0:T(8,128)(2,1)} %collective-permute-done.11) | data formatting | bytes 10240 | tf_op jit(solution)/shard_map/ppermute | solution.py:42
  62.2 2.1 %pad_maximum_fusion = bf16[10,32,8,130]{3,1,2,0:T(8,128)(2,1)S(1)} fusion(bf16[10,32,8,1]{3,1,2,0:T(8,128)(2,1)} %copy.29, bf16[10,32,8,128]{3,1,2,0:T(8,128)(2,1)S(1)} %constant_dynamic-update-slice_fusion.4, bf16[10,32,8,1]{3,1,2,0:T(8,128)(2,1)} %copy.28), kind=kLoop, calls=%fused_computation.34 | loop fusion | flops 1996800 | bytes 1331200 | tf_op jit(solution)/shard_map/concatenate | solution.py:43
  64.4 0.1 slice_bitcast_fusion.21
  64.7 0.1 constant_dynamic-update-slice_fusion.19
  64.9 0.1 constant_dynamic-update-slice_fusion.16
  65.3 0.2 fusion.313
  65.5 0.2 fusion.328
  65.7 1.1 %fusion.1 = (f32[19,32,8,128]{3,1,2,0:T(8,128)S(1)}, f32[19,32,8,128]{3,1,2,0:T(8,128)S(1)}, f32[19,32,8,128]{3,1,2,0:T(8,128)S(1)}) fusion(bf16[19,32,8,128]{3,1,2,0:T(8,128)(2,1)S(1)} %constant_dynamic-update-slice_fusion.12, pred[32,8,128]{2,0,1:T(8,128)(4,1)S(1)} %copy.19, pred[32,8,128]{2,0,1:T(8,128)(4,1)S(1)} %copy.18, pred[32,8,128]{2,0,1:T(8,128)(4,1)S(1)} %copy-done.4), kind=kLoop, calls=%fused_computation.3 | loop fusion | flops 5603328 | bytes 8814592 | tf_op jit(solution)/shard_map/transpose(jvp(jit(_where)))/select_n | solution.py:89
  66.8 0.3 bitcast_add_fusion.11
  67.1 0.5 bitcast_add_fusion.17
  67.7 0.2 fusion.34
  67.8 0.7 fusion.60
  68.5 0.7 bitcast_add_fusion.16
  69.2 2.8 %negate_add_fusion = (f32[32,8,128]{2,0,1:T(8,128)S(1)}, f32[32,8,128]{2,0,1:T(8,128)S(1)}, f32[32,8,128]{2,0,1:T(8,128)S(1)}, f32[32,8,128]{2,0,1:T(8,128)S(1)}...) fusion(f32[32,8,128]{2,0,1:T(8,128)S(1)} %get-tuple-element.39, ...), kind=kLoop, calls=%fused_computation.442 | loop fusion | flops 17006592 | bytes 12320768 | tf_op jit(solution)/shard_map/transpose(jvp())/add_any | solution.py:72
  72.0 0.3 fusion.273
  72.3 0.2 fusion.308
  72.5 0.2 fusion.310
  72.8 3.5 %collective-permute-start.12 = (f32[1,4,34]{2,0,1:T(1,128)S(1)}, f32[1,4,34]{2,0,1:T(1,128)S(1)}, u32[]{:S(2)}, u32[]{:S(2)}) collective-permute-start(f32[1,4,34]{2,0,1:T(1,128)S(1)} %get-tuple-element.165), channel_id=1, source_target_pairs={{0,4},{4,8},{8,12},{1,5},{5,9},{9,13},{2,6},{6,10},{10,14},{3,7},{... | collective-permute-start | bytes 1640 | tf_op jit(solution)/shard_map/ppermute | solution.py:39
  76.3 1.3 %collective-permute-start.13 = (f32[1,4,34]{2,0,1:T(1,128)S(1)}, f32[1,4,34]{2,0,1:T(1,128)S(1)}, u32[]{:S(2)}, u32[]{:S(2)}) collective-permute-start(f32[1,4,34]{2,0,1:T(1,128)S(1)} %get-tuple-element.166), channel_id=1, source_target_pairs={{4,0},{8,4},{12,8},{5,1},{9,5},{13,9},{6,2},{10,6},{14,10},{7,3},{... | collective-permute-start | bytes 1640 | tf_op jit(solution)/shard_map/ppermute | solution.py:42
  77.6 0.3 fusion.387
  77.9 3.9 %collective-permute-done.13 = f32[1,4,34]{2,0,1:T(1,128)S(1)} collective-permute-done((f32[1,4,34]{2,0,1:T(1,128)S(1)}, f32[1,4,34]{2,0,1:T(1,128)S(1)}, u32[]{:S(2)}, u32[]{:S(2)}) %collective-permute-start.13) | collective-permute-done | bytes 576 | tf_op jit(solution)/shard_map/ppermute | solution.py:42
  81.8 1.5 %collective-permute-start.14 = (f32[12,1,34]{2,0,1:T(8,128)S(1)}, f32[12,1,34]{2,0,1:T(8,128)S(1)}, u32[]{:S(2)}, u32[]{:S(2)}) collective-permute-start(f32[12,1,34]{2,0,1:T(8,128)S(1)} %get-tuple-element.163), channel_id=1, source_target_pairs={{0,2},{1,3},{4,6},{5,7},{8,10},{9,11},{12,14},{13,15},{16,18},{17,... | collective-permute-start | bytes 4904 | tf_op jit(solution)/shard_map/ppermute | solution.py:39
  83.3 1.3 %collective-permute-start.15 = (f32[12,1,34]{2,0,1:T(8,128)S(1)}, f32[12,1,34]{2,0,1:T(8,128)S(1)}, u32[]{:S(2)}, u32[]{:S(2)}) collective-permute-start(f32[12,1,34]{2,0,1:T(8,128)S(1)} %get-tuple-element.164), channel_id=1, source_target_pairs={{2,0},{3,1},{6,4},{7,5},{10,8},{11,9},{14,12},{15,13},{18,16},{19,... | collective-permute-start | bytes 4904 | tf_op jit(solution)/shard_map/ppermute | solution.py:42
  84.7 4.2 %collective-permute-done.15 = f32[12,1,34]{2,0,1:T(8,128)S(1)} collective-permute-done((f32[12,1,34]{2,0,1:T(8,128)S(1)}, f32[12,1,34]{2,0,1:T(8,128)S(1)}, u32[]{:S(2)}, u32[]{:S(2)}) %collective-permute-start.15) | collective-permute-done | bytes 1664 | tf_op jit(solution)/shard_map/ppermute | solution.py:42
  89.0 1.3 %collective-permute-start.16 = (f32[12,6,1]{2,0,1:T(8,128)S(1)}, f32[12,6,1]{2,0,1:T(8,128)S(1)}, u32[]{:S(2)}, u32[]{:S(2)}) collective-permute-start(f32[12,6,1]{2,0,1:T(8,128)S(1)} %get-tuple-element.161), channel_id=1, source_target_pairs={{0,1},{2,3},{4,5},{6,7},{8,9},{10,11},{12,13},{14,15},{16,17},{18,... | collective-permute-start | bytes 872 | tf_op jit(solution)/shard_map/ppermute | solution.py:39
  90.3 1.3 %collective-permute-start.17 = (f32[12,6,1]{2,0,1:T(8,128)S(1)}, f32[12,6,1]{2,0,1:T(8,128)S(1)}, u32[]{:S(2)}, u32[]{:S(2)}) collective-permute-start(f32[12,6,1]{2,0,1:T(8,128)S(1)} %get-tuple-element.162), channel_id=1, source_target_pairs={{1,0},{3,2},{5,4},{7,6},{9,8},{11,10},{13,12},{15,14},{17,16},{19,... | collective-permute-start | bytes 872 | tf_op jit(solution)/shard_map/ppermute | solution.py:42
  91.6 1.3 %add_convert_fusion = bf16[19,32,8,128]{3,1,2,0:T(8,128)(2,1)S(1)} fusion(f32[1,32,8,128]{3,1,2,0:T(8,128)S(1)} %get-tuple-element.154, f32[1,32,8,128]{3,1,2,0:T(8,128)S(1)} %get-tuple-element.155, bf16[19,32,8,128]{3,1,2,0:T(8,128)(2,1)S(1)} %constant_dynamic-update-slice_fusion.12, f32[1,32,8,128]{3,1,2,0:T(8,128)S(1)} %get-tuple-element.156, ...), kind=kLoop, calls=%fused_computation.33 | loop fusion | flops 36732928 | bytes 5832723 | tf_op jit(solution)/shard_map/convert_element_type | solution.py:158
  92.9 1.6 %copy.32 = bf16[19,32,8,128]{3,2,1,0:T(8,128)(2,1)} copy(bf16[19,32,8,128]{3,1,2,0:T(8,128)(2,1)S(1)} %add_convert_fusion) | data formatting | bytes 2490368
  95.0 0.6 copy.33
  (88 shorter events, 2.0 us)
Async XLA Ops:
  0.6 2.5 %copy-start.7 = (f32[8,2,32]{2,1,0:T(2,128)S(1)}, f32[8,2,32]{2,1,0:T(2,128)}, u32[]{:S(2)}) copy-start(f32[8,2,32]{2,1,0:T(2,128)} %param.6) | copy-start | bytes 6148
  0.6 15.2 %copy-start.1 = (bf16[19,32,8,128]{3,2,1,0:T(8,128)(2,1)S(1)}, bf16[19,32,8,128]{3,2,1,0:T(8,128)(2,1)}, u32[]{:S(2)}) copy-start(bf16[19,32,8,128]{3,2,1,0:T(8,128)(2,1)} %param.4) | copy-start | bytes 3735556
  3.1 15.1 %collective-permute-start = (f32[1,2,32]{2,1,0:T(2,128)S(1)}, f32[1,2,32]{2,1,0:T(2,128)S(1)}, u32[]{:S(2)}, u32[]{:S(2)}) collective-permute-start(f32[1,2,32]{2,1,0:T(2,128)S(1)} %get-tuple-element.171), channel_id=1, source_target_pairs={{0,4},{4,8},{8,12},{1,5},{5,9},{9,13},{2,6},{6,10},{10,14},{3,7},{... | collective-permute-start | bytes 776 | tf_op jit(solution)/shard_map/ppermute | solution.py:39
  8.1 10.1 %collective-permute-start.1 = (f32[1,2,32]{2,1,0:T(2,128)S(1)}, f32[1,2,32]{2,1,0:T(2,128)S(1)}, u32[]{:S(2)}, u32[]{:S(2)}) collective-permute-start(f32[1,2,32]{2,1,0:T(2,128)S(1)} %get-tuple-element.172), channel_id=1, source_target_pairs={{4,0},{8,4},{12,8},{5,1},{9,5},{13,9},{6,2},{10,6},{14,10},{7,3},{... | collective-permute-start | bytes 776 | tf_op jit(solution)/shard_map/ppermute | solution.py:42
  9.5 8.8 %collective-permute-start.2 = (bf16[10,1,8,128]{3,1,2,0:T(2,128)(2,1)S(1)}, bf16[10,1,8,128]{3,1,2,0:T(2,128)(2,1)S(1)}, u32[]{:S(2)}, u32[]{:S(2)}) collective-permute-start(bf16[10,1,8,128]{3,1,2,0:T(2,128)(2,1)S(1)} %get-tuple-element.142), channel_id=1, source_target_pairs={{0,4},{4,8},{8,12},{1,5},{5,9},{9,13},{2,6},{6,10},{10,14},{3,7},{... | collective-permute-start | bytes 61448 | tf_op jit(solution)/shard_map/ppermute | solution.py:39
  14.0 5.9 %collective-permute-start.3 = (bf16[10,1,8,128]{3,1,2,0:T(2,128)(2,1)S(1)}, bf16[10,1,8,128]{3,1,2,0:T(2,128)(2,1)S(1)}, u32[]{:S(2)}, u32[]{:S(2)}) collective-permute-start(bf16[10,1,8,128]{3,1,2,0:T(2,128)(2,1)S(1)} %get-tuple-element.143), channel_id=1, source_target_pairs={{4,0},{8,4},{12,8},{5,1},{9,5},{13,9},{6,2},{10,6},{14,10},{7,3},{... | collective-permute-start | bytes 61448 | tf_op jit(solution)/shard_map/ppermute | solution.py:42
  15.9 0.9 copy-start.5
  15.9 1.0 %slice-start = ((bf16[19,32,8,128]{3,2,1,0:T(8,128)(2,1)}), bf16[1,32,8,128]{3,2,1,0:T(8,128)(2,1)S(1)}, s32[]{:S(2)}) async-start(bf16[19,32,8,128]{3,2,1,0:T(8,128)(2,1)} %param.5), calls=%async_computation | async-start | bytes 131072 | tf_op jit(solution)/shard_map/slice | solution.py:132
  16.8 5.0 %slice-start.1 = ((bf16[19,32,8,128]{3,2,1,0:T(8,128)(2,1)}), bf16[4,32,8,128]{3,2,1,0:T(8,128)(2,1)S(1)}, s32[]{:S(2)}) async-start(bf16[19,32,8,128]{3,2,1,0:T(8,128)(2,1)} %param.5), calls=%async_computation.1 | async-start | bytes 524288 | tf_op jit(solution)/shard_map/slice | solution.py:132
  21.9 10.6 %collective-permute-start.4 = (f32[10,1,32]{2,1,0:T(1,128)S(1)}, f32[10,1,32]{2,1,0:T(1,128)S(1)}, u32[]{:S(2)}, u32[]{:S(2)}) collective-permute-start(f32[10,1,32]{2,1,0:T(1,128)S(1)} %get-tuple-element.169), channel_id=1, source_target_pairs={{0,2},{1,3},{4,6},{5,7},{8,10},{9,11},{12,14},{13,15},{16,18},{17,... | collective-permute-start | bytes 3848 | tf_op jit(solution)/shard_map/ppermute | solution.py:39
  25.3 7.2 %collective-permute-start.5 = (f32[10,1,32]{2,1,0:T(1,128)S(1)}, f32[10,1,32]{2,1,0:T(1,128)S(1)}, u32[]{:S(2)}, u32[]{:S(2)}) collective-permute-start(f32[10,1,32]{2,1,0:T(1,128)S(1)} %get-tuple-element.170), channel_id=1, source_target_pairs={{2,0},{3,1},{6,4},{7,5},{10,8},{11,9},{14,12},{15,13},{18,16},{19,... | collective-permute-start | bytes 3848 | tf_op jit(solution)/shard_map/ppermute | solution.py:42
  26.6 6.6 %collective-permute-start.6 = (bf16[10,32,1,128]{3,1,2,0:T(8,128)(2,1)S(1)}, bf16[10,32,1,128]{3,1,2,0:T(8,128)(2,1)S(1)}, u32[]{:S(2)}, u32[]{:S(2)}) collective-permute-start(bf16[10,32,1,128]{3,1,2,0:T(8,128)(2,1)S(1)} %get-tuple-element.140), channel_id=1, source_target_pairs={{0,2},{1,3},{4,6},{5,7},{8,10},{9,11},{12,14},{13,15},{16,18},{17,... | collective-permute-start | bytes 245768 | tf_op jit(solution)/shard_map/ppermute | solution.py:39
  31.1 6.3 %collective-permute-start.7 = (bf16[10,32,1,128]{3,1,2,0:T(8,128)(2,1)S(1)}, bf16[10,32,1,128]{3,1,2,0:T(8,128)(2,1)S(1)}, u32[]{:S(2)}, u32[]{:S(2)}) collective-permute-start(bf16[10,32,1,128]{3,1,2,0:T(8,128)(2,1)S(1)} %get-tuple-element.141), channel_id=1, source_target_pairs={{2,0},{3,1},{6,4},{7,5},{10,8},{11,9},{14,12},{15,13},{18,16},{19,... | collective-permute-start | bytes 245768 | tf_op jit(solution)/shard_map/ppermute | solution.py:42
  39.1 17.4 %collective-permute-start.8 = (f32[10,4,1]{2,1,0:T(4,128)}, f32[10,4,1]{2,1,0:T(4,128)S(1)}, u32[]{:S(2)}, u32[]{:S(2)}) collective-permute-start(f32[10,4,1]{2,1,0:T(4,128)} %get-tuple-element.167), channel_id=1, source_target_pairs={{0,1},{2,3},{4,5},{6,7},{8,9},{10,11},{12,13},{14,15},{16,17},{18,... | collective-permute-start | bytes 488 | tf_op jit(solution)/shard_map/ppermute | solution.py:39
  40.4 16.7 %collective-permute-start.9 = (f32[10,4,1]{2,1,0:T(4,128)}, f32[10,4,1]{2,1,0:T(4,128)}, u32[]{:S(2)}, u32[]{:S(2)}) collective-permute-start(f32[10,4,1]{2,1,0:T(4,128)} %get-tuple-element.168), channel_id=1, source_target_pairs={{1,0},{3,2},{5,4},{7,6},{9,8},{11,10},{13,12},{15,14},{17,16},{19,... | collective-permute-start | bytes 488 | tf_op jit(solution)/shard_map/ppermute | solution.py:42
  47.5 12.6 %collective-permute-start.11 = (bf16[10,32,8,1]{1,2,3,0:T(8,128)(2,1)}, bf16[10,32,8,1]{1,2,3,0:T(8,128)(2,1)}, u32[]{:S(2)}, u32[]{:S(2)}) collective-permute-start(bf16[10,32,8,1]{1,2,3,0:T(8,128)(2,1)} %copy.27), channel_id=1, source_target_pairs={{1,0},{3,2},{5,4},{7,6},{9,8},{11,10},{13,12},{15,14},{17,16},{19,... | collective-permute-start | bytes 15368 | tf_op jit(solution)/shard_map/ppermute | solution.py:42
  48.7 9.2 %collective-permute-start.10 = (bf16[10,32,8,1]{1,2,3,0:T(8,128)(2,1)}, bf16[10,32,8,1]{1,2,3,0:T(8,128)(2,1)}, u32[]{:S(2)}, u32[]{:S(2)}) collective-permute-start(bf16[10,32,8,1]{1,2,3,0:T(8,128)(2,1)} %copy.26), channel_id=1, source_target_pairs={{0,1},{2,3},{4,5},{6,7},{8,9},{10,11},{12,13},{14,15},{16,17},{18,... | collective-permute-start | bytes 15368 | tf_op jit(solution)/shard_map/ppermute | solution.py:39
  56.5 0.6 copy-start.6
  62.2 2.3 %copy-start = (bf16[19,32,8,128]{3,1,2,0:T(8,128)(2,1)S(1)}, bf16[19,32,8,128]{3,1,2,0:T(8,128)(2,1)}, u32[]{:S(2)}) copy-start(bf16[19,32,8,128]{3,1,2,0:T(8,128)(2,1)} %constant_dynamic-update-slice_fusion.26) | copy-start | bytes 3735556
  62.2 2.4 %copy-start.3 = (bf16[32,10,128]{2,0,1:T(8,128)(2,1)S(1)}, bf16[32,10,128]{2,0,1:T(8,128)(2,1)}, u32[]{:S(2)}) copy-start(bf16[32,10,128]{2,0,1:T(8,128)(2,1)} %get-tuple-element.121) | copy-start | bytes 245764
  62.2 2.5 %copy-start.2 = (bf16[32,10,128]{2,0,1:T(8,128)(2,1)S(1)}, bf16[32,10,128]{2,0,1:T(8,128)(2,1)}, u32[]{:S(2)}) copy-start(bf16[32,10,128]{2,0,1:T(8,128)(2,1)} %get-tuple-element.120) | copy-start | bytes 245764
  64.3 0.9 copy-start.12
  64.4 1.3 %copy-start.4 = (pred[32,8,128]{2,0,1:T(8,128)(4,1)S(1)}, pred[32,8,128]{2,0,1:T(8,128)(4,1)}, u32[]{:S(2)}) copy-start(pred[32,8,128]{2,0,1:T(8,128)(4,1)} %copy.31) | copy-start | bytes 98308
  72.8 5.1 %collective-permute-start.12 = (f32[1,4,34]{2,0,1:T(1,128)S(1)}, f32[1,4,34]{2,0,1:T(1,128)S(1)}, u32[]{:S(2)}, u32[]{:S(2)}) collective-permute-start(f32[1,4,34]{2,0,1:T(1,128)S(1)} %get-tuple-element.165), channel_id=1, source_target_pairs={{0,4},{4,8},{8,12},{1,5},{5,9},{9,13},{2,6},{6,10},{10,14},{3,7},{... | collective-permute-start | bytes 1640 | tf_op jit(solution)/shard_map/ppermute | solution.py:39
  76.3 5.5 %collective-permute-start.13 = (f32[1,4,34]{2,0,1:T(1,128)S(1)}, f32[1,4,34]{2,0,1:T(1,128)S(1)}, u32[]{:S(2)}, u32[]{:S(2)}) collective-permute-start(f32[1,4,34]{2,0,1:T(1,128)S(1)} %get-tuple-element.166), channel_id=1, source_target_pairs={{4,0},{8,4},{12,8},{5,1},{9,5},{13,9},{6,2},{10,6},{14,10},{7,3},{... | collective-permute-start | bytes 1640 | tf_op jit(solution)/shard_map/ppermute | solution.py:42
  77.6 14.0 %copy-start.11 = (pred[19]{0:T(512)(128)(4,1)S(1)}, pred[19]{0:T(512)(128)(4,1)}, u32[]{:S(2)}) copy-start(pred[19]{0:T(512)(128)(4,1)} %constant.77.clone.1) | copy-start | bytes 61
  81.8 2.9 %collective-permute-start.14 = (f32[12,1,34]{2,0,1:T(8,128)S(1)}, f32[12,1,34]{2,0,1:T(8,128)S(1)}, u32[]{:S(2)}, u32[]{:S(2)}) collective-permute-start(f32[12,1,34]{2,0,1:T(8,128)S(1)} %get-tuple-element.163), channel_id=1, source_target_pairs={{0,2},{1,3},{4,6},{5,7},{8,10},{9,11},{12,14},{13,15},{16,18},{17,... | collective-permute-start | bytes 4904 | tf_op jit(solution)/shard_map/ppermute | solution.py:39
  83.3 5.5 %collective-permute-start.15 = (f32[12,1,34]{2,0,1:T(8,128)S(1)}, f32[12,1,34]{2,0,1:T(8,128)S(1)}, u32[]{:S(2)}, u32[]{:S(2)}) collective-permute-start(f32[12,1,34]{2,0,1:T(8,128)S(1)} %get-tuple-element.164), channel_id=1, source_target_pairs={{2,0},{3,1},{6,4},{7,5},{10,8},{11,9},{14,12},{15,13},{18,16},{19,... | collective-permute-start | bytes 4904 | tf_op jit(solution)/shard_map/ppermute | solution.py:42
  89.0 5.5 %collective-permute-start.16 = (f32[12,6,1]{2,0,1:T(8,128)S(1)}, f32[12,6,1]{2,0,1:T(8,128)S(1)}, u32[]{:S(2)}, u32[]{:S(2)}) collective-permute-start(f32[12,6,1]{2,0,1:T(8,128)S(1)} %get-tuple-element.161), channel_id=1, source_target_pairs={{0,1},{2,3},{4,5},{6,7},{8,9},{10,11},{12,13},{14,15},{16,17},{18,... | collective-permute-start | bytes 872 | tf_op jit(solution)/shard_map/ppermute | solution.py:39
  90.3 4.2 %collective-permute-start.17 = (f32[12,6,1]{2,0,1:T(8,128)S(1)}, f32[12,6,1]{2,0,1:T(8,128)S(1)}, u32[]{:S(2)}, u32[]{:S(2)}) collective-permute-start(f32[12,6,1]{2,0,1:T(8,128)S(1)} %get-tuple-element.162), channel_id=1, source_target_pairs={{1,0},{3,2},{5,4},{7,6},{9,8},{11,10},{13,12},{15,14},{17,16},{19,... | collective-permute-start | bytes 872 | tf_op jit(solution)/shard_map/ppermute | solution.py:42
  92.9 1.7 %copy-start.10 = (pred[8]{0:T(512)(128)(4,1)S(1)}, pred[8]{0:T(512)(128)(4,1)}, u32[]{:S(2)}) copy-start(pred[8]{0:T(512)(128)(4,1)} %constant.95.clone.1) | copy-start | bytes 28
  92.9 1.8 %copy-start.9 = (pred[2]{0:T(512)(128)(4,1)S(1)}, pred[2]{0:T(512)(128)(4,1)}, u32[]{:S(2)}) copy-start(pred[2]{0:T(512)(128)(4,1)} %constant.96.clone.1) | copy-start | bytes 10
  92.9 2.0 %copy-start.8 = (pred[32]{0:T(512)(128)(4,1)S(1)}, pred[32]{0:T(512)(128)(4,1)}, u32[]{:S(2)}) copy-start(pred[32]{0:T(512)(128)(4,1)} %constant.97.clone.1) | copy-start | bytes 100

commit v6 on v0

--- a/solution.py
+++ b/solution.py
@@ -159,7 +159,7 @@
     partial_value = jnp.einsum("xyz,xi->iyz", sensitivity, basis_x, precision=highest)
     partial_value = jnp.einsum("iyz,yj->ijz", partial_value, basis_y, precision=highest)
     partial_value = jnp.einsum("ijz,zk->ijk", partial_value, basis_z, precision=highest)
-    bordered = padded(partial_value, (("gx", 0), ("gy", 1), ("gz", 2)), 1)
+    bordered = padded(partial_value, (("gz", 2), ("gy", 1), ("gx", 0)), 1)
     gradient = fold_rim(fold_rim(fold_rim(bordered, 0), 1), 2)
     return (prior_adjoint, gradient)
 

time: 96.6 us -> 95 us (0.983)
    concatenate x6 -> x5, other arithmetic: 2.48 us -> 2.45 us  [padded(): block = jnp.concatenate([low, block, high], axis=dim)]
    unnamed x47 -> x45, local copies, waits for them, and re-layouts: 7.38 us -> 7.37 us
    slice x8 -> x7, local copies, waits for them, and re-layouts: 3.82 us -> 3.83 us  [padded(): lax.slice_in_dim(block, block.shape[dim] - width, None, axis=dim)]
  transfers between devices with their start and end apart: 18 -> 18, of which waited for: 5 -> 6; matrix products, arithmetic and copies ran while one was open for 14% -> 14% of each run, Pallas kernels for 0% -> 0%
where the time goes in v6:
time: 95 us; the launch traced here: 94.1 us
  starting transfers between devices  39 us (41%)
  local copies, waits for them, and re-layouts  22.2 us (23%)
  waiting for transfers between devices  17.3 us (18%)
  other arithmetic  11.9 us (13%)
  matrix products  2.34 us (2%)
  between operations  1.32 us (1%)
    ppermute x9, starting transfers between devices, padded(): lax.ppermute(lax.slice_in_dim(block, block.shape[dim] - width, None, axis...  27.4 us
    ppermute x9, waiting for transfers between devices, padded(): lax.ppermute(lax.slice_in_dim(block, 0, width, axis=dim), axis, backward)  17.3 us
    ppermute x9, starting transfers between devices, padded(): lax.ppermute(lax.slice_in_dim(block, 0, width, axis=dim), axis, backward)  11.6 us
    unnamed x45, local copies, waits for them, and re-layouts  7.37 us
    slice x7, local copies, waits for them, and re-layouts, padded(): lax.slice_in_dim(block, block.shape[dim] - width, None, axis=dim)  3.83 us
    slice x2, local copies, waits for them, and re-layouts, padded(): lax.slice_in_dim(block, 0, width, axis=dim)  3.03 us
    add_any x1, other arithmetic, collide(): flow_x = moment(populations, 0) / density  2.8 us
    concatenate x5, other arithmetic, padded(): block = jnp.concatenate([low, block, high], axis=dim)  2.45 us
  transfers between devices with their start and end apart: 18, of which 6 were waited for; matrix products, arithmetic and copies ran while one was open for 14% of the time, Pallas kernels for 0%

profile of v6, /device:TPU:0, one launch (start us, length us, event | category | flops | bytes accessed | tf_op | source)
XLA Modules:
  0.0 94.1 jit_solution(8648691938815212656)
XLA Ops:
  0.6 0.8 fusion.385
  1.4 1.3 %collective-permute-start.7 = (f32[1,2,32]{2,1,0:T(2,128)S(1)}, f32[1,2,32]{2,1,0:T(2,128)S(1)}, u32[]{:S(2)}, u32[]{:S(2)}) collective-permute-start(f32[1,2,32]{2,1,0:T(2,128)S(1)} %get-tuple-element.147), channel_id=1, source_target_pairs={{4,0},{8,4},{12,8},{5,1},{9,5},{13,9},{6,2},{10,6},{14,10},{7,3},{... | collective-permute-start | bytes 776 | tf_op jit(solution)/shard_map/ppermute | solution.py:42
  2.7 5.6 %collective-permute-start.6 = (f32[1,2,32]{2,1,0:T(2,128)S(1)}, f32[1,2,32]{2,1,0:T(2,128)S(1)}, u32[]{:S(2)}, u32[]{:S(2)}) collective-permute-start(f32[1,2,32]{2,1,0:T(2,128)S(1)} %get-tuple-element.148), channel_id=1, source_target_pairs={{0,4},{4,8},{8,12},{1,5},{5,9},{9,13},{2,6},{6,10},{10,14},{3,7},{... | collective-permute-start | bytes 776 | tf_op jit(solution)/shard_map/ppermute | solution.py:39
  8.3 1.1 %fusion.378 = (bf16[2,32,8,128]{3,2,1,0:T(8,128)(2,1)S(1)}, bf16[2,32,8,128]{3,2,1,0:T(8,128)(2,1)S(1)}, bf16[2,32,8,128]{3,2,1,0:T(8,128)(2,1)S(1)}) fusion(bf16[19,32,8,128]{3,2,1,0:T(8,128)(2,1)} %param.5), kind=kLoop, calls=%fused_computation.679 | loop fusion | bytes 786432 | tf_op jit(solution)/shard_map/slice | solution.py:142
  9.4 1.1 %slice.372 = bf16[8,32,8,128]{3,2,1,0:T(8,128)(2,1)S(1)} slice(bf16[19,32,8,128]{3,2,1,0:T(8,128)(2,1)} %param.5), slice={[7:15], [0:32], [0:8], [0:128]} | slice | bytes 1048576 | tf_op jit(solution)/shard_map/slice | solution.py:142
  10.5 0.1 copy_dynamic-update-slice_fusion
  10.7 3.9 %collective-permute-start.1 = (bf16[10,1,8,128]{3,1,2,0:T(2,128)(2,1)S(1)}, bf16[10,1,8,128]{3,1,2,0:T(2,128)(2,1)S(1)}, u32[]{:S(2)}, u32[]{:S(2)}) collective-permute-start(bf16[10,1,8,128]{3,1,2,0:T(2,128)(2,1)S(1)} %get-tuple-element.118), channel_id=1, source_target_pairs={{0,4},{4,8},{8,12},{1,5},{5,9},{9,13},{2,6},{6,10},{10,14},{3,7},{... | collective-permute-start | bytes 61448 | tf_op jit(solution)/shard_map/ppermute | solution.py:39
  14.7 1.3 %collective-permute-start = (bf16[10,1,8,128]{3,1,2,0:T(2,128)(2,1)S(1)}, bf16[10,1,8,128]{3,1,2,0:T(2,128)(2,1)S(1)}, u32[]{:S(2)}, u32[]{:S(2)}) collective-permute-start(bf16[10,1,8,128]{3,1,2,0:T(2,128)(2,1)S(1)} %get-tuple-element.119), channel_id=1, source_target_pairs={{4,0},{8,4},{12,8},{5,1},{9,5},{13,9},{6,2},{10,6},{14,10},{7,3},{... | collective-permute-start | bytes 61448 | tf_op jit(solution)/shard_map/ppermute | solution.py:42
  16.1 0.3 copy_convert_fusion
  16.5 0.4 copy-done.4
  17.0 0.6 constant_dynamic-update-slice_fusion.30
  17.7 3.4 %collective-permute-start.8 = (f32[10,1,32]{2,1,0:T(1,128)S(1)}, f32[10,1,32]{2,1,0:T(1,128)S(1)}, u32[]{:S(2)}, u32[]{:S(2)}) collective-permute-start(f32[10,1,32]{2,1,0:T(1,128)S(1)} %get-tuple-element.145), channel_id=1, source_target_pairs={{0,2},{1,3},{4,6},{5,7},{8,10},{9,11},{12,14},{13,15},{16,18},{17,... | collective-permute-start | bytes 3848 | tf_op jit(solution)/shard_map/ppermute | solution.py:39
  21.1 1.3 %collective-permute-start.9 = (f32[10,1,32]{2,1,0:T(1,128)S(1)}, f32[10,1,32]{2,1,0:T(1,128)S(1)}, u32[]{:S(2)}, u32[]{:S(2)}) collective-permute-start(f32[10,1,32]{2,1,0:T(1,128)S(1)} %get-tuple-element.146), channel_id=1, source_target_pairs={{2,0},{3,1},{6,4},{7,5},{10,8},{11,9},{14,12},{15,13},{18,16},{19,... | collective-permute-start | bytes 3848 | tf_op jit(solution)/shard_map/ppermute | solution.py:42
  22.5 4.1 %collective-permute-done.9 = f32[10,1,32]{2,1,0:T(1,128)S(1)} collective-permute-done((f32[10,1,32]{2,1,0:T(1,128)S(1)}, f32[10,1,32]{2,1,0:T(1,128)S(1)}, u32[]{:S(2)}, u32[]{:S(2)}) %collective-permute-start.9) | collective-permute-done | bytes 1312 | tf_op jit(solution)/shard_map/ppermute | solution.py:42
  26.8 1.3 %collective-permute-start.10 = (f32[10,4,1]{2,1,0:T(4,128)S(1)}, f32[10,4,1]{2,1,0:T(4,128)S(1)}, u32[]{:S(2)}, u32[]{:S(2)}) collective-permute-start(f32[10,4,1]{2,1,0:T(4,128)S(1)} %get-tuple-element.143), channel_id=1, source_target_pairs={{0,1},{2,3},{4,5},{6,7},{8,9},{10,11},{12,13},{14,15},{16,17},{18,... | collective-permute-start | bytes 488 | tf_op jit(solution)/shard_map/ppermute | solution.py:39
  28.1 1.3 %collective-permute-start.11 = (f32[10,4,1]{2,1,0:T(4,128)S(1)}, f32[10,4,1]{2,1,0:T(4,128)S(1)}, u32[]{:S(2)}, u32[]{:S(2)}) collective-permute-start(f32[10,4,1]{2,1,0:T(4,128)S(1)} %get-tuple-element.144), channel_id=1, source_target_pairs={{1,0},{3,2},{5,4},{7,6},{9,8},{11,10},{13,12},{15,14},{17,16},{19,... | collective-permute-start | bytes 488 | tf_op jit(solution)/shard_map/ppermute | solution.py:42
  29.4 1.7 %collective-permute-done.11 = f32[10,4,1]{2,1,0:T(4,128)S(1)} collective-permute-done((f32[10,4,1]{2,1,0:T(4,128)S(1)}, f32[10,4,1]{2,1,0:T(4,128)S(1)}, u32[]{:S(2)}, u32[]{:S(2)}) %collective-permute-start.11) | collective-permute-done | bytes 192 | tf_op jit(solution)/shard_map/ppermute | solution.py:42
  31.1 0.1 pad_maximum_fusion.6
  31.3 0.2 fusion.313
  31.7 0.7 constant_dynamic-update-slice_fusion.9
  32.4 0.7 constant_dynamic-update-slice_fusion.8
  33.2 1.7 %collective-permute-start.2 = (bf16[10,32,1,128]{3,1,2,0:T(8,128)(2,1)S(1)}, bf16[10,32,1,128]{3,1,2,0:T(8,128)(2,1)S(1)}, u32[]{:S(2)}, u32[]{:S(2)}) collective-permute-start(bf16[10,32,1,128]{3,1,2,0:T(8,128)(2,1)S(1)} %get-tuple-element.116), channel_id=1, source_target_pairs={{0,2},{1,3},{4,6},{5,7},{8,10},{9,11},{12,14},{13,15},{16,18},{17,... | collective-permute-start | bytes 245768 | tf_op jit(solution)/shard_map/ppermute | solution.py:39
  34.8 1.3 %collective-permute-start.3 = (bf16[10,32,1,128]{3,1,2,0:T(8,128)(2,1)S(1)}, bf16[10,32,1,128]{3,1,2,0:T(8,128)(2,1)S(1)}, u32[]{:S(2)}, u32[]{:S(2)}) collective-permute-start(bf16[10,32,1,128]{3,1,2,0:T(8,128)(2,1)S(1)} %get-tuple-element.117), channel_id=1, source_target_pairs={{2,0},{3,1},{6,4},{7,5},{10,8},{11,9},{14,12},{15,13},{18,16},{19,... | collective-permute-start | bytes 245768 | tf_op jit(solution)/shard_map/ppermute | solution.py:42
  36.1 0.8 fusion.318
  36.9 4.2 %collective-permute-done.3 = bf16[10,32,1,128]{3,1,2,0:T(8,128)(2,1)S(1)} collective-permute-done((bf16[10,32,1,128]{3,1,2,0:T(8,128)(2,1)S(1)}, bf16[10,32,1,128]{3,1,2,0:T(8,128)(2,1)S(1)}, u32[]{:S(2)}, u32[]{:S(2)}) %collective-permute-start.3) | collective-permute-done | bytes 81952 | tf_op jit(solution)/shard_map/ppermute | solution.py:42
  41.3 0.8 slice_bitcast_fusion.31
  42.1 1.4 %fusion.379 = (bf16[10,32,8,1]{3,1,2,0:T(8,128)(2,1)}, bf16[10,32,8,1]{3,1,2,0:T(8,128)(2,1)}) fusion(bf16[10,32,8,128]{3,1,2,0:T(8,128)(2,1)S(1)} %constant_dynamic-update-slice_fusion.4), kind=kLoop, calls=%fused_computation.680 | loop fusion | bytes 20480 | tf_op jit(solution)/shard_map/slice | solution.py:40
  43.5 2.2 %copy.26 = bf16[10,32,8,1]{1,2,3,0:T(8,128)(2,1)} copy(bf16[10,32,8,1]{3,1,2,0:T(8,128)(2,1)} %get-tuple-element.114) | data formatting | bytes 10240 | tf_op jit(solution)/shard_map/slice | solution.py:40
  45.7 2.2 %copy.27 = bf16[10,32,8,1]{1,2,3,0:T(8,128)(2,1)} copy(bf16[10,32,8,1]{3,1,2,0:T(8,128)(2,1)} %get-tuple-element.115) | data formatting | bytes 10240 | tf_op jit(solution)/shard_map/slice | solution.py:42
  47.9 1.3 %collective-permute-start.5 = (bf16[10,32,8,1]{1,2,3,0:T(8,128)(2,1)}, bf16[10,32,8,1]{1,2,3,0:T(8,128)(2,1)}, u32[]{:S(2)}, u32[]{:S(2)}) collective-permute-start(bf16[10,32,8,1]{1,2,3,0:T(8,128)(2,1)} %copy.27), channel_id=1, source_target_pairs={{1,0},{3,2},{5,4},{7,6},{9,8},{11,10},{13,12},{15,14},{17,16},{19,... | collective-permute-start | bytes 15368 | tf_op jit(solution)/shard_map/ppermute | solution.py:42
  49.2 4.2 %collective-permute-start.4 = (bf16[10,32,8,1]{1,2,3,0:T(8,128)(2,1)}, bf16[10,32,8,1]{1,2,3,0:T(8,128)(2,1)}, u32[]{:S(2)}, u32[]{:S(2)}) collective-permute-start(bf16[10,32,8,1]{1,2,3,0:T(8,128)(2,1)} %copy.26), channel_id=1, source_target_pairs={{0,1},{2,3},{4,5},{6,7},{8,9},{10,11},{12,13},{14,15},{16,17},{18,... | collective-permute-start | bytes 15368 | tf_op jit(solution)/shard_map/ppermute | solution.py:39
  53.4 1.5 %constant_dynamic-update-slice_fusion.27 = bf16[19,32,8,128]{3,1,2,0:T(8,128)(2,1)} fusion(bf16[19,32,8,128]{3,1,2,0:T(8,128)(2,1)} %get-tuple-element.106, bf16[32,10,128]{2,0,1:T(8,128)(2,1)} %get-tuple-element.103), kind=kLoop, calls=%fused_computation.548 | loop fusion | bytes 131072
  54.9 1.5 %constant_dynamic-update-slice_fusion.26 = bf16[19,32,8,128]{3,1,2,0:T(8,128)(2,1)} fusion(bf16[19,32,8,128]{3,1,2,0:T(8,128)(2,1)} %constant_dynamic-update-slice_fusion.27, bf16[32,10,128]{2,0,1:T(8,128)(2,1)} %get-tuple-element.102), kind=kLoop, calls=%fused_computation.547 | loop fusion | bytes 131072
  56.4 2.1 %copy.28 = bf16[10,32,8,1]{3,1,2,0:T(8,128)(2,1)} copy(bf16[10,32,8,1]{1,2,3,0:T(8,128)(2,1)} %collective-permute-done.4) | data formatting | bytes 10240 | tf_op jit(solution)/shard_map/ppermute | solution.py:39
  58.5 2.1 %copy.29 = bf16[10,32,8,1]{3,1,2,0:T(8,128)(2,1)} copy(bf16[10,32,8,1]{1,2,3,0:T(8,128)(2,1)} %collective-permute-done.5) | data formatting | bytes 10240 | tf_op jit(solution)/shard_map/ppermute | solution.py:42
  60.6 2.1 %pad_maximum_fusion = bf16[10,32,8,130]{3,1,2,0:T(8,128)(2,1)S(1)} fusion(bf16[10,32,8,1]{3,1,2,0:T(8,128)(2,1)} %copy.29, bf16[10,32,8,128]{3,1,2,0:T(8,128)(2,1)S(1)} %constant_dynamic-update-slice_fusion.4, bf16[10,32,8,1]{3,1,2,0:T(8,128)(2,1)} %copy.28), kind=kLoop, calls=%fused_computation.34 | loop fusion | flops 1996800 | bytes 1331200 | tf_op jit(solution)/shard_map/concatenate | solution.py:43
  62.8 0.1 slice_bitcast_fusion.21
  62.9 0.1 constant_dynamic-update-slice_fusion.25
  63.2 0.1 constant_dynamic-update-slice_fusion.19
  63.6 0.1 constant_dynamic-update-slice_fusion.12
  63.7 1.1 %fusion.1 = (f32[19,32,8,128]{3,1,2,0:T(8,128)S(1)}, f32[19,32,8,128]{3,1,2,0:T(8,128)S(1)}, f32[19,32,8,128]{3,1,2,0:T(8,128)S(1)}) fusion(bf16[19,32,8,128]{3,1,2,0:T(8,128)(2,1)S(1)} %constant_dynamic-update-slice_fusion.12, pred[32,8,128]{2,0,1:T(8,128)(4,1)S(1)} %copy.19, pred[32,8,128]{2,0,1:T(8,128)(4,1)S(1)} %copy.18, pred[32,8,128]{2,0,1:T(8,128)(4,1)S(1)} %copy.31), kind=kLoop, calls=%fused_computation.3 | loop fusion | flops 5603328 | bytes 8814592 | tf_op jit(solution)/shard_map/transpose(jvp(jit(_where)))/select_n | solution.py:89
  64.8 0.3 bitcast_add_fusion.11
  65.1 0.4 copy-done.5
  65.5 0.5 bitcast_add_fusion.17
  66.1 0.2 fusion.34
  66.3 0.7 fusion.60
  66.9 0.7 bitcast_add_fusion.16
  67.6 0.2 fusion.377
  67.8 2.8 %negate_add_fusion = (f32[32,8,128]{2,0,1:T(8,128)S(1)}, f32[32,8,128]{2,0,1:T(8,128)S(1)}, f32[32,8,128]{2,0,1:T(8,128)S(1)}, f32[32,8,128]{2,0,1:T(8,128)S(1)}...) fusion(f32[32,8,128]{2,0,1:T(8,128)S(1)} %get-tuple-element.15, ...), kind=kLoop, calls=%fused_computation.452 | loop fusion | flops 17006592 | bytes 12320768 | tf_op jit(solution)/shard_map/transpose(jvp())/add_any | solution.py:72
  70.7 0.3 fusion.273
  70.9 0.2 fusion.308
  71.2 0.2 fusion.310
  71.5 1.3 %collective-permute-start.12 = (f32[10,4,1]{2,0,1:T(8,128)S(1)}, f32[10,4,1]{2,0,1:T(8,128)S(1)}, u32[]{:S(2)}, u32[]{:S(2)}) collective-permute-start(f32[10,4,1]{2,0,1:T(8,128)S(1)} %get-tuple-element.141), channel_id=1, source_target_pairs={{0,1},{2,3},{4,5},{6,7},{8,9},{10,11},{12,13},{14,15},{16,17},{18,... | collective-permute-start | bytes 488 | tf_op jit(solution)/shard_map/ppermute | solution.py:39
  72.8 1.3 %collective-permute-start.13 = (f32[10,4,1]{2,0,1:T(8,128)S(1)}, f32[10,4,1]{2,0,1:T(8,128)S(1)}, u32[]{:S(2)}, u32[]{:S(2)}) collective-permute-start(f32[10,4,1]{2,0,1:T(8,128)S(1)} %get-tuple-element.142), channel_id=1, source_target_pairs={{1,0},{3,2},{5,4},{7,6},{9,8},{11,10},{13,12},{15,14},{17,16},{19,... | collective-permute-start | bytes 488 | tf_op jit(solution)/shard_map/ppermute | solution.py:42
  74.2 1.7 %collective-permute-done.13 = f32[10,4,1]{2,0,1:T(8,128)S(1)} collective-permute-done((f32[10,4,1]{2,0,1:T(8,128)S(1)}, f32[10,4,1]{2,0,1:T(8,128)S(1)}, u32[]{:S(2)}, u32[]{:S(2)}) %collective-permute-start.13) | collective-permute-done | bytes 192 | tf_op jit(solution)/shard_map/ppermute | solution.py:42
  76.0 1.5 %collective-permute-start.14 = (f32[10,1,36]{2,0,1:T(8,128)S(1)}, f32[10,1,36]{2,0,1:T(8,128)S(1)}, u32[]{:S(2)}, u32[]{:S(2)}) collective-permute-start(f32[10,1,36]{2,0,1:T(8,128)S(1)} %get-tuple-element.139), channel_id=1, source_target_pairs={{0,2},{1,3},{4,6},{5,7},{8,10},{9,11},{12,14},{13,15},{16,18},{17,... | collective-permute-start | bytes 4328 | tf_op jit(solution)/shard_map/ppermute | solution.py:39
  77.5 1.3 %collective-permute-start.15 = (f32[10,1,36]{2,0,1:T(8,128)S(1)}, f32[10,1,36]{2,0,1:T(8,128)S(1)}, u32[]{:S(2)}, u32[]{:S(2)}) collective-permute-start(f32[10,1,36]{2,0,1:T(8,128)S(1)} %get-tuple-element.140), channel_id=1, source_target_pairs={{2,0},{3,1},{6,4},{7,5},{10,8},{11,9},{14,12},{15,13},{18,16},{19,... | collective-permute-start | bytes 4328 | tf_op jit(solution)/shard_map/ppermute | solution.py:42
  78.8 1.3 %add_convert_fusion = bf16[19,32,8,128]{3,1,2,0:T(8,128)(2,1)S(1)} fusion(f32[1,32,8,128]{3,1,2,0:T(8,128)S(1)} %get-tuple-element.130, f32[1,32,8,128]{3,1,2,0:T(8,128)S(1)} %get-tuple-element.131, bf16[19,32,8,128]{3,1,2,0:T(8,128)(2,1)S(1)} %constant_dynamic-update-slice_fusion.12, f32[1,32,8,128]{3,1,2,0:T(8,128)S(1)} %get-tuple-element.132, ...), kind=kLoop, calls=%fused_computation.33 | loop fusion | flops 36732928 | bytes 5832723 | tf_op jit(solution)/shard_map/convert_element_type | solution.py:157
  80.1 1.6 %copy.32 = bf16[19,32,8,128]{3,2,1,0:T(8,128)(2,1)} copy(bf16[19,32,8,128]{3,1,2,0:T(8,128)(2,1)S(1)} %add_convert_fusion) | data formatting | bytes 2490368
  81.7 1.4 %collective-permute-done.15 = f32[10,1,36]{2,0,1:T(8,128)S(1)} collective-permute-done((f32[10,1,36]{2,0,1:T(8,128)S(1)}, f32[10,1,36]{2,0,1:T(8,128)S(1)}, u32[]{:S(2)}, u32[]{:S(2)}) %collective-permute-start.15) | collective-permute-done | bytes 1472 | tf_op jit(solution)/shard_map/ppermute | solution.py:42
  83.2 4.5 %collective-permute-start.16 = (f32[1,6,36]{2,0,1:T(1,128)S(1)}, f32[1,6,36]{2,0,1:T(1,128)S(1)}, u32[]{:S(2)}, u32[]{:S(2)}) collective-permute-start(f32[1,6,36]{2,0,1:T(1,128)S(1)} %get-tuple-element.137), channel_id=1, source_target_pairs={{0,4},{4,8},{8,12},{1,5},{5,9},{9,13},{2,6},{6,10},{10,14},{3,7},{... | collective-permute-start | bytes 2600 | tf_op jit(solution)/shard_map/ppermute | solution.py:39
  87.7 1.3 %collective-permute-start.17 = (f32[1,6,36]{2,0,1:T(1,128)S(1)}, f32[1,6,36]{2,0,1:T(1,128)S(1)}, u32[]{:S(2)}, u32[]{:S(2)}) collective-permute-start(f32[1,6,36]{2,0,1:T(1,128)S(1)} %get-tuple-element.138), channel_id=1, source_target_pairs={{4,0},{8,4},{12,8},{5,1},{9,5},{13,9},{6,2},{10,6},{14,10},{7,3},{... | collective-permute-start | bytes 2600 | tf_op jit(solution)/shard_map/ppermute | solution.py:42
  89.1 4.1 %collective-permute-done.17 = f32[1,6,36]{2,0,1:T(1,128)S(1)} collective-permute-done((f32[1,6,36]{2,0,1:T(1,128)S(1)}, f32[1,6,36]{2,0,1:T(1,128)S(1)}, u32[]{:S(2)}, u32[]{:S(2)}) %collective-permute-start.17) | collective-permute-done | bytes 896 | tf_op jit(solution)/shard_map/ppermute | solution.py:42
  93.5 0.6 copy.33
  (81 shorter events, 2.0 us)
Async XLA Ops:
  0.6 15.3 %copy-start.1 = (bf16[19,32,8,128]{3,2,1,0:T(8,128)(2,1)S(1)}, bf16[19,32,8,128]{3,2,1,0:T(8,128)(2,1)}, u32[]{:S(2)}) copy-start(bf16[19,32,8,128]{3,2,1,0:T(8,128)(2,1)} %param.4) | copy-start | bytes 3735556
  1.4 16.3 %collective-permute-start.7 = (f32[1,2,32]{2,1,0:T(2,128)S(1)}, f32[1,2,32]{2,1,0:T(2,128)S(1)}, u32[]{:S(2)}, u32[]{:S(2)}) collective-permute-start(f32[1,2,32]{2,1,0:T(2,128)S(1)} %get-tuple-element.147), channel_id=1, source_target_pairs={{4,0},{8,4},{12,8},{5,1},{9,5},{13,9},{6,2},{10,6},{14,10},{7,3},{... | collective-permute-start | bytes 776 | tf_op jit(solution)/shard_map/ppermute | solution.py:42
  2.7 14.9 %collective-permute-start.6 = (f32[1,2,32]{2,1,0:T(2,128)S(1)}, f32[1,2,32]{2,1,0:T(2,128)S(1)}, u32[]{:S(2)}, u32[]{:S(2)}) collective-permute-start(f32[1,2,32]{2,1,0:T(2,128)S(1)} %get-tuple-element.148), channel_id=1, source_target_pairs={{0,4},{4,8},{8,12},{1,5},{5,9},{9,13},{2,6},{6,10},{10,14},{3,7},{... | collective-permute-start | bytes 776 | tf_op jit(solution)/shard_map/ppermute | solution.py:39
  10.7 20.9 %collective-permute-start.1 = (bf16[10,1,8,128]{3,1,2,0:T(2,128)(2,1)S(1)}, bf16[10,1,8,128]{3,1,2,0:T(2,128)(2,1)S(1)}, u32[]{:S(2)}, u32[]{:S(2)}) collective-permute-start(bf16[10,1,8,128]{3,1,2,0:T(2,128)(2,1)S(1)} %get-tuple-element.118), channel_id=1, source_target_pairs={{0,4},{4,8},{8,12},{1,5},{5,9},{9,13},{2,6},{6,10},{10,14},{3,7},{... | collective-permute-start | bytes 61448 | tf_op jit(solution)/shard_map/ppermute | solution.py:39
  14.7 16.8 %collective-permute-start = (bf16[10,1,8,128]{3,1,2,0:T(2,128)(2,1)S(1)}, bf16[10,1,8,128]{3,1,2,0:T(2,128)(2,1)S(1)}, u32[]{:S(2)}, u32[]{:S(2)}) collective-permute-start(bf16[10,1,8,128]{3,1,2,0:T(2,128)(2,1)S(1)} %get-tuple-element.119), channel_id=1, source_target_pairs={{4,0},{8,4},{12,8},{5,1},{9,5},{13,9},{6,2},{10,6},{14,10},{7,3},{... | collective-permute-start | bytes 61448 | tf_op jit(solution)/shard_map/ppermute | solution.py:42
  16.0 0.9 copy-start.4
  16.0 1.0 %slice-start = ((bf16[19,32,8,128]{3,2,1,0:T(8,128)(2,1)}), bf16[1,32,8,128]{3,2,1,0:T(8,128)(2,1)S(1)}, s32[]{:S(2)}) async-start(bf16[19,32,8,128]{3,2,1,0:T(8,128)(2,1)} %param.5), calls=%async_computation | async-start | bytes 131072 | tf_op jit(solution)/shard_map/slice | solution.py:142
  16.1 1.6 %copy-start.6 = (f32[8,2,32]{2,1,0:T(2,128)S(1)}, f32[8,2,32]{2,1,0:T(2,128)}, u32[]{:S(2)}) copy-start(f32[8,2,32]{2,1,0:T(2,128)} %param.6) | copy-start | bytes 6148
  17.6 15.5 %slice-start.1 = ((bf16[19,32,8,128]{3,2,1,0:T(8,128)(2,1)}), bf16[4,32,8,128]{3,2,1,0:T(8,128)(2,1)S(1)}, s32[]{:S(2)}) async-start(bf16[19,32,8,128]{3,2,1,0:T(8,128)(2,1)} %param.5), calls=%async_computation.1 | async-start | bytes 524288 | tf_op jit(solution)/shard_map/slice | solution.py:142
  17.7 4.8 %collective-permute-start.8 = (f32[10,1,32]{2,1,0:T(1,128)S(1)}, f32[10,1,32]{2,1,0:T(1,128)S(1)}, u32[]{:S(2)}, u32[]{:S(2)}) collective-permute-start(f32[10,1,32]{2,1,0:T(1,128)S(1)} %get-tuple-element.145), channel_id=1, source_target_pairs={{0,2},{1,3},{4,6},{5,7},{8,10},{9,11},{12,14},{13,15},{16,18},{17,... | collective-permute-start | bytes 3848 | tf_op jit(solution)/shard_map/ppermute | solution.py:39
  21.1 5.5 %collective-permute-start.9 = (f32[10,1,32]{2,1,0:T(1,128)S(1)}, f32[10,1,32]{2,1,0:T(1,128)S(1)}, u32[]{:S(2)}, u32[]{:S(2)}) collective-permute-start(f32[10,1,32]{2,1,0:T(1,128)S(1)} %get-tuple-element.146), channel_id=1, source_target_pairs={{2,0},{3,1},{6,4},{7,5},{10,8},{11,9},{14,12},{15,13},{18,16},{19,... | collective-permute-start | bytes 3848 | tf_op jit(solution)/shard_map/ppermute | solution.py:42
  26.8 2.6 %collective-permute-start.10 = (f32[10,4,1]{2,1,0:T(4,128)S(1)}, f32[10,4,1]{2,1,0:T(4,128)S(1)}, u32[]{:S(2)}, u32[]{:S(2)}) collective-permute-start(f32[10,4,1]{2,1,0:T(4,128)S(1)} %get-tuple-element.143), channel_id=1, source_target_pairs={{0,1},{2,3},{4,5},{6,7},{8,9},{10,11},{12,13},{14,15},{16,17},{18,... | collective-permute-start | bytes 488 | tf_op jit(solution)/shard_map/ppermute | solution.py:39
  28.1 3.1 %collective-permute-start.11 = (f32[10,4,1]{2,1,0:T(4,128)S(1)}, f32[10,4,1]{2,1,0:T(4,128)S(1)}, u32[]{:S(2)}, u32[]{:S(2)}) collective-permute-start(f32[10,4,1]{2,1,0:T(4,128)S(1)} %get-tuple-element.144), channel_id=1, source_target_pairs={{1,0},{3,2},{5,4},{7,6},{9,8},{11,10},{13,12},{15,14},{17,16},{19,... | collective-permute-start | bytes 488 | tf_op jit(solution)/shard_map/ppermute | solution.py:42
  33.2 3.8 %collective-permute-start.2 = (bf16[10,32,1,128]{3,1,2,0:T(8,128)(2,1)S(1)}, bf16[10,32,1,128]{3,1,2,0:T(8,128)(2,1)S(1)}, u32[]{:S(2)}, u32[]{:S(2)}) collective-permute-start(bf16[10,32,1,128]{3,1,2,0:T(8,128)(2,1)S(1)} %get-tuple-element.116), channel_id=1, source_target_pairs={{0,2},{1,3},{4,6},{5,7},{8,10},{9,11},{12,14},{13,15},{16,18},{17,... | collective-permute-start | bytes 245768 | tf_op jit(solution)/shard_map/ppermute | solution.py:39
  34.8 6.3 %collective-permute-start.3 = (bf16[10,32,1,128]{3,1,2,0:T(8,128)(2,1)S(1)}, bf16[10,32,1,128]{3,1,2,0:T(8,128)(2,1)S(1)}, u32[]{:S(2)}, u32[]{:S(2)}) collective-permute-start(bf16[10,32,1,128]{3,1,2,0:T(8,128)(2,1)S(1)} %get-tuple-element.117), channel_id=1, source_target_pairs={{2,0},{3,1},{6,4},{7,5},{10,8},{11,9},{14,12},{15,13},{18,16},{19,... | collective-permute-start | bytes 245768 | tf_op jit(solution)/shard_map/ppermute | solution.py:42
  47.9 10.6 %collective-permute-start.5 = (bf16[10,32,8,1]{1,2,3,0:T(8,128)(2,1)}, bf16[10,32,8,1]{1,2,3,0:T(8,128)(2,1)}, u32[]{:S(2)}, u32[]{:S(2)}) collective-permute-start(bf16[10,32,8,1]{1,2,3,0:T(8,128)(2,1)} %copy.27), channel_id=1, source_target_pairs={{1,0},{3,2},{5,4},{7,6},{9,8},{11,10},{13,12},{15,14},{17,16},{19,... | collective-permute-start | bytes 15368 | tf_op jit(solution)/shard_map/ppermute | solution.py:42
  49.2 7.2 %collective-permute-start.4 = (bf16[10,32,8,1]{1,2,3,0:T(8,128)(2,1)}, bf16[10,32,8,1]{1,2,3,0:T(8,128)(2,1)}, u32[]{:S(2)}, u32[]{:S(2)}) collective-permute-start(bf16[10,32,8,1]{1,2,3,0:T(8,128)(2,1)} %copy.26), channel_id=1, source_target_pairs={{0,1},{2,3},{4,5},{6,7},{8,9},{10,11},{12,13},{14,15},{16,17},{18,... | collective-permute-start | bytes 15368 | tf_op jit(solution)/shard_map/ppermute | solution.py:39
  60.6 2.3 %copy-start = (bf16[19,32,8,128]{3,1,2,0:T(8,128)(2,1)S(1)}, bf16[19,32,8,128]{3,1,2,0:T(8,128)(2,1)}, u32[]{:S(2)}) copy-start(bf16[19,32,8,128]{3,1,2,0:T(8,128)(2,1)} %constant_dynamic-update-slice_fusion.26) | copy-start | bytes 3735556
  60.6 2.4 %copy-start.3 = (bf16[32,10,128]{2,0,1:T(8,128)(2,1)S(1)}, bf16[32,10,128]{2,0,1:T(8,128)(2,1)}, u32[]{:S(2)}) copy-start(bf16[32,10,128]{2,0,1:T(8,128)(2,1)} %get-tuple-element.97) | copy-start | bytes 245764
  60.6 2.5 %copy-start.2 = (bf16[32,10,128]{2,0,1:T(8,128)(2,1)S(1)}, bf16[32,10,128]{2,0,1:T(8,128)(2,1)}, u32[]{:S(2)}) copy-start(bf16[32,10,128]{2,0,1:T(8,128)(2,1)} %get-tuple-element.96) | copy-start | bytes 245764
  64.8 0.8 copy-start.5
  70.6 8.2 %copy-start.9 = (pred[19]{0:T(512)(128)(4,1)S(1)}, pred[19]{0:T(512)(128)(4,1)}, u32[]{:S(2)}) copy-start(pred[19]{0:T(512)(128)(4,1)} %constant.76.clone.1) | copy-start | bytes 61
  71.5 2.7 %collective-permute-start.12 = (f32[10,4,1]{2,0,1:T(8,128)S(1)}, f32[10,4,1]{2,0,1:T(8,128)S(1)}, u32[]{:S(2)}, u32[]{:S(2)}) collective-permute-start(f32[10,4,1]{2,0,1:T(8,128)S(1)} %get-tuple-element.141), channel_id=1, source_target_pairs={{0,1},{2,3},{4,5},{6,7},{8,9},{10,11},{12,13},{14,15},{16,17},{18,... | collective-permute-start | bytes 488 | tf_op jit(solution)/shard_map/ppermute | solution.py:39
  72.8 3.1 %collective-permute-start.13 = (f32[10,4,1]{2,0,1:T(8,128)S(1)}, f32[10,4,1]{2,0,1:T(8,128)S(1)}, u32[]{:S(2)}, u32[]{:S(2)}) collective-permute-start(f32[10,4,1]{2,0,1:T(8,128)S(1)} %get-tuple-element.142), channel_id=1, source_target_pairs={{1,0},{3,2},{5,4},{7,6},{9,8},{11,10},{13,12},{15,14},{17,16},{19,... | collective-permute-start | bytes 488 | tf_op jit(solution)/shard_map/ppermute | solution.py:42
  76.0 5.7 %collective-permute-start.14 = (f32[10,1,36]{2,0,1:T(8,128)S(1)}, f32[10,1,36]{2,0,1:T(8,128)S(1)}, u32[]{:S(2)}, u32[]{:S(2)}) collective-permute-start(f32[10,1,36]{2,0,1:T(8,128)S(1)} %get-tuple-element.139), channel_id=1, source_target_pairs={{0,2},{1,3},{4,6},{5,7},{8,10},{9,11},{12,14},{13,15},{16,18},{17,... | collective-permute-start | bytes 4328 | tf_op jit(solution)/shard_map/ppermute | solution.py:39
  77.5 5.5 %collective-permute-start.15 = (f32[10,1,36]{2,0,1:T(8,128)S(1)}, f32[10,1,36]{2,0,1:T(8,128)S(1)}, u32[]{:S(2)}, u32[]{:S(2)}) collective-permute-start(f32[10,1,36]{2,0,1:T(8,128)S(1)} %get-tuple-element.140), channel_id=1, source_target_pairs={{2,0},{3,1},{6,4},{7,5},{10,8},{11,9},{14,12},{15,13},{18,16},{19,... | collective-permute-start | bytes 4328 | tf_op jit(solution)/shard_map/ppermute | solution.py:42
  80.1 13.1 %copy-start.8 = (pred[2]{0:T(512)(128)(4,1)S(1)}, pred[2]{0:T(512)(128)(4,1)}, u32[]{:S(2)}) copy-start(pred[2]{0:T(512)(128)(4,1)} %constant.94.clone.1) | copy-start | bytes 10
  80.1 13.3 %copy-start.7 = (pred[32]{0:T(512)(128)(4,1)S(1)}, pred[32]{0:T(512)(128)(4,1)}, u32[]{:S(2)}) copy-start(pred[32]{0:T(512)(128)(4,1)} %constant.95.clone.1) | copy-start | bytes 100
  83.2 5.9 %collective-permute-start.16 = (f32[1,6,36]{2,0,1:T(1,128)S(1)}, f32[1,6,36]{2,0,1:T(1,128)S(1)}, u32[]{:S(2)}, u32[]{:S(2)}) collective-permute-start(f32[1,6,36]{2,0,1:T(1,128)S(1)} %get-tuple-element.137), channel_id=1, source_target_pairs={{0,4},{4,8},{8,12},{1,5},{5,9},{9,13},{2,6},{6,10},{10,14},{3,7},{... | collective-permute-start | bytes 2600 | tf_op jit(solution)/shard_map/ppermute | solution.py:39
  87.7 5.5 %collective-permute-start.17 = (f32[1,6,36]{2,0,1:T(1,128)S(1)}, f32[1,6,36]{2,0,1:T(1,128)S(1)}, u32[]{:S(2)}, u32[]{:S(2)}) collective-permute-start(f32[1,6,36]{2,0,1:T(1,128)S(1)} %get-tuple-element.138), channel_id=1, source_target_pairs={{4,0},{8,4},{12,8},{5,1},{9,5},{13,9},{6,2},{10,6},{14,10},{7,3},{... | collective-permute-start | bytes 2600 | tf_op jit(solution)/shard_map/ppermute | solution.py:42

commit v7 on v6

--- a/solution.py
+++ b/solution.py
@@ -129,7 +129,7 @@
 def per_device(forward_pops, adjoint_pops, coefficients, node_kind):
     cells_x, cells_y, cells_z = node_kind.shape
     coarse_x, coarse_y, coarse_z = coefficients.shape
-    window = padded(coefficients, (("gx", 0), ("gy", 1), ("gz", 2)), 1)
+    window = padded(coefficients, (("gz", 2), ("gy", 1), ("gx", 0)), 1)
     basis_x = basis_matrix(cells_x, coarse_x + 2, 0, -1)
     basis_y = basis_matrix(cells_y, coarse_y + 2, 0, -1)
     basis_z = basis_matrix(cells_z, coarse_z + 2, 0, -1)

time: 95 us -> 95.9 us (level)
  waiting for transfers between devices: 17.3 us -> 19.7 us
  local copies, waits for them, and re-layouts: 22.2 us -> 21.2 us
    ppermute x9, waiting for transfers between devices: 17.3 us -> 19.7 us  [padded(): lax.ppermute(lax.slice_in_dim(block, 0, width, axis=dim), axis, backward)]
    slice x6 -> x7, local copies, waits for them, and re-layouts: 2.15 us -> 1.08 us  [per_device(): lane_list = [adjoint_pops[component] for component in range(19)]]
    slice x2 -> x1, local copies, waits for them, and re-layouts: 3.03 us -> 2.22 us  [padded(): lax.slice_in_dim(block, 0, width, axis=dim)]
    unnamed x45 -> x43, local copies, waits for them, and re-layouts: 7.37 us -> 7.36 us
  transfers between devices with their start and end apart: 18 -> 18, of which waited for: 6 -> 6; matrix products, arithmetic and copies ran while one was open for 14% -> 13% of each run, Pallas kernels for 0% -> 0%
where the time goes in v7:
time: 95.9 us; the launch traced here: 95 us
  starting transfers between devices  38.4 us (40%)
  local copies, waits for them, and re-layouts  21.2 us (22%)
  waiting for transfers between devices  19.7 us (21%)
  other arithmetic  12 us (13%)
  matrix products  2.35 us (2%)
  between operations  1.31 us (1%)
    ppermute x9, starting transfers between devices, padded(): lax.ppermute(lax.slice_in_dim(block, block.shape[dim] - width, None, axis...  26.8 us
    ppermute x9, waiting for transfers between devices, padded(): lax.ppermute(lax.slice_in_dim(block, 0, width, axis=dim), axis, backward)  19.7 us
    ppermute x9, starting transfers between devices, padded(): lax.ppermute(lax.slice_in_dim(block, 0, width, axis=dim), axis, backward)  11.6 us
    unnamed x43, local copies, waits for them, and re-layouts  7.36 us
    slice x7, local copies, waits for them, and re-layouts, padded(): lax.slice_in_dim(block, block.shape[dim] - width, None, axis=dim)  4.65 us
    add_any x1, other arithmetic, collide(): flow_x = moment(populations, 0) / density  2.81 us
    concatenate x5, other arithmetic, padded(): block = jnp.concatenate([low, block, high], axis=dim)  2.5 us
    slice x1, local copies, waits for them, and re-layouts, padded(): lax.slice_in_dim(block, 0, width, axis=dim)  2.22 us
  transfers between devices with their start and end apart: 18, of which 6 were waited for; matrix products, arithmetic and copies ran while one was open for 13% of the time, Pallas kernels for 0%

profile of v7, /device:TPU:0, one launch (start us, length us, event | category | flops | bytes accessed | tf_op | source)
XLA Modules:
  0.0 95.0 jit_solution(746676454343980537)
XLA Ops:
  0.7 0.9 fusion.384
  1.6 2.4 %collective-permute-start.6 = (f32[8,2,1]{2,1,0:T(2,128)S(1)}, f32[8,2,1]{2,1,0:T(2,128)S(1)}, u32[]{:S(2)}, u32[]{:S(2)}) collective-permute-start(f32[8,2,1]{2,1,0:T(2,128)S(1)} %get-tuple-element.147), channel_id=1, source_target_pairs={{0,1},{2,3},{4,5},{6,7},{8,9},{10,11},{12,13},{14,15},{16,17},{18,... | collective-permute-start | bytes 200 | tf_op jit(solution)/shard_map/ppermute | solution.py:39
  4.0 1.3 %collective-permute-start.7 = (f32[8,2,1]{2,1,0:T(2,128)S(1)}, f32[8,2,1]{2,1,0:T(2,128)S(1)}, u32[]{:S(2)}, u32[]{:S(2)}) collective-permute-start(f32[8,2,1]{2,1,0:T(2,128)S(1)} %get-tuple-element.148), channel_id=1, source_target_pairs={{1,0},{3,2},{5,4},{7,6},{9,8},{11,10},{13,12},{15,14},{17,16},{19,... | collective-permute-start | bytes 200 | tf_op jit(solution)/shard_map/ppermute | solution.py:42
  5.3 1.1 %fusion.378 = (bf16[2,32,8,128]{3,2,1,0:T(8,128)(2,1)S(1)}, bf16[2,32,8,128]{3,2,1,0:T(8,128)(2,1)S(1)}, bf16[2,32,8,128]{3,2,1,0:T(8,128)(2,1)S(1)}) fusion(bf16[19,32,8,128]{3,2,1,0:T(8,128)(2,1)} %param.5), kind=kLoop, calls=%fused_computation.681 | loop fusion | bytes 786432 | tf_op jit(solution)/shard_map/slice | solution.py:142
  6.4 0.1 copy_dynamic-update-slice_fusion
  6.6 4.3 %collective-permute-start.1 = (bf16[10,1,8,128]{3,1,2,0:T(2,128)(2,1)S(1)}, bf16[10,1,8,128]{3,1,2,0:T(2,128)(2,1)S(1)}, u32[]{:S(2)}, u32[]{:S(2)}) collective-permute-start(bf16[10,1,8,128]{3,1,2,0:T(2,128)(2,1)S(1)} %get-tuple-element.118), channel_id=1, source_target_pairs={{0,4},{4,8},{8,12},{1,5},{5,9},{9,13},{2,6},{6,10},{10,14},{3,7},{... | collective-permute-start | bytes 61448 | tf_op jit(solution)/shard_map/ppermute | solution.py:39
  10.9 1.3 %collective-permute-start = (bf16[10,1,8,128]{3,1,2,0:T(2,128)(2,1)S(1)}, bf16[10,1,8,128]{3,1,2,0:T(2,128)(2,1)S(1)}, u32[]{:S(2)}, u32[]{:S(2)}) collective-permute-start(bf16[10,1,8,128]{3,1,2,0:T(2,128)(2,1)S(1)} %get-tuple-element.119), channel_id=1, source_target_pairs={{4,0},{8,4},{12,8},{5,1},{9,5},{13,9},{6,2},{10,6},{14,10},{7,3},{... | collective-permute-start | bytes 61448 | tf_op jit(solution)/shard_map/ppermute | solution.py:42
  12.3 0.3 copy_convert_fusion
  12.7 0.4 copy-done.5
  13.2 0.6 constant_dynamic-update-slice_fusion.30
  14.0 3.4 %collective-permute-start.8 = (f32[8,1,34]{2,1,0:T(1,128)S(1)}, f32[8,1,34]{2,1,0:T(1,128)S(1)}, u32[]{:S(2)}, u32[]{:S(2)}) collective-permute-start(f32[8,1,34]{2,1,0:T(1,128)S(1)} %get-tuple-element.145), channel_id=1, source_target_pairs={{0,2},{1,3},{4,6},{5,7},{8,10},{9,11},{12,14},{13,15},{16,18},{17,... | collective-permute-start | bytes 3272 | tf_op jit(solution)/shard_map/ppermute | solution.py:39
  17.4 1.3 %collective-permute-start.9 = (f32[8,1,34]{2,1,0:T(1,128)S(1)}, f32[8,1,34]{2,1,0:T(1,128)S(1)}, u32[]{:S(2)}, u32[]{:S(2)}) collective-permute-start(f32[8,1,34]{2,1,0:T(1,128)S(1)} %get-tuple-element.146), channel_id=1, source_target_pairs={{2,0},{3,1},{6,4},{7,5},{10,8},{11,9},{14,12},{15,13},{18,16},{19,... | collective-permute-start | bytes 3272 | tf_op jit(solution)/shard_map/ppermute | solution.py:42
  18.8 4.2 %collective-permute-done.9 = f32[8,1,34]{2,1,0:T(1,128)S(1)} collective-permute-done((f32[8,1,34]{2,1,0:T(1,128)S(1)}, f32[8,1,34]{2,1,0:T(1,128)S(1)}, u32[]{:S(2)}, u32[]{:S(2)}) %collective-permute-start.9) | collective-permute-done | bytes 1120 | tf_op jit(solution)/shard_map/ppermute | solution.py:42
  23.0 4.5 %collective-permute-start.10 = (f32[1,4,34]{2,1,0:T(4,128)S(1)}, f32[1,4,34]{2,1,0:T(4,128)S(1)}, u32[]{:S(2)}, u32[]{:S(2)}) collective-permute-start(f32[1,4,34]{2,1,0:T(4,128)S(1)} %get-tuple-element.143), channel_id=1, source_target_pairs={{0,4},{4,8},{8,12},{1,5},{5,9},{9,13},{2,6},{6,10},{10,14},{3,7},{... | collective-permute-start | bytes 1640 | tf_op jit(solution)/shard_map/ppermute | solution.py:39
  27.6 1.3 %collective-permute-start.11 = (f32[1,4,34]{2,1,0:T(4,128)S(1)}, f32[1,4,34]{2,1,0:T(4,128)S(1)}, u32[]{:S(2)}, u32[]{:S(2)}) collective-permute-start(f32[1,4,34]{2,1,0:T(4,128)S(1)} %get-tuple-element.144), channel_id=1, source_target_pairs={{4,0},{8,4},{12,8},{5,1},{9,5},{13,9},{6,2},{10,6},{14,10},{7,3},{... | collective-permute-start | bytes 1640 | tf_op jit(solution)/shard_map/ppermute | solution.py:42
  29.0 4.1 %collective-permute-done.11 = f32[1,4,34]{2,1,0:T(4,128)S(1)} collective-permute-done((f32[1,4,34]{2,1,0:T(4,128)S(1)}, f32[1,4,34]{2,1,0:T(4,128)S(1)}, u32[]{:S(2)}, u32[]{:S(2)}) %collective-permute-start.11) | collective-permute-done | bytes 576 | tf_op jit(solution)/shard_map/ppermute | solution.py:42
  33.1 0.2 fusion.313
  33.5 0.7 constant_dynamic-update-slice_fusion.9
  34.3 0.7 constant_dynamic-update-slice_fusion.8
  35.1 1.7 %collective-permute-start.2 = (bf16[10,32,1,128]{3,1,2,0:T(8,128)(2,1)S(1)}, bf16[10,32,1,128]{3,1,2,0:T(8,128)(2,1)S(1)}, u32[]{:S(2)}, u32[]{:S(2)}) collective-permute-start(bf16[10,32,1,128]{3,1,2,0:T(8,128)(2,1)S(1)} %get-tuple-element.116), channel_id=1, source_target_pairs={{0,2},{1,3},{4,6},{5,7},{8,10},{9,11},{12,14},{13,15},{16,18},{17,... | collective-permute-start | bytes 245768 | tf_op jit(solution)/shard_map/ppermute | solution.py:39
  36.7 1.3 %collective-permute-start.3 = (bf16[10,32,1,128]{3,1,2,0:T(8,128)(2,1)S(1)}, bf16[10,32,1,128]{3,1,2,0:T(8,128)(2,1)S(1)}, u32[]{:S(2)}, u32[]{:S(2)}) collective-permute-start(bf16[10,32,1,128]{3,1,2,0:T(8,128)(2,1)S(1)} %get-tuple-element.117), channel_id=1, source_target_pairs={{2,0},{3,1},{6,4},{7,5},{10,8},{11,9},{14,12},{15,13},{18,16},{19,... | collective-permute-start | bytes 245768 | tf_op jit(solution)/shard_map/ppermute | solution.py:42
  38.0 0.8 fusion.318
  38.8 4.2 %collective-permute-done.3 = bf16[10,32,1,128]{3,1,2,0:T(8,128)(2,1)S(1)} collective-permute-done((bf16[10,32,1,128]{3,1,2,0:T(8,128)(2,1)S(1)}, bf16[10,32,1,128]{3,1,2,0:T(8,128)(2,1)S(1)}, u32[]{:S(2)}, u32[]{:S(2)}) %collective-permute-start.3) | collective-permute-done | bytes 81952 | tf_op jit(solution)/shard_map/ppermute | solution.py:42
  43.2 0.8 slice_bitcast_fusion.31
  44.0 1.3 %fusion.379 = (bf16[10,32,8,1]{3,1,2,0:T(8,128)(2,1)}, bf16[10,32,8,1]{3,1,2,0:T(8,128)(2,1)}) fusion(bf16[10,32,8,128]{3,1,2,0:T(8,128)(2,1)S(1)} %constant_dynamic-update-slice_fusion.4), kind=kLoop, calls=%fused_computation.682 | loop fusion | bytes 20480 | tf_op jit(solution)/shard_map/slice | solution.py:40
  45.3 2.2 %copy.26 = bf16[10,32,8,1]{1,2,3,0:T(8,128)(2,1)} copy(bf16[10,32,8,1]{3,1,2,0:T(8,128)(2,1)} %get-tuple-element.114) | data formatting | bytes 10240 | tf_op jit(solution)/shard_map/slice | solution.py:40
  47.6 2.2 %copy.27 = bf16[10,32,8,1]{1,2,3,0:T(8,128)(2,1)} copy(bf16[10,32,8,1]{3,1,2,0:T(8,128)(2,1)} %get-tuple-element.115) | data formatting | bytes 10240 | tf_op jit(solution)/shard_map/slice | solution.py:42
  49.8 1.3 %collective-permute-start.5 = (bf16[10,32,8,1]{1,2,3,0:T(8,128)(2,1)}, bf16[10,32,8,1]{1,2,3,0:T(8,128)(2,1)}, u32[]{:S(2)}, u32[]{:S(2)}) collective-permute-start(bf16[10,32,8,1]{1,2,3,0:T(8,128)(2,1)} %copy.27), channel_id=1, source_target_pairs={{1,0},{3,2},{5,4},{7,6},{9,8},{11,10},{13,12},{15,14},{17,16},{19,... | collective-permute-start | bytes 15368 | tf_op jit(solution)/shard_map/ppermute | solution.py:42
  51.1 4.2 %collective-permute-start.4 = (bf16[10,32,8,1]{1,2,3,0:T(8,128)(2,1)}, bf16[10,32,8,1]{1,2,3,0:T(8,128)(2,1)}, u32[]{:S(2)}, u32[]{:S(2)}) collective-permute-start(bf16[10,32,8,1]{1,2,3,0:T(8,128)(2,1)} %copy.26), channel_id=1, source_target_pairs={{0,1},{2,3},{4,5},{6,7},{8,9},{10,11},{12,13},{14,15},{16,17},{18,... | collective-permute-start | bytes 15368 | tf_op jit(solution)/shard_map/ppermute | solution.py:39
  55.3 1.5 %constant_dynamic-update-slice_fusion.27 = bf16[19,32,8,128]{3,1,2,0:T(8,128)(2,1)} fusion(bf16[19,32,8,128]{3,1,2,0:T(8,128)(2,1)} %get-tuple-element.106, bf16[32,10,128]{2,0,1:T(8,128)(2,1)} %get-tuple-element.103), kind=kLoop, calls=%fused_computation.558 | loop fusion | bytes 131072
  56.8 1.5 %constant_dynamic-update-slice_fusion.26 = bf16[19,32,8,128]{3,1,2,0:T(8,128)(2,1)} fusion(bf16[19,32,8,128]{3,1,2,0:T(8,128)(2,1)} %constant_dynamic-update-slice_fusion.27, bf16[32,10,128]{2,0,1:T(8,128)(2,1)} %get-tuple-element.102), kind=kLoop, calls=%fused_computation.557 | loop fusion | bytes 131072
  58.2 2.1 %copy.28 = bf16[10,32,8,1]{3,1,2,0:T(8,128)(2,1)} copy(bf16[10,32,8,1]{1,2,3,0:T(8,128)(2,1)} %collective-permute-done.4) | data formatting | bytes 10240 | tf_op jit(solution)/shard_map/ppermute | solution.py:39
  60.4 2.1 %copy.29 = bf16[10,32,8,1]{3,1,2,0:T(8,128)(2,1)} copy(bf16[10,32,8,1]{1,2,3,0:T(8,128)(2,1)} %collective-permute-done.5) | data formatting | bytes 10240 | tf_op jit(solution)/shard_map/ppermute | solution.py:42
  62.5 2.1 %pad_maximum_fusion = bf16[10,32,8,130]{3,1,2,0:T(8,128)(2,1)S(1)} fusion(bf16[10,32,8,1]{3,1,2,0:T(8,128)(2,1)} %copy.29, bf16[10,32,8,128]{3,1,2,0:T(8,128)(2,1)S(1)} %constant_dynamic-update-slice_fusion.4, bf16[10,32,8,1]{3,1,2,0:T(8,128)(2,1)} %copy.28), kind=kLoop, calls=%fused_computation.34 | loop fusion | flops 1996800 | bytes 1331200 | tf_op jit(solution)/shard_map/concatenate | solution.py:43
  64.6 0.1 slice_bitcast_fusion.21
  64.8 0.1 constant_dynamic-update-slice_fusion.25
  65.0 0.1 constant_dynamic-update-slice_fusion.19
  65.2 0.1 constant_dynamic-update-slice_fusion.16
  65.3 0.1 constant_dynamic-update-slice_fusion.15
  65.4 0.1 constant_dynamic-update-slice_fusion.12
  65.5 1.1 %fusion.1 = (f32[19,32,8,128]{3,1,2,0:T(8,128)S(1)}, f32[19,32,8,128]{3,1,2,0:T(8,128)S(1)}, f32[19,32,8,128]{3,1,2,0:T(8,128)S(1)}) fusion(bf16[19,32,8,128]{3,1,2,0:T(8,128)(2,1)S(1)} %constant_dynamic-update-slice_fusion.12, pred[32,8,128]{2,0,1:T(8,128)(4,1)S(1)} %copy.19, pred[32,8,128]{2,0,1:T(8,128)(4,1)S(1)} %copy.18, pred[32,8,128]{2,0,1:T(8,128)(4,1)S(1)} %copy.31), kind=kLoop, calls=%fused_computation.3 | loop fusion | flops 5603328 | bytes 8814592 | tf_op jit(solution)/shard_map/transpose(jvp(jit(_where)))/select_n | solution.py:89
  66.6 0.3 bitcast_add_fusion.11
  66.9 0.4 copy-done.6
  67.4 0.5 bitcast_add_fusion.17
  67.9 0.2 fusion.34
  68.1 0.7 fusion.60
  68.8 0.7 bitcast_add_fusion.16
  69.5 0.3 fusion.377
  69.8 2.8 %negate_add_fusion = (f32[32,8,128]{2,0,1:T(8,128)S(1)}, f32[32,8,128]{2,0,1:T(8,128)S(1)}, f32[32,8,128]{2,0,1:T(8,128)S(1)}, f32[32,8,128]{2,0,1:T(8,128)S(1)}...) fusion(f32[32,8,128]{2,0,1:T(8,128)S(1)} %get-tuple-element.15, ...), kind=kLoop, calls=%fused_computation.452 | loop fusion | flops 17006592 | bytes 12320768 | tf_op jit(solution)/shard_map/transpose(jvp())/add_any | solution.py:72
  72.6 0.3 fusion.273
  72.9 0.2 fusion.308
  73.1 0.2 fusion.310
  73.4 1.3 %collective-permute-start.12 = (f32[10,4,1]{2,0,1:T(8,128)S(1)}, f32[10,4,1]{2,0,1:T(8,128)S(1)}, u32[]{:S(2)}, u32[]{:S(2)}) collective-permute-start(f32[10,4,1]{2,0,1:T(8,128)S(1)} %get-tuple-element.141), channel_id=1, source_target_pairs={{0,1},{2,3},{4,5},{6,7},{8,9},{10,11},{12,13},{14,15},{16,17},{18,... | collective-permute-start | bytes 488 | tf_op jit(solution)/shard_map/ppermute | solution.py:39
  74.7 1.3 %collective-permute-start.13 = (f32[10,4,1]{2,0,1:T(8,128)S(1)}, f32[10,4,1]{2,0,1:T(8,128)S(1)}, u32[]{:S(2)}, u32[]{:S(2)}) collective-permute-start(f32[10,4,1]{2,0,1:T(8,128)S(1)} %get-tuple-element.142), channel_id=1, source_target_pairs={{1,0},{3,2},{5,4},{7,6},{9,8},{11,10},{13,12},{15,14},{17,16},{19,... | collective-permute-start | bytes 488 | tf_op jit(solution)/shard_map/ppermute | solution.py:42
  76.1 1.7 %collective-permute-done.13 = f32[10,4,1]{2,0,1:T(8,128)S(1)} collective-permute-done((f32[10,4,1]{2,0,1:T(8,128)S(1)}, f32[10,4,1]{2,0,1:T(8,128)S(1)}, u32[]{:S(2)}, u32[]{:S(2)}) %collective-permute-start.13) | collective-permute-done | bytes 192 | tf_op jit(solution)/shard_map/ppermute | solution.py:42
  77.9 1.5 %collective-permute-start.14 = (f32[10,1,36]{2,0,1:T(8,128)S(1)}, f32[10,1,36]{2,0,1:T(8,128)S(1)}, u32[]{:S(2)}, u32[]{:S(2)}) collective-permute-start(f32[10,1,36]{2,0,1:T(8,128)S(1)} %get-tuple-element.139), channel_id=1, source_target_pairs={{0,2},{1,3},{4,6},{5,7},{8,10},{9,11},{12,14},{13,15},{16,18},{17,... | collective-permute-start | bytes 4328 | tf_op jit(solution)/shard_map/ppermute | solution.py:39
  79.5 1.3 %collective-permute-start.15 = (f32[10,1,36]{2,0,1:T(8,128)S(1)}, f32[10,1,36]{2,0,1:T(8,128)S(1)}, u32[]{:S(2)}, u32[]{:S(2)}) collective-permute-start(f32[10,1,36]{2,0,1:T(8,128)S(1)} %get-tuple-element.140), channel_id=1, source_target_pairs={{2,0},{3,1},{6,4},{7,5},{10,8},{11,9},{14,12},{15,13},{18,16},{19,... | collective-permute-start | bytes 4328 | tf_op jit(solution)/shard_map/ppermute | solution.py:42
  80.8 1.2 %add_convert_fusion = bf16[19,32,8,128]{3,1,2,0:T(8,128)(2,1)S(1)} fusion(f32[1,32,8,128]{3,1,2,0:T(8,128)S(1)} %get-tuple-element.130, f32[1,32,8,128]{3,1,2,0:T(8,128)S(1)} %get-tuple-element.131, bf16[19,32,8,128]{3,1,2,0:T(8,128)(2,1)S(1)} %constant_dynamic-update-slice_fusion.12, f32[1,32,8,128]{3,1,2,0:T(8,128)S(1)} %get-tuple-element.132, ...), kind=kLoop, calls=%fused_computation.33 | loop fusion | flops 36732928 | bytes 5832723 | tf_op jit(solution)/shard_map/convert_element_type | solution.py:157
  82.1 1.6 %copy.32 = bf16[19,32,8,128]{3,2,1,0:T(8,128)(2,1)} copy(bf16[19,32,8,128]{3,1,2,0:T(8,128)(2,1)S(1)} %add_convert_fusion) | data formatting | bytes 2490368
  83.6 1.4 %collective-permute-done.15 = f32[10,1,36]{2,0,1:T(8,128)S(1)} collective-permute-done((f32[10,1,36]{2,0,1:T(8,128)S(1)}, f32[10,1,36]{2,0,1:T(8,128)S(1)}, u32[]{:S(2)}, u32[]{:S(2)}) %collective-permute-start.15) | collective-permute-done | bytes 1472 | tf_op jit(solution)/shard_map/ppermute | solution.py:42
  85.1 3.5 %collective-permute-start.16 = (f32[1,6,36]{2,0,1:T(1,128)S(1)}, f32[1,6,36]{2,0,1:T(1,128)S(1)}, u32[]{:S(2)}, u32[]{:S(2)}) collective-permute-start(f32[1,6,36]{2,0,1:T(1,128)S(1)} %get-tuple-element.137), channel_id=1, source_target_pairs={{0,4},{4,8},{8,12},{1,5},{5,9},{9,13},{2,6},{6,10},{10,14},{3,7},{... | collective-permute-start | bytes 2600 | tf_op jit(solution)/shard_map/ppermute | solution.py:39
  88.6 1.3 %collective-permute-start.17 = (f32[1,6,36]{2,0,1:T(1,128)S(1)}, f32[1,6,36]{2,0,1:T(1,128)S(1)}, u32[]{:S(2)}, u32[]{:S(2)}) collective-permute-start(f32[1,6,36]{2,0,1:T(1,128)S(1)} %get-tuple-element.138), channel_id=1, source_target_pairs={{4,0},{8,4},{12,8},{5,1},{9,5},{13,9},{6,2},{10,6},{14,10},{7,3},{... | collective-permute-start | bytes 2600 | tf_op jit(solution)/shard_map/ppermute | solution.py:42
  90.0 4.1 %collective-permute-done.17 = f32[1,6,36]{2,0,1:T(1,128)S(1)} collective-permute-done((f32[1,6,36]{2,0,1:T(1,128)S(1)}, f32[1,6,36]{2,0,1:T(1,128)S(1)}, u32[]{:S(2)}, u32[]{:S(2)}) %collective-permute-start.17) | collective-permute-done | bytes 896 | tf_op jit(solution)/shard_map/ppermute | solution.py:42
  94.3 0.6 copy.33
  (79 shorter events, 1.9 us)
Async XLA Ops:
  0.6 5.7 %slice-start = ((bf16[19,32,8,128]{3,2,1,0:T(8,128)(2,1)}), bf16[8,32,8,128]{3,2,1,0:T(8,128)(2,1)S(1)}, s32[]{:S(2)}) async-start(bf16[19,32,8,128]{3,2,1,0:T(8,128)(2,1)} %param.5), calls=%async_computation | async-start | bytes 1048576 | tf_op jit(solution)/shard_map/slice | solution.py:142
  0.6 11.6 %copy-start.1 = (bf16[19,32,8,128]{3,2,1,0:T(8,128)(2,1)S(1)}, bf16[19,32,8,128]{3,2,1,0:T(8,128)(2,1)}, u32[]{:S(2)}) copy-start(bf16[19,32,8,128]{3,2,1,0:T(8,128)(2,1)} %param.4) | copy-start | bytes 3735556
  1.6 12.3 %collective-permute-start.6 = (f32[8,2,1]{2,1,0:T(2,128)S(1)}, f32[8,2,1]{2,1,0:T(2,128)S(1)}, u32[]{:S(2)}, u32[]{:S(2)}) collective-permute-start(f32[8,2,1]{2,1,0:T(2,128)S(1)} %get-tuple-element.147), channel_id=1, source_target_pairs={{0,1},{2,3},{4,5},{6,7},{8,9},{10,11},{12,13},{14,15},{16,17},{18,... | collective-permute-start | bytes 200 | tf_op jit(solution)/shard_map/ppermute | solution.py:39
  4.0 9.9 %collective-permute-start.7 = (f32[8,2,1]{2,1,0:T(2,128)S(1)}, f32[8,2,1]{2,1,0:T(2,128)S(1)}, u32[]{:S(2)}, u32[]{:S(2)}) collective-permute-start(f32[8,2,1]{2,1,0:T(2,128)S(1)} %get-tuple-element.148), channel_id=1, source_target_pairs={{1,0},{3,2},{5,4},{7,6},{9,8},{11,10},{13,12},{15,14},{17,16},{19,... | collective-permute-start | bytes 200 | tf_op jit(solution)/shard_map/ppermute | solution.py:42
  6.6 26.9 %collective-permute-start.1 = (bf16[10,1,8,128]{3,1,2,0:T(2,128)(2,1)S(1)}, bf16[10,1,8,128]{3,1,2,0:T(2,128)(2,1)S(1)}, u32[]{:S(2)}, u32[]{:S(2)}) collective-permute-start(bf16[10,1,8,128]{3,1,2,0:T(2,128)(2,1)S(1)} %get-tuple-element.118), channel_id=1, source_target_pairs={{0,4},{4,8},{8,12},{1,5},{5,9},{9,13},{2,6},{6,10},{10,14},{3,7},{... | collective-permute-start | bytes 61448 | tf_op jit(solution)/shard_map/ppermute | solution.py:39
  10.9 22.5 %collective-permute-start = (bf16[10,1,8,128]{3,1,2,0:T(2,128)(2,1)S(1)}, bf16[10,1,8,128]{3,1,2,0:T(2,128)(2,1)S(1)}, u32[]{:S(2)}, u32[]{:S(2)}) collective-permute-start(bf16[10,1,8,128]{3,1,2,0:T(2,128)(2,1)S(1)} %get-tuple-element.119), channel_id=1, source_target_pairs={{4,0},{8,4},{12,8},{5,1},{9,5},{13,9},{6,2},{10,6},{14,10},{7,3},{... | collective-permute-start | bytes 61448 | tf_op jit(solution)/shard_map/ppermute | solution.py:42
  12.2 0.9 copy-start.5
  12.2 1.0 %slice-start.1 = ((bf16[19,32,8,128]{3,2,1,0:T(8,128)(2,1)}), bf16[1,32,8,128]{3,2,1,0:T(8,128)(2,1)S(1)}, s32[]{:S(2)}) async-start(bf16[19,32,8,128]{3,2,1,0:T(8,128)(2,1)} %param.5), calls=%async_computation.1 | async-start | bytes 131072 | tf_op jit(solution)/shard_map/slice | solution.py:142
  12.3 1.6 %copy-start.4 = (f32[8,2,32]{2,1,0:T(2,128)S(1)}, f32[8,2,32]{2,1,0:T(2,128)}, u32[]{:S(2)}) copy-start(f32[8,2,32]{2,1,0:T(2,128)} %param.6) | copy-start | bytes 6148
  13.8 21.1 %slice-start.2 = ((bf16[19,32,8,128]{3,2,1,0:T(8,128)(2,1)}), bf16[4,32,8,128]{3,2,1,0:T(8,128)(2,1)S(1)}, s32[]{:S(2)}) async-start(bf16[19,32,8,128]{3,2,1,0:T(8,128)(2,1)} %param.5), calls=%async_computation.2 | async-start | bytes 524288 | tf_op jit(solution)/shard_map/slice | solution.py:142
  14.0 4.7 %collective-permute-start.8 = (f32[8,1,34]{2,1,0:T(1,128)S(1)}, f32[8,1,34]{2,1,0:T(1,128)S(1)}, u32[]{:S(2)}, u32[]{:S(2)}) collective-permute-start(f32[8,1,34]{2,1,0:T(1,128)S(1)} %get-tuple-element.145), channel_id=1, source_target_pairs={{0,2},{1,3},{4,6},{5,7},{8,10},{9,11},{12,14},{13,15},{16,18},{17,... | collective-permute-start | bytes 3272 | tf_op jit(solution)/shard_map/ppermute | solution.py:39
  17.4 5.5 %collective-permute-start.9 = (f32[8,1,34]{2,1,0:T(1,128)S(1)}, f32[8,1,34]{2,1,0:T(1,128)S(1)}, u32[]{:S(2)}, u32[]{:S(2)}) collective-permute-start(f32[8,1,34]{2,1,0:T(1,128)S(1)} %get-tuple-element.146), channel_id=1, source_target_pairs={{2,0},{3,1},{6,4},{7,5},{10,8},{11,9},{14,12},{15,13},{18,16},{19,... | collective-permute-start | bytes 3272 | tf_op jit(solution)/shard_map/ppermute | solution.py:42
  23.0 5.9 %collective-permute-start.10 = (f32[1,4,34]{2,1,0:T(4,128)S(1)}, f32[1,4,34]{2,1,0:T(4,128)S(1)}, u32[]{:S(2)}, u32[]{:S(2)}) collective-permute-start(f32[1,4,34]{2,1,0:T(4,128)S(1)} %get-tuple-element.143), channel_id=1, source_target_pairs={{0,4},{4,8},{8,12},{1,5},{5,9},{9,13},{2,6},{6,10},{10,14},{3,7},{... | collective-permute-start | bytes 1640 | tf_op jit(solution)/shard_map/ppermute | solution.py:39
  27.6 5.5 %collective-permute-start.11 = (f32[1,4,34]{2,1,0:T(4,128)S(1)}, f32[1,4,34]{2,1,0:T(4,128)S(1)}, u32[]{:S(2)}, u32[]{:S(2)}) collective-permute-start(f32[1,4,34]{2,1,0:T(4,128)S(1)} %get-tuple-element.144), channel_id=1, source_target_pairs={{4,0},{8,4},{12,8},{5,1},{9,5},{13,9},{6,2},{10,6},{14,10},{7,3},{... | collective-permute-start | bytes 1640 | tf_op jit(solution)/shard_map/ppermute | solution.py:42
  35.1 3.8 %collective-permute-start.2 = (bf16[10,32,1,128]{3,1,2,0:T(8,128)(2,1)S(1)}, bf16[10,32,1,128]{3,1,2,0:T(8,128)(2,1)S(1)}, u32[]{:S(2)}, u32[]{:S(2)}) collective-permute-start(bf16[10,32,1,128]{3,1,2,0:T(8,128)(2,1)S(1)} %get-tuple-element.116), channel_id=1, source_target_pairs={{0,2},{1,3},{4,6},{5,7},{8,10},{9,11},{12,14},{13,15},{16,18},{17,... | collective-permute-start | bytes 245768 | tf_op jit(solution)/shard_map/ppermute | solution.py:39
  36.7 6.3 %collective-permute-start.3 = (bf16[10,32,1,128]{3,1,2,0:T(8,128)(2,1)S(1)}, bf16[10,32,1,128]{3,1,2,0:T(8,128)(2,1)S(1)}, u32[]{:S(2)}, u32[]{:S(2)}) collective-permute-start(bf16[10,32,1,128]{3,1,2,0:T(8,128)(2,1)S(1)} %get-tuple-element.117), channel_id=1, source_target_pairs={{2,0},{3,1},{6,4},{7,5},{10,8},{11,9},{14,12},{15,13},{18,16},{19,... | collective-permute-start | bytes 245768 | tf_op jit(solution)/shard_map/ppermute | solution.py:42
  49.8 10.6 %collective-permute-start.5 = (bf16[10,32,8,1]{1,2,3,0:T(8,128)(2,1)}, bf16[10,32,8,1]{1,2,3,0:T(8,128)(2,1)}, u32[]{:S(2)}, u32[]{:S(2)}) collective-permute-start(bf16[10,32,8,1]{1,2,3,0:T(8,128)(2,1)} %copy.27), channel_id=1, source_target_pairs={{1,0},{3,2},{5,4},{7,6},{9,8},{11,10},{13,12},{15,14},{17,16},{19,... | collective-permute-start | bytes 15368 | tf_op jit(solution)/shard_map/ppermute | solution.py:42
  51.1 7.2 %collective-permute-start.4 = (bf16[10,32,8,1]{1,2,3,0:T(8,128)(2,1)}, bf16[10,32,8,1]{1,2,3,0:T(8,128)(2,1)}, u32[]{:S(2)}, u32[]{:S(2)}) collective-permute-start(bf16[10,32,8,1]{1,2,3,0:T(8,128)(2,1)} %copy.26), channel_id=1, source_target_pairs={{0,1},{2,3},{4,5},{6,7},{8,9},{10,11},{12,13},{14,15},{16,17},{18,... | collective-permute-start | bytes 15368 | tf_op jit(solution)/shard_map/ppermute | solution.py:39
  62.5 2.3 %copy-start = (bf16[19,32,8,128]{3,1,2,0:T(8,128)(2,1)S(1)}, bf16[19,32,8,128]{3,1,2,0:T(8,128)(2,1)}, u32[]{:S(2)}) copy-start(bf16[19,32,8,128]{3,1,2,0:T(8,128)(2,1)} %constant_dynamic-update-slice_fusion.26) | copy-start | bytes 3735556
  62.5 2.4 %copy-start.3 = (bf16[32,10,128]{2,0,1:T(8,128)(2,1)S(1)}, bf16[32,10,128]{2,0,1:T(8,128)(2,1)}, u32[]{:S(2)}) copy-start(bf16[32,10,128]{2,0,1:T(8,128)(2,1)} %get-tuple-element.97) | copy-start | bytes 245764
  62.5 2.4 %copy-start.2 = (bf16[32,10,128]{2,0,1:T(8,128)(2,1)S(1)}, bf16[32,10,128]{2,0,1:T(8,128)(2,1)}, u32[]{:S(2)}) copy-start(bf16[32,10,128]{2,0,1:T(8,128)(2,1)} %get-tuple-element.96) | copy-start | bytes 245764
  66.6 0.8 copy-start.6
  72.6 8.2 %copy-start.9 = (pred[19]{0:T(512)(128)(4,1)S(1)}, pred[19]{0:T(512)(128)(4,1)}, u32[]{:S(2)}) copy-start(pred[19]{0:T(512)(128)(4,1)} %constant.76.clone.1) | copy-start | bytes 61
  73.4 2.7 %collective-permute-start.12 = (f32[10,4,1]{2,0,1:T(8,128)S(1)}, f32[10,4,1]{2,0,1:T(8,128)S(1)}, u32[]{:S(2)}, u32[]{:S(2)}) collective-permute-start(f32[10,4,1]{2,0,1:T(8,128)S(1)} %get-tuple-element.141), channel_id=1, source_target_pairs={{0,1},{2,3},{4,5},{6,7},{8,9},{10,11},{12,13},{14,15},{16,17},{18,... | collective-permute-start | bytes 488 | tf_op jit(solution)/shard_map/ppermute | solution.py:39
  74.7 3.1 %collective-permute-start.13 = (f32[10,4,1]{2,0,1:T(8,128)S(1)}, f32[10,4,1]{2,0,1:T(8,128)S(1)}, u32[]{:S(2)}, u32[]{:S(2)}) collective-permute-start(f32[10,4,1]{2,0,1:T(8,128)S(1)} %get-tuple-element.142), channel_id=1, source_target_pairs={{1,0},{3,2},{5,4},{7,6},{9,8},{11,10},{13,12},{15,14},{17,16},{19,... | collective-permute-start | bytes 488 | tf_op jit(solution)/shard_map/ppermute | solution.py:42
  77.9 5.7 %collective-permute-start.14 = (f32[10,1,36]{2,0,1:T(8,128)S(1)}, f32[10,1,36]{2,0,1:T(8,128)S(1)}, u32[]{:S(2)}, u32[]{:S(2)}) collective-permute-start(f32[10,1,36]{2,0,1:T(8,128)S(1)} %get-tuple-element.139), channel_id=1, source_target_pairs={{0,2},{1,3},{4,6},{5,7},{8,10},{9,11},{12,14},{13,15},{16,18},{17,... | collective-permute-start | bytes 4328 | tf_op jit(solution)/shard_map/ppermute | solution.py:39
  79.5 5.5 %collective-permute-start.15 = (f32[10,1,36]{2,0,1:T(8,128)S(1)}, f32[10,1,36]{2,0,1:T(8,128)S(1)}, u32[]{:S(2)}, u32[]{:S(2)}) collective-permute-start(f32[10,1,36]{2,0,1:T(8,128)S(1)} %get-tuple-element.140), channel_id=1, source_target_pairs={{2,0},{3,1},{6,4},{7,5},{10,8},{11,9},{14,12},{15,13},{18,16},{19,... | collective-permute-start | bytes 4328 | tf_op jit(solution)/shard_map/ppermute | solution.py:42
  82.0 12.1 %copy-start.8 = (pred[2]{0:T(512)(128)(4,1)S(1)}, pred[2]{0:T(512)(128)(4,1)}, u32[]{:S(2)}) copy-start(pred[2]{0:T(512)(128)(4,1)} %constant.94.clone.1) | copy-start | bytes 10
  82.0 12.2 %copy-start.7 = (pred[32]{0:T(512)(128)(4,1)S(1)}, pred[32]{0:T(512)(128)(4,1)}, u32[]{:S(2)}) copy-start(pred[32]{0:T(512)(128)(4,1)} %constant.95.clone.1) | copy-start | bytes 100
  85.1 4.9 %collective-permute-start.16 = (f32[1,6,36]{2,0,1:T(1,128)S(1)}, f32[1,6,36]{2,0,1:T(1,128)S(1)}, u32[]{:S(2)}, u32[]{:S(2)}) collective-permute-start(f32[1,6,36]{2,0,1:T(1,128)S(1)} %get-tuple-element.137), channel_id=1, source_target_pairs={{0,4},{4,8},{8,12},{1,5},{5,9},{9,13},{2,6},{6,10},{10,14},{3,7},{... | collective-permute-start | bytes 2600 | tf_op jit(solution)/shard_map/ppermute | solution.py:39
  88.6 5.5 %collective-permute-start.17 = (f32[1,6,36]{2,0,1:T(1,128)S(1)}, f32[1,6,36]{2,0,1:T(1,128)S(1)}, u32[]{:S(2)}, u32[]{:S(2)}) collective-permute-start(f32[1,6,36]{2,0,1:T(1,128)S(1)} %get-tuple-element.138), channel_id=1, source_target_pairs={{4,0},{8,4},{12,8},{5,1},{9,5},{13,9},{6,2},{10,6},{14,10},{7,3},{... | collective-permute-start | bytes 2600 | tf_op jit(solution)/shard_map/ppermute | solution.py:42
